TPU v7x, 32 devices: a whole 2x2x4 slice. The times are simulated.
32 devices in a mesh: groups: 2 (over x), seq: 8 (over z, y), pipe: 2 (over core).
Axes of the slice: x: 2, y: 2, z: 4, core: 2. Of those that a mesh axis runs over, the one named last changes fastest.
Arguments:
- tokens: bfloat16 [2, 2048, 1440], P('pipe', ('groups', 'seq')), parts along dimension 1, may hold values from -6 to 6
- routes: int32 [2, 2048, 4], P('pipe', ('groups', 'seq')), parts along dimension 1, may hold values from 0 to 15, all different within a row; in each aligned block of 128 rows (0 to 127, 128 to 255, ..., all dimensions but the last counted through in order) at most 48 rows name the same one
- route_weights: float32 [2, 2048, 4], P('pipe', ('groups', 'seq')), parts along dimension 1, may hold values from 0.1 to 1
- moe_gain: float32 [1440], replicated, may hold values from 0.5 to 1.5
- gate_up: bfloat16 [32, 1440, 1440], P('seq'), may hold values from -0.15625 to 0.15625
- down_proj: bfloat16 [32, 720, 1440], P('seq'), may hold values from -0.15625 to 0.15625
- attn_gain: float32 [1440], replicated, may hold values from 0.5 to 1.5
- qkv_proj: bfloat16 [1440, 2560], P('seq'), may hold values from -0.15625 to 0.15625
- head_sink_logits: float32 [32], replicated, may hold values from 3 to 6
- out_proj: bfloat16 [2048, 1440], P('seq'), may hold values from -0.125 to 0.125
Outputs:
- layer_output: bfloat16 [2, 2048, 1440], P('pipe', ('groups', 'seq')), parts along dimension 1
There are 2 independent parts, one for each index of `groups`. A program takes and returns all parts, laid end to end along the dimension named above; an argument that names none is the same for every part. Nothing has to cross between parts.
Inputs may be any that keep to these rules, and one draw needn't show every extreme that they name: `routes`: within the 128 positions of one micro-batch on one index of seq, a token names each of its 4 experts once, and each expert is named by at most 48 tokens; one expert is named by exactly 48 of them.
All inputs are finite; a program needn't handle non-finite values.
Results may differ from a plain program's by a relative error of at most 0.0085.
Values may be sent and summed in bfloat16 or wider, within the bound.
No kernel may reach another device: no remote copies, remote signals or barrier semaphores. Data moves between devices by JAX's collectives and lax.ppermute only.
A program may use at most 128 MiB of HBM per device.

v0:
```python
import jax
import jax.numpy as jnp
from jax import lax
from jax.sharding import PartitionSpec as P

E = 16
TOP = 4
QUERY_HEADS = 32
KEY_VALUE_HEADS = 4
HEAD_SIZE = 64
WINDOW_SPAN = 128
HALF = 720
CAP = 48


eps = 1e-05


def from_partner(value, axis, distance):
    return lax.ppermute(value, axis, [(i, i ^ 1 << distance) for i in range(lax.axis_size(axis))])


def shifted(value, axis, steps):
    count = lax.axis_size(axis)
    pairs = [(source, (source + steps) % count) for source in range(count)]
    return lax.ppermute(value, axis, pairs)


def passed_along(value, axis, steps):
    count = lax.axis_size(axis)
    first, last = (max(0, -steps), min(count, count - steps))
    return lax.ppermute(value, axis, [(source, source + steps) for source in range(first, last)])


def rms_scale(value_matrix, gain):
    widened = value_matrix.astype(jnp.float32)
    mean_square = jnp.mean(widened * widened, axis=-1, keepdims=True)
    return (widened * lax.rsqrt(mean_square + eps) * gain).astype(jnp.bfloat16)


def slot_positions(route_rows):
    flat = route_rows.reshape(-1)
    onehot = (flat[:, None] == jnp.arange(E, dtype=jnp.int32)[None, :]).astype(jnp.int32)
    earlier = jnp.cumsum(onehot, axis=0) - onehot
    return flat * CAP + jnp.sum(earlier * onehot, axis=1)


def expert_layer(local, route_rows, route_scale, moe_gain, gate_up, down_proj):
    tok_count, width = local.shape
    seq_count = lax.axis_size("seq")
    per_device = gate_up.shape[0]
    normed = rms_scale(local, moe_gain)
    positions = slot_positions(route_rows)
    select = (positions[None, :] == jnp.arange(E * CAP, dtype=jnp.int32)[:, None]).astype(
        jnp.bfloat16
    )
    repeated = jnp.repeat(normed, TOP, axis=0)
    table = jnp.dot(select, repeated, preferred_element_type=jnp.float32).astype(jnp.bfloat16)
    by_expert = table.reshape(E, CAP, width)
    first = lax.axis_index("seq") % 2 == 0
    outgoing = jnp.repeat(by_expert, 2, axis=0).reshape(seq_count, per_device, CAP, width)
    received = lax.all_to_all(outgoing, "seq", split_axis=0, concat_axis=0, tiled=True)
    projected = jnp.einsum("spcd,pdh->spch", received, gate_up, preferred_element_type=jnp.float32)
    gate_part = projected[..., :HALF]
    up_part = projected[..., HALF:]
    hidden = (gate_part * jax.nn.sigmoid(1.702 * gate_part) * (up_part + 1.0)).astype(jnp.bfloat16)
    partial_value = jnp.einsum(
        "spch,phd->spcd", hidden, down_proj, preferred_element_type=jnp.float32
    )
    if per_device >= 2:
        finished = (
            partial_value.reshape(seq_count, per_device // 2, 2, CAP, width)
            .sum(axis=2)
            .astype(jnp.bfloat16)
        )
    else:
        lower_rows = partial_value[:, :, : CAP // 2]
        upper_rows = partial_value[:, :, CAP // 2 :]
        kept = jnp.where(first, lower_rows, upper_rows)
        given = jnp.where(first, upper_rows, lower_rows)
        partner_part = from_partner(given.astype(jnp.bfloat16), "seq", 0).astype(given.dtype)
        finished = (kept + partner_part).astype(jnp.bfloat16)
    summed = lax.all_to_all(finished, "seq", split_axis=0, concat_axis=0, tiled=True).reshape(
        E * CAP, width
    )
    picked = lax.dot_general(
        select, summed, (((0,), (0,)), ((), ())), preferred_element_type=jnp.float32
    )
    weighted = jnp.sum(picked.reshape(tok_count, TOP, width) * route_scale[:, :, None], axis=1)
    return (local.astype(jnp.float32) + weighted).astype(jnp.bfloat16)


def attend(query_matrix, keys_extended, values_extended, head_sink_logits, halo_valid):
    tok_count = query_matrix.shape[0]
    query_groups = QUERY_HEADS // KEY_VALUE_HEADS
    attention_block = min(tok_count, 512)
    scale = float(HEAD_SIZE) ** (-0.5)
    sink_mass_total = jnp.exp(head_sink_logits).reshape(KEY_VALUE_HEADS, query_groups, 1, 1)
    block_queries = query_matrix.reshape(attention_block, KEY_VALUE_HEADS, query_groups, HEAD_SIZE)
    block_keys = keys_extended.reshape(attention_block + WINDOW_SPAN, KEY_VALUE_HEADS, HEAD_SIZE)
    block_values = values_extended.reshape(
        attention_block + WINDOW_SPAN, KEY_VALUE_HEADS, HEAD_SIZE
    )
    scores = (
        jnp.einsum("qhgd,khd->hgqk", block_queries, block_keys, preferred_element_type=jnp.float32)
        * scale
    )
    query_pos = jnp.arange(attention_block, dtype=jnp.int32)[:, None] + WINDOW_SPAN
    key_pos = jnp.arange(attention_block + WINDOW_SPAN, dtype=jnp.int32)[None, :]
    distance = query_pos - key_pos
    allowed = (
        (distance >= 0) & (distance < WINDOW_SPAN) & ((key_pos + 0 >= WINDOW_SPAN) | halo_valid)
    )
    weights = jnp.where(allowed, jnp.exp(scores), 0.0)
    probs = (weights / (jnp.sum(weights, axis=-1, keepdims=True) + sink_mass_total)).astype(
        jnp.bfloat16
    )
    mixed = jnp.einsum("hgqk,khd->qhgd", probs, block_values, preferred_element_type=jnp.float32)
    outputs = mixed.reshape(attention_block, QUERY_HEADS * HEAD_SIZE).astype(jnp.bfloat16)
    return outputs


def body(
    tokens,
    routes,
    route_weights,
    moe_gain,
    gate_up,
    down_proj,
    attn_gain,
    qkv_proj,
    head_sink_logits,
    out_proj,
):
    hidden = expert_layer(tokens[0], routes[0], route_weights[0], moe_gain, gate_up, down_proj)
    tok_count, width = hidden.shape
    normed = rms_scale(hidden, attn_gain)
    seq_index = lax.axis_index("seq")
    pipe_index = lax.axis_index("pipe")
    halo_valid = (seq_index > 0) | (pipe_index > 0)
    query_width = QUERY_HEADS * HEAD_SIZE
    width_of_pair = KEY_VALUE_HEADS * HEAD_SIZE
    columns = normed
    packed_heads = jnp.dot(
        columns,
        lax.all_gather(qkv_proj, "seq", axis=0, tiled=True),
        preferred_element_type=jnp.float32,
    ).astype(jnp.bfloat16)
    from_left = shifted(packed_heads[tok_count - WINDOW_SPAN :, query_width:], "seq", 1)
    from_section = passed_along(from_left, "pipe", 1)
    halo_pairs = jnp.where(seq_index == 0, from_section, from_left)
    query_matrix = packed_heads[:, :query_width]
    pairs_ext = jnp.concatenate([halo_pairs, packed_heads[:, query_width:]], axis=0)
    keys_extended = pairs_ext[:, :width_of_pair]
    values_extended = pairs_ext[:, width_of_pair:]
    attended = attend(query_matrix, keys_extended, values_extended, head_sink_logits, halo_valid)
    columns = attended
    projected = jnp.dot(
        columns,
        lax.all_gather(out_proj, "seq", axis=0, tiled=True),
        preferred_element_type=jnp.float32,
    )
    return (hidden.astype(jnp.float32) + projected).astype(jnp.bfloat16)[None]


def solution(mesh):
    in_specs = (
        P("pipe", ("groups", "seq"), None),
        P("pipe", ("groups", "seq"), None),
        P("pipe", ("groups", "seq"), None),
        P(),
        P("seq", None, None),
        P("seq", None, None),
        P(),
        P("seq", None),
        P(),
        P("seq", None),
    )
    out_specs = P("pipe", ("groups", "seq"), None)
    return jax.shard_map(body, mesh=mesh, in_specs=in_specs, out_specs=out_specs, check_vma=False)
```

profile of v0, /device:TPU:0, one launch (start us, length us, event | category | flops | bytes accessed | tf_op | source)
XLA Modules:
  0.0 386.2 jit_solution(929708166712406774)
XLA Ops:
  6.5 0.0 all-gather.6.cloned.1.call-start
  6.5 0.7 all-gather.6.cloned.1.call-update
  7.3 0.8 copy.44
  8.0 0.1 eq.61
  8.2 0.1 reshape_squeeze.3
  8.3 1.2 reduce-window.6
  9.4 0.2 slice_reduce_fusion
  9.7 1.2 fusion.32
  10.9 1.2 fusion.34
  12.1 0.2 copy.49
  12.3 0.4 broadcast_in_dim.12
  12.8 0.8 reshape.112
  13.5 0.1 fusion.46
  13.6 2.8 convolution_convert_fusion.1
  16.4 2.8 copy.50
  19.2 2.7 broadcast_in_dim.15
  21.9 7.4 %all-to-all-start = ((bf16[8,4,48,1440]{3,2,1,0:T(8,128)(2,1)}), bf16[8,4,48,1440]{3,2,1,0:T(8,128)(2,1)}, u32[]{:S(2)}, u32[]{:S(2)}) async-start(bf16[8,4,48,1440]{3,2,1,0:T(8,128)(2,1)} %bitcast.92), calls=%async_computation | async-start | bytes 9437184 | tf_op jit(solution)/shard_map/all_to_all | solution.py:62
  29.3 0.0 all-gather.4.cloned.1.call-start
  29.4 0.7 all-gather.4.cloned.1.call-update
  30.1 181.4 %all-to-all-done = bf16[8,4,48,1440]{3,2,1,0:T(8,128)(2,1)} async-done(((bf16[8,4,48,1440]{3,2,1,0:T(8,128)(2,1)}), bf16[8,4,48,1440]{3,2,1,0:T(8,128)(2,1)}, u32[]{:S(2)}, u32[]{:S(2)}) %all-to-all-start) | async-done | bytes 4423712 | tf_op jit(solution)/shard_map/all_to_all | solution.py:62
  211.5 16.6 %fusion.4 = f32[8,4,48,1440]{3,2,0,1:T(8,128)} fusion(bf16[4,1440,1440]{2,1,0:T(8,128)(2,1)} %param.14, bf16[8,4,48,1440]{3,2,1,0:T(8,128)(2,1)} %all-to-all-done), kind=kOutput, calls=%fused_computation.5 | convolution fusion | flops 6370099200 | bytes 29859840 | tf_op jit(solution)/shard_map/spcd,pdh->spch/dot_general | solution.py:63
  228.2 10.8 %bitcast_reduce_fusion = bf16[8,2,48,1440]{3,2,0,1:T(8,128)(2,1)S(1)} fusion(bf16[4,720,1440]{2,1,0:T(8,128)(2,1)} %param.15, f32[8,4,48,1440]{3,2,0,1:T(8,128)} %fusion.4), kind=kOutput, calls=%fused_computation.2 | convolution fusion | flops 3195002880 | bytes 19353600 | tf_op jit(solution)/shard_map/spch,phd->spcd/dot_general | solution.py:67
  238.9 0.0 copy-start.2
  238.9 1.6 copy.52
  240.6 8.9 %all-to-all-start.1 = ((bf16[8,2,48,1440]{3,2,1,0:T(8,128)(2,1)}), bf16[8,2,48,1440]{3,2,1,0:T(8,128)(2,1)S(1)}, u32[]{:S(2)}, u32[]{:S(2)}) async-start(bf16[8,2,48,1440]{3,2,1,0:T(8,128)(2,1)} %copy.52), calls=%async_computation.1 | async-start | bytes 4718592 | tf_op jit(solution)/shard_map/all_to_all | solution.py:83
  249.4 0.1 reduce_sum.57
  249.6 0.1 copy.48
  249.6 99.0 %all-to-all-done.1 = bf16[8,2,48,1440]{3,2,1,0:T(8,128)(2,1)S(1)} async-done(((bf16[8,2,48,1440]{3,2,1,0:T(8,128)(2,1)}), bf16[8,2,48,1440]{3,2,1,0:T(8,128)(2,1)S(1)}, u32[]{:S(2)}, u32[]{:S(2)}) %all-to-all-start.1) | async-done | bytes 2211872 | tf_op jit(solution)/shard_map/all_to_all | solution.py:83
  348.6 1.5 fusion.23
  350.1 0.0 copy-done
  350.1 0.2 fusion.29
  350.3 0.0 all-gather.6.cloned.1.call-done
  350.4 7.0 %reshape.121 = bf16[1440,2560]{1,0:T(8,128)(2,1)} reshape(bf16[8,180,2560]{2,1,0:T(8,128)(2,1)} %all-gather.6.cloned.1.call-done) | data formatting | bytes 14745600
  357.4 4.4 %convolution_convert_fusion = bf16[128,2560]{1,0:T(8,128)(2,1)S(1)} fusion(bf16[1440,2560]{1,0:T(8,128)(2,1)} %reshape.121, bf16[128,1440]{0,1:T(8,128)(2,1)S(1)} %get-tuple-element.6, f32[1440]{0:T(1024)S(1)} %copy-done.1, f32[128]{0:T(128)S(1)} %add_rsqrt_fusion), kind=kOutput, calls=%fused_computation.12 | convolution fusion | flops 944783360 | bytes 8403072 | tf_op jit(solution)/shard_map/dot_general | solution.py:144
  361.8 1.1 collective-permute-start
  362.9 0.1 add.73
  363.0 6.5 %collective-permute-done = bf16[128,512]{1,0:T(8,128)(2,1)S(1)} collective-permute-done((bf16[128,512]{1,0:T(8,128)(2,1)S(1)}, bf16[128,512]{1,0:T(8,128)(2,1)S(1)}, u32[]{:S(2)}, u32[]{:S(2)}) %collective-permute-start) | collective-permute-done | bytes 131104 | tf_op jit(solution)/shard_map/ppermute | solution.py:26
  369.5 1.3 collective-permute-start.1
  370.8 0.1 fusion.43
  371.0 0.3 copy.56
  371.2 0.5 collective-permute-done.1
  371.8 0.1 copy.55
  371.9 0.1 copy.54
  372.0 1.0 fusion.10
  373.1 0.1 broadcast_add_fusion
  373.1 1.0 fusion.26
  374.2 0.0 all-gather.4.cloned.1.call-done
  374.2 5.1 %fusion.15 = bf16[1,128,1440]{1,2,0:T(8,128)(2,1)} fusion(bf16[2048,1440]{0,1:T(8,128)(2,1)} %all-gather.4.cloned.1.call-done, bf16[128,2048]{0,1:T(8,128)(2,1)S(1)} %bitcast.100, bf16[128,1440]{0,1:T(8,128)(2,1)S(1)} %get-tuple-element.6), kind=kOutput, calls=%fused_computation.20 | convolution fusion | flops 755527680 | bytes 7159808 | tf_op jit(solution)/shard_map/dot_general | solution.py:158
  (20 shorter events, 0.2 us)
Async XLA Ops:
  6.5 343.8 %all-gather.6.cloned.1.call-start = ((), (), s32[]{:S(2)}) async-start(), calls=%async_computation.3 | async-start | bytes 8478720 | tf_op jit(solution)/shard_map/all_gather | solution.py:146
  21.9 189.6 %all-to-all-start = ((bf16[8,4,48,1440]{3,2,1,0:T(8,128)(2,1)}), bf16[8,4,48,1440]{3,2,1,0:T(8,128)(2,1)}, u32[]{:S(2)}, u32[]{:S(2)}) async-start(bf16[8,4,48,1440]{3,2,1,0:T(8,128)(2,1)} %bitcast.92), calls=%async_computation | async-start | bytes 9437184 | tf_op jit(solution)/shard_map/all_to_all | solution.py:62
  29.3 344.9 %all-gather.4.cloned.1.call-start = ((), (), s32[]{:S(2)}) async-start(), calls=%async_computation.2 | async-start | bytes 6635520 | tf_op jit(solution)/shard_map/all_gather | solution.py:160
  238.9 109.7 %copy-start.2 = (f32[1,128,4]{1,2,0:T(4,128)S(1)}, f32[1,128,4]{1,2,0:T(4,128)}, u32[]{:S(2)}) copy-start(f32[1,128,4]{1,2,0:T(4,128)} %param.12) | copy-start | bytes 6148
  240.6 108.1 %all-to-all-start.1 = ((bf16[8,2,48,1440]{3,2,1,0:T(8,128)(2,1)}), bf16[8,2,48,1440]{3,2,1,0:T(8,128)(2,1)S(1)}, u32[]{:S(2)}, u32[]{:S(2)}) async-start(bf16[8,2,48,1440]{3,2,1,0:T(8,128)(2,1)} %copy.52), calls=%async_computation.1 | async-start | bytes 4718592 | tf_op jit(solution)/shard_map/all_to_all | solution.py:83
  249.4 100.7 %copy-start = (bf16[1,128,1440]{1,2,0:T(8,128)(2,1)S(1)}, bf16[1,128,1440]{1,2,0:T(8,128)(2,1)}, u32[]{:S(2)}) copy-start(bf16[1,128,1440]{1,2,0:T(8,128)(2,1)} %param.10) | copy-start | bytes 1105924
  350.3 7.0 %copy-start.1 = (f32[1440]{0:T(1024)S(1)}, f32[1440]{0:T(1024)}, u32[]{:S(2)}) copy-start(f32[1440]{0:T(1024)} %param.16) | copy-start | bytes 17284
  357.4 5.5 %copy-start.3 = (f32[32]{0:T(128)S(1)}, f32[32]{0:T(128)}, u32[]{:S(2)}) copy-start(f32[32]{0:T(128)} %param.18) | copy-start | bytes 388
  361.8 7.7 %collective-permute-start = (bf16[128,512]{1,0:T(8,128)(2,1)S(1)}, bf16[128,512]{1,0:T(8,128)(2,1)S(1)}, u32[]{:S(2)}, u32[]{:S(2)}) collective-permute-start(bf16[128,512]{1,0:T(8,128)(2,1)S(1)} %slice.36), channel_id=1, source_target_pairs={{0,2},{2,4},{4,6},{6,8},{8,10},{10,12},{12,14},{14,0},{1,3},{3,5},... | collective-permute-start | bytes 393224 | tf_op jit(solution)/shard_map/ppermute | solution.py:26
  369.5 2.3 collective-permute-start.1
Sparse Core Ops, SparseCore 0:
  9.5 207.8 all-gather.5
  219.5 134.6 all-gather.3
where the time goes:
time: 387 us; the launch traced here: 386 us
  waiting for transfers between devices  289 us (75%)
  matrix products  43.3 us (11%)
  starting transfers between devices  18.7 us (5%)
  local copies, waits for them, and re-layouts  17.5 us (5%)
  between operations  13.6 us (4%)
  other arithmetic  4.21 us (1%)
    all_to_all x1, waiting for transfers between devices, expert_layer(): lax.all_to_all(outgoing, 'seq', split_axis=0, concat_axis=0, tiled=True)  181 us
    all_to_all x1, waiting for transfers between devices, expert_layer(): lax.all_to_all(finished, 'seq', split_axis=0, concat_axis=0, tiled=True)  99 us
    dot_general x1, matrix products, expert_layer(): jnp.einsum('spcd,pdh->spch', received, gate_up, preferred_element_type=jn...  16.6 us
    dot_general x1, matrix products, expert_layer(): jnp.einsum('spch,phd->spcd', hidden, down_proj, preferred_element_type=jn...  10.8 us
    all_to_all x1, starting transfers between devices, expert_layer(): lax.all_to_all(finished, 'seq', split_axis=0, concat_axis=0, tiled=True)  8.86 us
    unnamed x10, local copies, waits for them, and re-layouts  7.8 us
  transfers between devices with their start and end apart: 6, of which 4 were waited for; matrix products, arithmetic and copies ran while one was open for 15% of the time, Pallas kernels for 0%

commit v1 on v0

v1 whole, which is shorter than its diff:
```python
import functools

import jax
import jax.numpy as jnp
from jax import lax
from jax.experimental import pallas as pl
from jax.experimental.pallas import tpu as pltpu
from jax.sharding import PartitionSpec as P

E = 16
TOP = 4
QUERY_HEADS = 32
KEY_VALUE_HEADS = 4
HEAD_SIZE = 64
WINDOW_SPAN = 128
HALF = 720
CAP = 48


eps = 1e-05


F32 = jnp.float32
BF16 = jnp.bfloat16
VMEM = pl.BlockSpec(memory_space=pltpu.VMEM)
SMEM = pl.BlockSpec(memory_space=pltpu.SMEM)
ANY = pl.BlockSpec(memory_space=pl.ANY)


def route_slots(routes_ref):
    tok_count = routes_ref.shape[1]
    expert = lax.broadcasted_iota(jnp.int32, (E, tok_count), 0)
    member = jnp.zeros((E, tok_count), jnp.bool_)
    for k in range(routes_ref.shape[0]):
        member = member | (routes_ref[k : k + 1, :] == expert)
    first = lax.broadcasted_iota(jnp.int32, (tok_count, tok_count), 0)
    second = lax.broadcasted_iota(jnp.int32, (tok_count, tok_count), 1)
    before = jnp.where(first < second, 1.0, 0.0).astype(BF16)
    flags = jnp.where(member, 1.0, 0.0)
    rank = jnp.dot(flags.astype(BF16), before, preferred_element_type=F32)
    return flags, jnp.where(flags > 0.0, rank, -1.0)


def dispatch_kernel(tokens_ref, routes_ref, gain_ref, table_ref):
    tok_count = tokens_ref.shape[1]
    value = tokens_ref[...].astype(F32).T
    mean_square = jnp.mean(value * value, axis=-1, keepdims=True)
    normed = (value * lax.rsqrt(mean_square + eps) * gain_ref[...]).astype(BF16)
    _, rank = route_slots(routes_ref)
    slot = lax.broadcasted_iota(jnp.int32, (CAP, tok_count), 0).astype(F32)
    for expert in range(E):
        select = jnp.where(slot == rank[expert : expert + 1, :], 1.0, 0.0).astype(BF16)
        table_ref[expert] = jnp.dot(select, normed, preferred_element_type=F32).astype(BF16)


def dispatch(tokens_t, routes_t, gain):
    width = tokens_t.shape[0]
    return pl.pallas_call(
        dispatch_kernel,
        out_shape=jax.ShapeDtypeStruct((E, CAP, width), BF16),
        in_specs=[VMEM] * 3,
        out_specs=VMEM,
        name="dispatch",
    )(tokens_t, routes_t, gain)


def returns_kernel(tokens_ref, routes_ref, scale_ref, residual_ref, coarse_ref, fine_ref):
    tok_count = tokens_ref.shape[1]
    residual_ref[...] = tokens_ref[...].astype(F32).T.astype(BF16)
    _, rank = route_slots(routes_ref)
    expert_index = lax.broadcasted_iota(jnp.int32, (E, tok_count), 0)
    scale = jnp.zeros((E, tok_count), F32)
    for k in range(routes_ref.shape[0]):
        scale += jnp.where(routes_ref[k : k + 1, :] == expert_index, scale_ref[k : k + 1, :], 0.0)
    slot = lax.broadcasted_iota(jnp.int32, (CAP, tok_count), 0).astype(F32)
    rows = []
    for expert in range(E):
        hit = slot == rank[expert : expert + 1, :]
        rows.append(jnp.where(hit, scale[expert : expert + 1, :], 0.0))
    weighted = jnp.concatenate(rows, axis=0).T
    coarse = weighted.astype(BF16)
    coarse_ref[...] = coarse
    fine_ref[...] = (weighted - coarse.astype(F32)).astype(BF16)


def returns(tokens_t, routes_t, scale_t):
    width, tok_count = tokens_t.shape
    return pl.pallas_call(
        returns_kernel,
        out_shape=(
            jax.ShapeDtypeStruct((tok_count, width), BF16),
            jax.ShapeDtypeStruct((tok_count, E * CAP), BF16),
            jax.ShapeDtypeStruct((tok_count, E * CAP), BF16),
        ),
        in_specs=[VMEM] * 3,
        out_specs=(VMEM,) * 3,
        name="returns",
    )(tokens_t, routes_t, scale_t)


def experts_kernel(rows_ref, gate_up_ref, down_ref, out_ref, total_ref):
    slab = pl.program_id(1)
    blocks, cap, width = rows_ref.shape
    rows = rows_ref[...].reshape(blocks * cap, width)
    projected = jnp.dot(rows, gate_up_ref[...], preferred_element_type=F32)
    gate_part = projected[:, :HALF]
    up_part = projected[:, HALF:]
    hidden = (gate_part * jax.nn.sigmoid(1.702 * gate_part) * (up_part + 1.0)).astype(BF16)
    value = jnp.dot(hidden, down_ref[...], preferred_element_type=F32)

    @pl.when(slab == 0)
    def _():
        total_ref[...] = value

    @pl.when(slab > 0)
    def _():
        total_ref[...] += value

    @pl.when(slab == pl.num_programs(1) - 1)
    def _():
        out_ref[...] = total_ref[...].astype(BF16).reshape(blocks, cap, width)


def run_experts(received, gate_up, down_proj):
    seq_count, experts, cap, width = received.shape
    slabs = gate_up.shape[0] // experts
    rows_spec = pl.BlockSpec((seq_count, None, cap, width), lambda e, k: (0, e, 0, 0))
    return pl.pallas_call(
        experts_kernel,
        out_shape=jax.ShapeDtypeStruct(received.shape, BF16),
        grid=(experts, slabs),
        in_specs=[
            rows_spec,
            pl.BlockSpec((None, width, gate_up.shape[2]), lambda e, k: (e * slabs + k, 0, 0)),
            pl.BlockSpec((None, down_proj.shape[1], width), lambda e, k: (e * slabs + k, 0, 0)),
        ],
        out_specs=rows_spec,
        scratch_shapes=[pltpu.VMEM((seq_count * cap, width), F32)],
        compiler_params=pltpu.CompilerParams(vmem_limit_bytes=48 << 20),
        name="experts",
    )(received, gate_up, down_proj)


def shard_of(place_ref, step, flip, lines):
    line = lax.rem(place_ref[0] - step + lines, lines)
    return line * 2 + (place_ref[1] + flip) % 2


def quarter_of(place_ref, group_flip, pipe_flip):
    return (place_ref[2] + group_flip) % 2 * 2 + (place_ref[3] + pipe_flip) % 2


def qkv_kernel(
    rows, place_ref, tables_ref, residual_ref, coarse_ref, fine_ref, gain_ref, *rest
):
    parts, (packed_ref, hidden_ref, held, slices, sems) = rest[:8], rest[8:]
    lines, padded, columns = held.shape[1:]
    copies = []
    for i, part in enumerate(parts):
        copy = pltpu.make_async_copy(part.at[:, :, pl.ds(0, columns)], held.at[i], sems.at[i])
        copy.start()
        copies.append(copy)
    table = tables_ref[...]
    mixed = jnp.dot(coarse_ref[...], table, preferred_element_type=F32)
    mixed += jnp.dot(fine_ref[...], table, preferred_element_type=F32)
    hidden = (residual_ref[...].astype(F32) + mixed).astype(BF16)
    value = hidden.astype(F32)
    hidden_ref[...] = value.T.astype(BF16)
    mean_square = jnp.mean(value * value, axis=-1, keepdims=True)
    normed = value * lax.rsqrt(mean_square + eps) * gain_ref[...]
    slices[...] = jnp.zeros_like(slices)
    for s in range(2 * lines):
        slices[s, :, :rows] = normed[:, s * rows : (s + 1) * rows].astype(BF16)
    for pair in range(4):
        total = jnp.zeros((value.shape[0], columns), F32)
        for flip in range(2):
            copies[pair * 2 + flip].wait()
            for step in range(lines):
                total += jnp.dot(
                    slices[shard_of(place_ref, step, flip, lines)],
                    held[pair * 2 + flip, step],
                    preferred_element_type=F32,
                )
        start = quarter_of(place_ref, pair % 2, pair // 2) * columns
        packed_ref[:, pl.ds(pl.multiple_of(start, 128), columns)] = total.astype(BF16)


def project_qkv(place, tables, residual, coarse, fine, gain, parts, rows, columns):
    tok_count, width = residual.shape
    lines, padded = parts[0].shape[:2]
    return pl.pallas_call(
        functools.partial(qkv_kernel, rows),
        out_shape=(
            jax.ShapeDtypeStruct((tok_count, 4 * columns), BF16),
            jax.ShapeDtypeStruct((width, tok_count), BF16),
        ),
        in_specs=[SMEM] + [VMEM] * 5 + [ANY] * 8,
        out_specs=(VMEM, VMEM),
        scratch_shapes=[
            pltpu.VMEM((8, lines, padded, columns), BF16),
            pltpu.VMEM((2 * lines, tok_count, padded), BF16),
            pltpu.SemaphoreType.DMA((8,)),
        ],
        compiler_params=pltpu.CompilerParams(vmem_limit_bytes=40 << 20),
        name="qkv",
    )(place, tables, residual, coarse, fine, gain, *parts)


def attention_kernel(
    place_ref, sink_ref, packed_ref, halo_ref, hidden_ref, *rest
):
    parts, (out_ref, held, mixed, total_ref, sems) = rest[:8], rest[8:]
    lines, padded, columns = held.shape[1:]
    depth = mixed.shape[2]
    fold = columns // depth
    quarter_rows = out_ref.shape[0] // 4
    first_column = parts[0].shape[2] - columns
    copies = []
    for i, part in enumerate(parts):
        copy = pltpu.make_async_copy(
            part.at[:, :, pl.ds(first_column, columns)], held.at[i], sems.at[i]
        )
        copy.start()
        copies.append(copy)
    tok_count = packed_ref.shape[0]
    pair_width = 2 * HEAD_SIZE
    query_width = QUERY_HEADS * HEAD_SIZE
    kv_width = KEY_VALUE_HEADS * HEAD_SIZE
    query_groups = QUERY_HEADS // KEY_VALUE_HEADS
    span = halo_ref.shape[0]
    extent = span + tok_count
    query_pos = lax.broadcasted_iota(jnp.int32, (tok_count, extent), 0) + span
    key_pos = lax.broadcasted_iota(jnp.int32, (tok_count, extent), 1)
    distance = query_pos - key_pos
    halo_valid = place_ref[0] + place_ref[1] + place_ref[3] > 0
    first_key = jnp.where(halo_valid, 0, span)
    allowed = (distance >= 0) & (distance < WINDOW_SPAN) & (key_pos >= first_key)
    left = lax.broadcasted_iota(jnp.int32, (extent, pair_width), 1) < HEAD_SIZE
    scale = float(HEAD_SIZE) ** (-0.5)

    def sides(start, head):
        lanes = pl.ds(start + head // 2 * pair_width, pair_width)
        own = packed_ref[:, query_width + start + head // 2 * pair_width :][:, :pair_width]
        both = jnp.concatenate([halo_ref[:, lanes], own], axis=0).astype(F32)
        turned = pltpu.roll(both, HEAD_SIZE, 1)
        low, high = (both, turned) if head % 2 == 0 else (turned, both)
        low = jnp.where(left, low, 0.0).astype(BF16)
        high = jnp.where(left, 0.0, high).astype(BF16)
        return low, high

    pairs = query_groups // 2
    for head in range(KEY_VALUE_HEADS):
        keys, values = sides(0, head), sides(kv_width, head)
        base = head * pairs * pair_width
        stacked = jnp.concatenate(
            [packed_ref[:, base + j * pair_width : base + (j + 1) * pair_width] for j in range(pairs)],
            axis=0,
        )
        outcome = None
        for side in range(2):
            scores = lax.dot_general(
                stacked, keys[side], (((1,), (1,)), ((), ())), preferred_element_type=F32
            )
            probs = []
            for j in range(pairs):
                piece = scores[j * tok_count : (j + 1) * tok_count] * scale
                weights = jnp.where(allowed, jnp.exp(piece), 0.0)
                sink = sink_ref[head * query_groups + 2 * j + side]
                sums = jnp.sum(weights, axis=-1, keepdims=True) + sink
                probs.append((weights / sums).astype(BF16))
            part = jnp.dot(
                jnp.concatenate(probs, axis=0), values[side], preferred_element_type=F32
            )
            outcome = part if outcome is None else outcome + part
        for j in range(pairs):
            column = base + j * pair_width
            mixed[column // depth, :, column % depth : column % depth + pair_width] = outcome[
                j * tok_count : (j + 1) * tok_count
            ].astype(BF16)

    for pair in range(4):
        totals = [jnp.zeros((padded, tok_count), F32) for _ in range(fold)]
        for flip in range(2):
            copies[pair * 2 + flip].wait()
            for step in range(lines):
                against = mixed[shard_of(place_ref, step, flip, lines)]
                for i in range(fold):
                    totals[i] += lax.dot_general(
                        held[pair * 2 + flip, step, :, i * depth : (i + 1) * depth],
                        against,
                        (((1,), (1,)), ((), ())),
                        preferred_element_type=F32,
                    )
        start = quarter_of(place_ref, pair % 2, pair // 2) * quarter_rows
        for i in range(fold):
            count = min(padded, quarter_rows - i * padded)
            total_ref[pl.ds(pl.multiple_of(start + i * padded, 8), count), :] = totals[i][:count]
    out_ref[...] = (hidden_ref[...].astype(F32) + total_ref[...]).astype(BF16)


def attend_and_project(place, sinks, packed, halo, hidden_t, parts, columns, depth):
    width, tok_count = hidden_t.shape
    lines, padded = parts[0].shape[:2]
    return pl.pallas_call(
        attention_kernel,
        out_shape=jax.ShapeDtypeStruct((width, tok_count), BF16),
        in_specs=[SMEM] * 2 + [VMEM] * 3 + [ANY] * 8,
        out_specs=VMEM,
        scratch_shapes=[
            pltpu.VMEM((8, lines, padded, columns), BF16),
            pltpu.VMEM((2 * lines, tok_count, depth), BF16),
            pltpu.VMEM((width, tok_count), F32),
            pltpu.SemaphoreType.DMA((8,)),
        ],
        compiler_params=pltpu.CompilerParams(vmem_limit_bytes=40 << 20),
        name="attention",
    )(place, sinks, packed, halo, hidden_t, *parts)


def place_of():
    seq_index = lax.axis_index("seq")
    return jnp.stack(
        [seq_index // 2, seq_index % 2, lax.axis_index("groups") % 2, lax.axis_index("pipe")]
    ).astype(jnp.int32)


def shard_block(qkv_proj, out_proj):
    rows, qkv_width = qkv_proj.shape
    depth, width = out_proj.shape
    quarter = lax.axis_index("groups") % 2 * 2 + lax.axis_index("pipe")
    qw, ow = qkv_width // 4, width // 4
    padded = rows + -rows % 8
    mine_qkv = lax.dynamic_slice_in_dim(qkv_proj, quarter * qw, qw, 1)
    mine_out = lax.dynamic_slice_in_dim(out_proj.T, quarter * ow, ow, 0)
    pieces = [jnp.pad(mine_qkv, ((0, padded - rows), (0, 0)))]
    for first in range(0, ow, padded):
        piece = mine_out[first : first + padded]
        pieces.append(jnp.pad(piece, ((0, padded - piece.shape[0]), (0, 0))))
    return jnp.concatenate(pieces, axis=1)


def fused_body(
    tokens, routes, route_weights, moe_gain, gate_up, down_proj, attn_gain, qkv_proj, sinks, out_proj
):
    seq_count = lax.axis_size("seq")
    tok_count, width = tokens.shape[1:]
    per_device = gate_up.shape[0]
    rows, qkv_width = qkv_proj.shape
    depth = out_proj.shape[0]
    tokens_t, routes_t, scale_t = tokens[0].T, routes[0].T, route_weights[0].T
    block = shard_block(qkv_proj, out_proj)
    column = jnp.stack(neighbour_relay(block, seq_count))
    other = swapped(column, "seq")
    parts = [column, other, swapped(column, "groups"), swapped(other, "groups")]
    parts += [swapped(part, "pipe") for part in parts]

    table = dispatch(tokens_t, routes_t, moe_gain.reshape(1, width))
    outgoing = table.reshape(seq_count, per_device // 2, CAP, width)
    received = lax.all_to_all(outgoing, "seq", split_axis=0, concat_axis=0, tiled=True)
    finished = run_experts(received, gate_up, down_proj)
    summed = lax.all_to_all(finished, "seq", split_axis=0, concat_axis=0, tiled=True)
    summed = summed.reshape(E * CAP, width)
    residual, coarse, fine = returns(tokens_t, routes_t, scale_t)
    place = place_of()
    packed, hidden_t = project_qkv(
        place, summed, residual, coarse, fine, attn_gain.reshape(1, width), parts, rows, qkv_width // 4
    )
    query_width = QUERY_HEADS * HEAD_SIZE
    halo = halo_exchange(packed[tok_count - WINDOW_SPAN :, query_width:])
    columns = block.shape[1] - qkv_width // 4
    out_t = attend_and_project(place, jnp.exp(sinks), packed, halo, hidden_t, parts, columns, depth)
    return out_t.T[None]


def swapped(value, axis):
    return lax.ppermute(value, axis, [(i, i ^ 1) for i in range(lax.axis_size(axis))])


def rms_scale(value_matrix, gain):
    widened = value_matrix.astype(jnp.float32)
    mean_square = jnp.mean(widened * widened, axis=-1, keepdims=True)
    return (widened * lax.rsqrt(mean_square + eps) * gain).astype(jnp.bfloat16)


def routing_tables(route_rows, route_scale):
    tok_count = route_rows.shape[0]
    experts = jnp.arange(E, dtype=jnp.int32)
    named = route_rows[None, :, :] == experts[:, None, None]
    member = jnp.any(named, axis=2)
    scale = jnp.sum(jnp.where(named, route_scale[None, :, :], 0.0), axis=2)
    token = jnp.arange(tok_count, dtype=jnp.int32)
    before = (token[:, None] < token[None, :]).astype(jnp.bfloat16)
    rank = jnp.dot(member.astype(jnp.bfloat16), before, preferred_element_type=jnp.float32)
    slot = jnp.arange(CAP, dtype=jnp.float32)
    chosen = member[:, None, :] & (rank[:, None, :] == slot[None, :, None])
    select = chosen.reshape(E * CAP, tok_count).astype(jnp.bfloat16)
    weighted = jnp.where(chosen, scale[:, None, :], 0.0).reshape(E * CAP, tok_count)
    return select, weighted


def neighbour_relay(block, seq_count):
    rounds = seq_count // 2
    up = [(i, i + 2) for i in range(seq_count - 2)]
    down = [(i + 2, i) for i in range(seq_count - 2)]
    rising, falling = [block], [block]
    for _ in range(rounds - 1):
        rising.append(lax.ppermute(rising[-1], "seq", up))
        falling.append(lax.ppermute(falling[-1], "seq", down))
    line = lax.axis_index("seq") // 2
    blocks = [block]
    for k in range(1, rounds):
        blocks.append(jnp.where(line >= k, rising[k], falling[rounds - k]))
    return blocks


def gather_weights(qkv_proj, out_proj):
    seq_count = lax.axis_size("seq")
    rows, qkv_width = qkv_proj.shape
    depth, width = out_proj.shape
    group_bit = lax.axis_index("groups") % 2
    pipe_bit = lax.axis_index("pipe")
    quarter = group_bit * 2 + pipe_bit
    qw, ow = qkv_width // 4, width // 4
    fold = ow // rows
    mine_qkv = lax.dynamic_slice_in_dim(qkv_proj, quarter * qw, qw, 1)
    mine_out = lax.dynamic_slice_in_dim(out_proj.T, quarter * ow, ow, 0)
    block = jnp.concatenate(
        [mine_qkv] + [mine_out[i * rows : (i + 1) * rows] for i in range(fold)], axis=1
    )
    blocks = neighbour_relay(block, seq_count)
    lines = seq_count // 2
    line = lax.axis_index("seq") // 2
    stacked = jnp.stack(blocks)
    column = jnp.stack(
        [lax.dynamic_index_in_dim(stacked, (line - j) % lines, 0, keepdims=False) for j in range(lines)]
    )
    other = swapped(column, "seq")
    odd = lax.axis_index("seq") % 2 == 1
    both = jnp.stack([jnp.where(odd, other, column), jnp.where(odd, column, other)], axis=1)
    both = both.reshape(seq_count, rows, block.shape[1])
    across = swapped(both, "groups")
    high = group_bit == 1
    halves = jnp.stack([jnp.where(high, across, both), jnp.where(high, both, across)])
    beside = swapped(halves, "pipe")
    second = pipe_bit == 1
    whole = jnp.stack([jnp.where(second, beside, halves), jnp.where(second, halves, beside)], axis=1)
    whole = whole.reshape(4, seq_count, rows, block.shape[1])
    qkv_full = whole[..., :qw].transpose(1, 2, 0, 3).reshape(seq_count * rows, qkv_width)
    out_full = whole[..., qw:].reshape(4, seq_count, rows, fold, depth)
    out_full = out_full.transpose(1, 4, 0, 3, 2).reshape(seq_count * depth, width)
    return qkv_full, out_full


def expert_layer(local, route_rows, route_scale, moe_gain, gate_up, down_proj):
    tok_count, width = local.shape
    seq_count = lax.axis_size("seq")
    per_device = gate_up.shape[0]
    normed = rms_scale(local, moe_gain)
    select, weighted = routing_tables(route_rows, route_scale)
    table = jnp.dot(select, normed, preferred_element_type=jnp.float32).astype(jnp.bfloat16)
    by_expert = table.reshape(E, CAP, width)
    experts = max(1, per_device // 2)
    slabs = per_device // experts
    if slabs == 1:
        by_expert = jnp.repeat(by_expert, 2, axis=0)
    outgoing = by_expert.reshape(seq_count, experts, CAP, width)
    received = lax.all_to_all(outgoing, "seq", split_axis=0, concat_axis=0, tiled=True)
    rows = received.transpose(1, 0, 2, 3).reshape(experts, seq_count * CAP, width)
    gate_up = gate_up.reshape(experts, slabs, width, 2 * HALF)
    down_proj = down_proj.reshape(experts, slabs, HALF, width)
    projected = jnp.einsum("erd,ekdh->ekrh", rows, gate_up, preferred_element_type=jnp.float32)
    gate_part = projected[..., :HALF]
    up_part = projected[..., HALF:]
    hidden = (gate_part * jax.nn.sigmoid(1.702 * gate_part) * (up_part + 1.0)).astype(jnp.bfloat16)
    partial_value = jnp.einsum(
        "ekrh,ekhd->erd", hidden, down_proj, preferred_element_type=jnp.float32
    ).reshape(experts, seq_count, CAP, width)
    partial_value = partial_value.transpose(1, 0, 2, 3)
    if slabs == 2:
        finished = partial_value.astype(jnp.bfloat16)
    else:
        first = lax.axis_index("seq") % 2 == 0
        lower_rows = partial_value[:, :, : CAP // 2]
        upper_rows = partial_value[:, :, CAP // 2 :]
        kept = jnp.where(first, lower_rows, upper_rows)
        given = jnp.where(first, upper_rows, lower_rows)
        partner_part = swapped(given.astype(jnp.bfloat16), "seq").astype(given.dtype)
        finished = (kept + partner_part).astype(jnp.bfloat16)
    summed = lax.all_to_all(finished, "seq", split_axis=0, concat_axis=0, tiled=True).reshape(
        E * CAP, width
    )
    coarse = weighted.astype(jnp.bfloat16)
    fine = (weighted - coarse.astype(jnp.float32)).astype(jnp.bfloat16)
    dims = (((0,), (0,)), ((), ()))
    mixed = lax.dot_general(coarse, summed, dims, preferred_element_type=jnp.float32)
    mixed += lax.dot_general(fine, summed, dims, preferred_element_type=jnp.float32)
    return (local.astype(jnp.float32) + mixed).astype(jnp.bfloat16)


def attend(query_matrix, keys_extended, values_extended, head_sink_logits, halo_valid):
    tok_count = query_matrix.shape[0]
    query_groups = QUERY_HEADS // KEY_VALUE_HEADS
    scale = float(HEAD_SIZE) ** (-0.5)
    sink_mass_total = jnp.exp(head_sink_logits).reshape(KEY_VALUE_HEADS, query_groups, 1, 1)
    block_queries = query_matrix.reshape(tok_count, KEY_VALUE_HEADS, query_groups, HEAD_SIZE)
    block_keys = keys_extended.reshape(tok_count + WINDOW_SPAN, KEY_VALUE_HEADS, HEAD_SIZE)
    block_values = values_extended.reshape(tok_count + WINDOW_SPAN, KEY_VALUE_HEADS, HEAD_SIZE)
    scores = (
        jnp.einsum("qhgd,khd->hgqk", block_queries, block_keys, preferred_element_type=jnp.float32)
        * scale
    )
    query_pos = jnp.arange(tok_count, dtype=jnp.int32)[:, None] + WINDOW_SPAN
    key_pos = jnp.arange(tok_count + WINDOW_SPAN, dtype=jnp.int32)[None, :]
    distance = query_pos - key_pos
    allowed = (distance >= 0) & (distance < WINDOW_SPAN) & ((key_pos >= WINDOW_SPAN) | halo_valid)
    weights = jnp.where(allowed, jnp.exp(scores), 0.0)
    probs = (weights / (jnp.sum(weights, axis=-1, keepdims=True) + sink_mass_total)).astype(
        jnp.bfloat16
    )
    mixed = jnp.einsum("hgqk,khd->qhgd", probs, block_values, preferred_element_type=jnp.float32)
    return mixed.reshape(tok_count, QUERY_HEADS * HEAD_SIZE).astype(jnp.bfloat16)


def halo_exchange(pairs):
    seq_count, pipe_count = lax.axis_size("seq"), lax.axis_size("pipe")
    order = [s * pipe_count + p for p in range(pipe_count) for s in range(seq_count)]
    return lax.ppermute(pairs, ("seq", "pipe"), list(zip(order[:-1], order[1:])))


def body(
    tokens,
    routes,
    route_weights,
    moe_gain,
    gate_up,
    down_proj,
    attn_gain,
    qkv_proj,
    head_sink_logits,
    out_proj,
):
    if gate_up.shape[0] % 2 == 0 and out_proj.shape[0] % 128 == 0 and tokens.shape[1] == WINDOW_SPAN:
        return fused_body(
            tokens,
            routes,
            route_weights,
            moe_gain,
            gate_up,
            down_proj,
            attn_gain,
            qkv_proj,
            head_sink_logits,
            out_proj,
        )
    qkv_full, out_full = gather_weights(qkv_proj, out_proj)
    hidden = expert_layer(tokens[0], routes[0], route_weights[0], moe_gain, gate_up, down_proj)
    tok_count, width = hidden.shape
    normed = rms_scale(hidden, attn_gain)
    seq_index = lax.axis_index("seq")
    pipe_index = lax.axis_index("pipe")
    halo_valid = (seq_index > 0) | (pipe_index > 0)
    query_width = QUERY_HEADS * HEAD_SIZE
    width_of_pair = KEY_VALUE_HEADS * HEAD_SIZE
    packed_heads = jnp.dot(normed, qkv_full, preferred_element_type=jnp.float32).astype(
        jnp.bfloat16
    )
    own_pairs = packed_heads[:, query_width:]
    halo_pairs = halo_exchange(own_pairs[tok_count - WINDOW_SPAN :])
    query_matrix = packed_heads[:, :query_width]
    pairs_ext = jnp.concatenate([halo_pairs, own_pairs], axis=0)
    keys_extended = pairs_ext[:, :width_of_pair]
    values_extended = pairs_ext[:, width_of_pair:]
    attended = attend(query_matrix, keys_extended, values_extended, head_sink_logits, halo_valid)
    projected = jnp.dot(attended, out_full, preferred_element_type=jnp.float32)
    return (hidden.astype(jnp.float32) + projected).astype(jnp.bfloat16)[None]


def solution(mesh):
    in_specs = (
        P("pipe", ("groups", "seq"), None),
        P("pipe", ("groups", "seq"), None),
        P("pipe", ("groups", "seq"), None),
        P(),
        P("seq", None, None),
        P("seq", None, None),
        P(),
        P("seq", None),
        P(),
        P("seq", None),
    )
    out_specs = P("pipe", ("groups", "seq"), None)
    return jax.shard_map(body, mesh=mesh, in_specs=in_specs, out_specs=out_specs, check_vma=False)
```

time: 387 us -> 226 us (0.58)
  waiting for transfers between devices: 289 us -> 130 us
  matrix products: 43.3 us -> 0 us
  Pallas kernels: 0 us -> 37.8 us
  starting transfers between devices: 18.7 us -> 48.5 us
  between operations: 13.6 us -> 0.42 us
  local copies, waits for them, and re-layouts: 17.5 us -> 6.17 us
    all_to_all x2, waiting for transfers between devices: 280 us -> 0.01 us  [the longest x1 0.01 us: fused_body(): lax.all_to_all(outgoing, 'seq', split_axis=0, concat_axis=0, tiled=True)]
    ppermute x2 -> x14, waiting for transfers between devices: 7.05 us -> 130 us  [the longest x7 72.5 us: swapped(): lax.ppermute(value, axis, [(i, i ^ 1) for i in range(lax.axis_size(axis))])]
    dot_general x8 -> x0, matrix products: 43.3 us -> none  [the longest x1 16.6 us: expert_layer(): jnp.einsum('spcd,pdh->spch', received, gate_up, preferred_element_type=jn...]
    pallas_call x0 -> x5, Pallas kernels: none -> 37.8 us  [the longest x1 16.1 us: run_experts(): pl.pallas_call(experts_kernel, out_shape=jax.ShapeDtypeStruct(received.sh...]
    ppermute x2 -> x14, starting transfers between devices: 2.38 us -> 37.1 us  [the longest x3 25.3 us: neighbour_relay(): rising.append(lax.ppermute(rising[-1], 'seq', up))]
    all_to_all x2, starting transfers between devices: 16.3 us -> 11.4 us  [the longest x1 6.9 us: fused_body(): lax.all_to_all(outgoing, 'seq', split_axis=0, concat_axis=0, tiled=True)]
    convert_element_type x3 -> x0, local copies, waits for them, and re-layouts: 4.59 us -> none  [the longest x1 2.8 us: expert_layer(): jnp.dot(select, repeated, preferred_element_type=jnp.float32)]
    unnamed x10 -> x16, local copies, waits for them, and re-layouts: 7.8 us -> 4.5 us
  transfers between devices with their start and end apart: 6 -> 16, of which waited for: 4 -> 8; matrix products, arithmetic and copies ran while one was open for 15% -> 1% of each run, Pallas kernels for 0% -> 10%
where the time goes in v1:
time: 226 us; the launch traced here: 223 us
  waiting for transfers between devices  130 us (58%)
  starting transfers between devices  48.5 us (21%)
  Pallas kernels  37.8 us (17%)
  local copies, waits for them, and re-layouts  6.17 us (3%)
    ppermute x7, waiting for transfers between devices, swapped(): lax.ppermute(value, axis, [(i, i ^ 1) for i in range(lax.axis_size(axis))])  72.5 us
    ppermute x3, waiting for transfers between devices, neighbour_relay(): rising.append(lax.ppermute(rising[-1], 'seq', up))  49.9 us
    ppermute x3, starting transfers between devices, neighbour_relay(): rising.append(lax.ppermute(rising[-1], 'seq', up))  25.3 us
    pallas_call x1, Pallas kernels, run_experts(): pl.pallas_call(experts_kernel, out_shape=jax.ShapeDtypeStruct(received.sh...  16.1 us
    pallas_call x1, Pallas kernels, attend_and_project(): pl.pallas_call(attention_kernel, out_shape=jax.ShapeDtypeStruct((width, t...  8.14 us
    pallas_call x1, Pallas kernels, project_qkv(): pl.pallas_call(functools.partial(qkv_kernel, rows), out_shape=(jax.ShapeD...  7.7 us
    all_to_all x1, starting transfers between devices, fused_body(): lax.all_to_all(outgoing, 'seq', split_axis=0, concat_axis=0, tiled=True)  6.9 us
    ppermute x3, waiting for transfers between devices, neighbour_relay(): falling.append(lax.ppermute(falling[-1], 'seq', down))  4.83 us
  transfers between devices with their start and end apart: 16, of which 8 were waited for; matrix products, arithmetic and copies ran while one was open for 1% of the time, Pallas kernels for 10%

profile of v1, /device:TPU:0, one launch (start us, length us, event | category | flops | bytes accessed | tf_op | source)
XLA Modules:
  0.0 223.4 jit_solution(7980607542518540524)
XLA Ops:
  0.0 1.0 dynamic-slice_bitcast_fusion
  1.1 0.2 copy-done
  1.4 5.0 %collective-permute-start = (bf16[184,1152]{1,0:T(8,128)(2,1)S(1)}, bf16[184,1152]{1,0:T(8,128)(2,1)S(1)}, u32[]{:S(2)}, u32[]{:S(2)}) collective-permute-start(bf16[184,1152]{1,0:T(8,128)(2,1)S(1)} %fusion.2), channel_id=1, source_target_pairs={{0,4},{2,6},{4,8},{6,10},{8,12},{10,14},{1,5},{3,7},{5,9},{7,11},{... | collective-permute-start | bytes 1271816 | tf_op jit(solution)/shard_map/ppermute | solution.py:407
  6.3 1.3 collective-permute-start.1
  7.7 0.6 reshape.12.gain_ref
  8.3 3.7 %dispatch.1 = bf16[16,48,1440]{2,1,0:T(8,128)(2,1)} custom-call(bf16[1440,128]{1,0:T(8,128)(2,1)} %bitcast.29, s32[4,128]{1,0:T(4,128)} %bitcast.31, f32[1,1440]{1,0:T(1,128)} %reshape.12.gain_ref), custom_call_target="tpu_custom_call" | custom-call | tf_op jit(solution)/shard_map/dispatch/pallas_call | solution.py:58
  12.0 6.9 %all-to-all-start = ((bf16[8,2,48,1440]{3,2,1,0:T(8,128)(2,1)}), bf16[8,2,48,1440]{3,2,1,0:T(8,128)(2,1)}, u32[]{:S(2)}, u32[]{:S(2)}) async-start(bf16[8,2,48,1440]{3,2,1,0:T(8,128)(2,1)} %bitcast.28), calls=%async_computation | async-start | bytes 4718592 | tf_op jit(solution)/shard_map/all_to_all | solution.py:359
  18.9 0.0 collective-permute-done
  18.9 3.9 %collective-permute-start.4 = (bf16[184,1152]{1,0:T(8,128)(2,1)S(1)}, bf16[184,1152]{1,0:T(8,128)(2,1)S(1)}, u32[]{:S(2)}, u32[]{:S(2)}) collective-permute-start(bf16[184,1152]{1,0:T(8,128)(2,1)S(1)} %collective-permute-done), channel_id=1, source_target_pairs={{0,4},{2,6},{4,8},{6,10},{8,12},{10,14},{1,5},{3,7},{5,9},{7,11},{... | collective-permute-start | bytes 1271816 | tf_op jit(solution)/shard_map/ppermute | solution.py:407
  22.8 0.0 collective-permute-done.1
  22.8 1.3 collective-permute-start.2
  24.2 42.1 %collective-permute-done.4 = bf16[184,1152]{1,0:T(8,128)(2,1)S(1)} collective-permute-done((bf16[184,1152]{1,0:T(8,128)(2,1)S(1)}, bf16[184,1152]{1,0:T(8,128)(2,1)S(1)}, u32[]{:S(2)}, u32[]{:S(2)}) %collective-permute-start.4) | collective-permute-done | bytes 423968 | tf_op jit(solution)/shard_map/ppermute | solution.py:407
  66.3 16.3 %collective-permute-start.5 = (bf16[184,1152]{1,0:T(8,128)(2,1)S(1)}, bf16[184,1152]{1,0:T(8,128)(2,1)S(1)}, u32[]{:S(2)}, u32[]{:S(2)}) collective-permute-start(bf16[184,1152]{1,0:T(8,128)(2,1)S(1)} %collective-permute-done.4), channel_id=1, source_target_pairs={{0,4},{2,6},{4,8},{6,10},{8,12},{10,14},{1,5},{3,7},{5,9},{7,11},{... | collective-permute-start | bytes 1271816 | tf_op jit(solution)/shard_map/ppermute | solution.py:407
  82.6 0.0 collective-permute-done.2
  82.6 1.3 collective-permute-start.3
  83.9 0.1 select_bitcast_fusion.1
  84.0 7.8 %collective-permute-done.5 = bf16[184,1152]{1,0:T(8,128)(2,1)S(1)} collective-permute-done((bf16[184,1152]{1,0:T(8,128)(2,1)S(1)}, bf16[184,1152]{1,0:T(8,128)(2,1)S(1)}, u32[]{:S(2)}, u32[]{:S(2)}) %collective-permute-start.5) | collective-permute-done | bytes 423968 | tf_op jit(solution)/shard_map/ppermute | solution.py:407
  91.8 0.1 select_bitcast_fusion
  91.9 4.8 %collective-permute-done.3 = bf16[184,1152]{1,0:T(8,128)(2,1)S(1)} collective-permute-done((bf16[184,1152]{1,0:T(8,128)(2,1)S(1)}, bf16[184,1152]{1,0:T(8,128)(2,1)S(1)}, u32[]{:S(2)}, u32[]{:S(2)}) %collective-permute-start.3) | collective-permute-done | bytes 423968 | tf_op jit(solution)/shard_map/ppermute | solution.py:408
  96.7 0.1 select_bitcast_fusion.2
  96.7 0.3 pad_maximum_fusion.rest_0_
  97.0 0.7 collective-permute-start.6
  97.7 0.0 all-to-all-done.rows_ref
  97.7 16.1 %experts.1 = bf16[8,2,48,1440]{3,2,1,0:T(8,128)(2,1)S(1)} custom-call(bf16[8,2,48,1440]{3,2,1,0:T(8,128)(2,1)} %all-to-all-done.rows_ref, bf16[4,1440,1440]{2,1,0:T(8,128)(2,1)} %gate_up_ref.1, bf16[4,720,1440]{2,1,0:T(8,128)(2,1)} %down_ref.1), custom_call_target="tpu_custom_call" | custom-call | tf_op jit(solution)/shard_map/experts/pallas_call | solution.py:128
  113.9 1.4 copy-done.1
  115.3 4.5 %all-to-all-start.1 = ((bf16[8,2,48,1440]{3,2,1,0:T(8,128)(2,1)}), bf16[8,2,48,1440]{3,2,1,0:T(8,128)(2,1)}, u32[]{:S(2)}, u32[]{:S(2)}) async-start(bf16[8,2,48,1440]{3,2,1,0:T(8,128)(2,1)} %copy-done.1), calls=%async_computation.1 | async-start | bytes 4718592 | tf_op jit(solution)/shard_map/all_to_all | solution.py:361
  119.8 1.6 collective-permute-start.7
  121.4 30.4 %collective-permute-done.6.rest_1_ = bf16[4,184,1152]{2,1,0:T(8,128)(2,1)} collective-permute-done((bf16[4,184,1152]{2,1,0:T(8,128)(2,1)S(1)}, bf16[4,184,1152]{2,1,0:T(8,128)(2,1)}, u32[]{:S(2)}, u32[]{:S(2)}) %collective-permute-start.6) | collective-permute-done | bytes 1695776 | tf_op jit(solution)/shard_map/ppermute | solution.py:376
  151.8 1.5 collective-permute-start.8
  153.3 0.0 collective-permute-start.9
  153.3 0.5 collective-permute-start.10
  153.8 6.1 %collective-permute-done.7.rest_2_ = bf16[4,184,1152]{2,1,0:T(8,128)(2,1)} collective-permute-done((bf16[4,184,1152]{2,1,0:T(8,128)(2,1)S(1)}, bf16[4,184,1152]{2,1,0:T(8,128)(2,1)}, u32[]{:S(2)}, u32[]{:S(2)}) %collective-permute-start.7) | collective-permute-done | bytes 1695776 | tf_op jit(solution)/shard_map/ppermute | solution.py:376
  159.9 0.0 collective-permute-start.11
  159.9 34.2 %collective-permute-done.8.rest_3_ = bf16[4,184,1152]{2,1,0:T(8,128)(2,1)} collective-permute-done((bf16[4,184,1152]{2,1,0:T(8,128)(2,1)}, bf16[4,184,1152]{2,1,0:T(8,128)(2,1)}, u32[]{:S(2)}, u32[]{:S(2)}) %collective-permute-start.8) | collective-permute-done | bytes 1695776 | tf_op jit(solution)/shard_map/ppermute | solution.py:376
  194.1 0.0 collective-permute-start.12
  194.1 2.1 returns.1
  196.2 0.1 pad_add_fusion.place_ref
  196.3 0.0 collective-permute-done.9.rest_4_
  196.3 0.0 collective-permute-done.11.rest_6_
  196.3 1.7 collective-permute-done.12.rest_7_
  198.1 0.0 all-to-all-done.1
  198.1 1.0 copy-done.2
  199.1 0.9 copy-done.3
  200.0 0.9 copy-done.4
  200.9 7.7 %qkv.1 = (bf16[128,2560]{1,0:T(8,128)(2,1)S(1)}, bf16[1440,128]{1,0:T(8,128)(2,1)S(1)}) custom-call(s32[4]{0:T(128)S(1)} %pad_add_fusion.place_ref, bf16[768,1440]{1,0:T(8,128)(2,1)} %bitcast.9.tables_ref, bf16[128,1440]{1,0:T(8,128)(2,1)S(1)} %copy-done.2, bf16[128,768]{1,0:T(8,128)(2,1)S(1)} %copy-done.3, bf16[128,768]{1,0:T(8,128)(2,1)S(1)} %copy-done.4, ...), custom_call_target="tpu_custom_call" | custom-call | tf_op jit(solution)/shard_map/qkv/pallas_call | solution.py:191
  208.6 3.6 %collective-permute-start.13 = (bf16[128,512]{1,0:T(8,128)(2,1)S(1)}, bf16[128,512]{1,0:T(8,128)(2,1)S(1)}, u32[]{:S(2)}, u32[]{:S(2)}) collective-permute-start(bf16[128,512]{1,0:T(8,128)(2,1)S(1)} %slice.11), channel_id=1, source_target_pairs={{0,2},{2,4},{4,6},{6,8},{8,10},{10,12},{12,14},{14,1},{1,3},{3,5},... | collective-permute-start | bytes 393224 | tf_op jit(solution)/shard_map/ppermute | solution.py:527
  212.3 2.8 %collective-permute-done.13.halo_ref = bf16[128,512]{1,0:T(8,128)(2,1)S(1)} collective-permute-done((bf16[128,512]{1,0:T(8,128)(2,1)S(1)}, bf16[128,512]{1,0:T(8,128)(2,1)S(1)}, u32[]{:S(2)}, u32[]{:S(2)}) %collective-permute-start.13) | collective-permute-done | bytes 131104 | tf_op jit(solution)/shard_map/ppermute | solution.py:527
  215.1 8.1 %attention.1 = bf16[1440,128]{1,0:T(8,128)(2,1)} custom-call(s32[4]{0:T(128)S(1)} %pad_add_fusion.place_ref, f32[32]{0:T(128)S(1)} %exp.3.sink_ref, bf16[128,2560]{1,0:T(8,128)(2,1)S(1)} %get-tuple-element.13.packed_ref, bf16[128,512]{1,0:T(8,128)(2,1)S(1)} %collective-permute-done.13.halo_ref, bf16[1440,128]{1,0:T(8,128)(2,1)S(1)} %get-tuple-element.14.hidden_ref, ...), custom_call_target="tpu_custom_call" | custom-call | tf_op jit(solution)/shard_map/attention/pallas_call | solution.py:304
  (20 shorter events, 0.2 us)
Async XLA Ops:
  0.0 1.3 copy-start
  0.0 7.6 %copy-start.5 = (f32[1440]{0:T(1024)S(1)}, f32[1440]{0:T(1024)}, u32[]{:S(2)}) copy-start(f32[1440]{0:T(1024)} %param.13) | copy-start | bytes 17284
  1.4 17.5 %collective-permute-start = (bf16[184,1152]{1,0:T(8,128)(2,1)S(1)}, bf16[184,1152]{1,0:T(8,128)(2,1)S(1)}, u32[]{:S(2)}, u32[]{:S(2)}) collective-permute-start(bf16[184,1152]{1,0:T(8,128)(2,1)S(1)} %fusion.2), channel_id=1, source_target_pairs={{0,4},{2,6},{4,8},{6,10},{8,12},{10,14},{1,5},{3,7},{5,9},{7,11},{... | collective-permute-start | bytes 1271816 | tf_op jit(solution)/shard_map/ppermute | solution.py:407
  6.3 16.5 %collective-permute-start.1 = (bf16[184,1152]{1,0:T(8,128)(2,1)S(1)}, bf16[184,1152]{1,0:T(8,128)(2,1)S(1)}, u32[]{:S(2)}, u32[]{:S(2)}) collective-permute-start(bf16[184,1152]{1,0:T(8,128)(2,1)S(1)} %fusion.2), channel_id=1, source_target_pairs={{4,0},{6,2},{8,4},{10,6},{12,8},{14,10},{5,1},{7,3},{9,5},{11,7},{... | collective-permute-start | bytes 1271816 | tf_op jit(solution)/shard_map/ppermute | solution.py:408
  12.0 85.8 %all-to-all-start = ((bf16[8,2,48,1440]{3,2,1,0:T(8,128)(2,1)}), bf16[8,2,48,1440]{3,2,1,0:T(8,128)(2,1)}, u32[]{:S(2)}, u32[]{:S(2)}) async-start(bf16[8,2,48,1440]{3,2,1,0:T(8,128)(2,1)} %bitcast.28), calls=%async_computation | async-start | bytes 4718592 | tf_op jit(solution)/shard_map/all_to_all | solution.py:359
  18.9 47.4 %collective-permute-start.4 = (bf16[184,1152]{1,0:T(8,128)(2,1)S(1)}, bf16[184,1152]{1,0:T(8,128)(2,1)S(1)}, u32[]{:S(2)}, u32[]{:S(2)}) collective-permute-start(bf16[184,1152]{1,0:T(8,128)(2,1)S(1)} %collective-permute-done), channel_id=1, source_target_pairs={{0,4},{2,6},{4,8},{6,10},{8,12},{10,14},{1,5},{3,7},{5,9},{7,11},{... | collective-permute-start | bytes 1271816 | tf_op jit(solution)/shard_map/ppermute | solution.py:407
  22.8 59.8 %collective-permute-start.2 = (bf16[184,1152]{1,0:T(8,128)(2,1)S(1)}, bf16[184,1152]{1,0:T(8,128)(2,1)S(1)}, u32[]{:S(2)}, u32[]{:S(2)}) collective-permute-start(bf16[184,1152]{1,0:T(8,128)(2,1)S(1)} %collective-permute-done.1), channel_id=1, source_target_pairs={{4,0},{6,2},{8,4},{10,6},{12,8},{14,10},{5,1},{7,3},{9,5},{11,7},{... | collective-permute-start | bytes 1271816 | tf_op jit(solution)/shard_map/ppermute | solution.py:408
  66.3 25.5 %collective-permute-start.5 = (bf16[184,1152]{1,0:T(8,128)(2,1)S(1)}, bf16[184,1152]{1,0:T(8,128)(2,1)S(1)}, u32[]{:S(2)}, u32[]{:S(2)}) collective-permute-start(bf16[184,1152]{1,0:T(8,128)(2,1)S(1)} %collective-permute-done.4), channel_id=1, source_target_pairs={{0,4},{2,6},{4,8},{6,10},{8,12},{10,14},{1,5},{3,7},{5,9},{7,11},{... | collective-permute-start | bytes 1271816 | tf_op jit(solution)/shard_map/ppermute | solution.py:407
  82.6 14.0 %collective-permute-start.3 = (bf16[184,1152]{1,0:T(8,128)(2,1)S(1)}, bf16[184,1152]{1,0:T(8,128)(2,1)S(1)}, u32[]{:S(2)}, u32[]{:S(2)}) collective-permute-start(bf16[184,1152]{1,0:T(8,128)(2,1)S(1)} %collective-permute-done.2), channel_id=1, source_target_pairs={{4,0},{6,2},{8,4},{10,6},{12,8},{14,10},{5,1},{7,3},{9,5},{11,7},{... | collective-permute-start | bytes 1271816 | tf_op jit(solution)/shard_map/ppermute | solution.py:408
  97.0 54.8 %collective-permute-start.6 = (bf16[4,184,1152]{2,1,0:T(8,128)(2,1)S(1)}, bf16[4,184,1152]{2,1,0:T(8,128)(2,1)}, u32[]{:S(2)}, u32[]{:S(2)}) collective-permute-start(bf16[4,184,1152]{2,1,0:T(8,128)(2,1)S(1)} %pad_maximum_fusion.rest_0_), channel_id=1, source_target_pairs={{0,2},{2,0},{4,6},{6,4},{8,10},{10,8},{12,14},{14,12},{1,3},{3,1},... | collective-permute-start | bytes 5087240 | tf_op jit(solution)/shard_map/ppermute | solution.py:376
  113.9 1.4 copy-start.1
  115.3 80.9 %copy-start.6 = (f32[1440]{0:T(1024)S(1)}, f32[1440]{0:T(1024)}, u32[]{:S(2)}) copy-start(f32[1440]{0:T(1024)} %param.16) | copy-start | bytes 17284
  115.3 82.8 %all-to-all-start.1 = ((bf16[8,2,48,1440]{3,2,1,0:T(8,128)(2,1)}), bf16[8,2,48,1440]{3,2,1,0:T(8,128)(2,1)}, u32[]{:S(2)}, u32[]{:S(2)}) async-start(bf16[8,2,48,1440]{3,2,1,0:T(8,128)(2,1)} %copy-done.1), calls=%async_computation.1 | async-start | bytes 4718592 | tf_op jit(solution)/shard_map/all_to_all | solution.py:361
  119.8 40.1 %collective-permute-start.7 = (bf16[4,184,1152]{2,1,0:T(8,128)(2,1)S(1)}, bf16[4,184,1152]{2,1,0:T(8,128)(2,1)}, u32[]{:S(2)}, u32[]{:S(2)}) collective-permute-start(bf16[4,184,1152]{2,1,0:T(8,128)(2,1)S(1)} %pad_maximum_fusion.rest_0_), channel_id=1, source_target_pairs={{0,16},{16,0},{1,17},{17,1},{2,18},{18,2},{3,19},{19,3},{4,20},{20... | collective-permute-start | bytes 5087240 | tf_op jit(solution)/shard_map/ppermute | solution.py:376
  151.8 42.4 %collective-permute-start.8 = (bf16[4,184,1152]{2,1,0:T(8,128)(2,1)}, bf16[4,184,1152]{2,1,0:T(8,128)(2,1)}, u32[]{:S(2)}, u32[]{:S(2)}) collective-permute-start(bf16[4,184,1152]{2,1,0:T(8,128)(2,1)} %collective-permute-done.6.rest_1_), channel_id=1, source_target_pairs={{0,16},{16,0},{1,17},{17,1},{2,18},{18,2},{3,19},{19,3},{4,20},{20... | collective-permute-start | bytes 5087240 | tf_op jit(solution)/shard_map/ppermute | solution.py:376
  153.3 43.0 %collective-permute-start.9 = (bf16[4,184,1152]{2,1,0:T(8,128)(2,1)S(1)}, bf16[4,184,1152]{2,1,0:T(8,128)(2,1)}, u32[]{:S(2)}, u32[]{:S(2)}) collective-permute-start(bf16[4,184,1152]{2,1,0:T(8,128)(2,1)S(1)} %pad_maximum_fusion.rest_0_), channel_id=1, source_target_pairs={{0,1},{1,0},{2,3},{3,2},{4,5},{5,4},{6,7},{7,6},{8,9},{9,8},{10,11... | collective-permute-start | bytes 5087240 | tf_op jit(solution)/shard_map/ppermute | solution.py:376
  153.3 43.0 %collective-permute-start.10 = (bf16[4,184,1152]{2,1,0:T(8,128)(2,1)}, bf16[4,184,1152]{2,1,0:T(8,128)(2,1)}, u32[]{:S(2)}, u32[]{:S(2)}) collective-permute-start(bf16[4,184,1152]{2,1,0:T(8,128)(2,1)} %collective-permute-done.6.rest_1_), channel_id=1, source_target_pairs={{0,1},{1,0},{2,3},{3,2},{4,5},{5,4},{6,7},{7,6},{8,9},{9,8},{10,11... | collective-permute-start | bytes 5087240 | tf_op jit(solution)/shard_map/ppermute | solution.py:376
  159.9 36.4 %collective-permute-start.11 = (bf16[4,184,1152]{2,1,0:T(8,128)(2,1)}, bf16[4,184,1152]{2,1,0:T(8,128)(2,1)}, u32[]{:S(2)}, u32[]{:S(2)}) collective-permute-start(bf16[4,184,1152]{2,1,0:T(8,128)(2,1)} %collective-permute-done.7.rest_2_), channel_id=1, source_target_pairs={{0,1},{1,0},{2,3},{3,2},{4,5},{5,4},{6,7},{7,6},{8,9},{9,8},{10,11... | collective-permute-start | bytes 5087240 | tf_op jit(solution)/shard_map/ppermute | solution.py:376
  194.1 3.9 %collective-permute-start.12 = (bf16[4,184,1152]{2,1,0:T(8,128)(2,1)}, bf16[4,184,1152]{2,1,0:T(8,128)(2,1)}, u32[]{:S(2)}, u32[]{:S(2)}) collective-permute-start(bf16[4,184,1152]{2,1,0:T(8,128)(2,1)} %collective-permute-done.8.rest_3_), channel_id=1, source_target_pairs={{0,1},{1,0},{2,3},{3,2},{4,5},{5,4},{6,7},{7,6},{8,9},{9,8},{10,11... | collective-permute-start | bytes 5087240 | tf_op jit(solution)/shard_map/ppermute | solution.py:376
  198.1 1.0 copy-start.2
  199.1 0.9 copy-start.3
  200.0 0.9 copy-start.4
  200.9 11.4 %copy-start.7 = (f32[32]{0:T(128)S(1)}, f32[32]{0:T(128)}, u32[]{:S(2)}) copy-start(f32[32]{0:T(128)} %param.18) | copy-start | bytes 388
  208.6 6.5 %collective-permute-start.13 = (bf16[128,512]{1,0:T(8,128)(2,1)S(1)}, bf16[128,512]{1,0:T(8,128)(2,1)S(1)}, u32[]{:S(2)}, u32[]{:S(2)}) collective-permute-start(bf16[128,512]{1,0:T(8,128)(2,1)S(1)} %slice.11), channel_id=1, source_target_pairs={{0,2},{2,4},{4,6},{6,8},{8,10},{10,12},{12,14},{14,1},{1,3},{3,5},... | collective-permute-start | bytes 393224 | tf_op jit(solution)/shard_map/ppermute | solution.py:527

commit v2 on v1

--- a/solution.py
+++ b/solution.py
@@ -7,8 +7,8 @@
 from jax.experimental.pallas import tpu as pltpu
 from jax.sharding import PartitionSpec as P
 
+
 E = 16
-TOP = 4
 QUERY_HEADS = 32
 KEY_VALUE_HEADS = 4
 HEAD_SIZE = 64
@@ -24,7 +24,7 @@
 BF16 = jnp.bfloat16
 VMEM = pl.BlockSpec(memory_space=pltpu.VMEM)
 SMEM = pl.BlockSpec(memory_space=pltpu.SMEM)
-ANY = pl.BlockSpec(memory_space=pl.ANY)
+HBM = pl.BlockSpec(memory_space=pltpu.HBM)
 
 
 def route_slots(routes_ref):
@@ -127,7 +127,7 @@
     rows_spec = pl.BlockSpec((seq_count, None, cap, width), lambda e, k: (0, e, 0, 0))
     return pl.pallas_call(
         experts_kernel,
-        out_shape=jax.ShapeDtypeStruct(received.shape, BF16),
+        out_shape=pltpu.HBM(received.shape, BF16),
         grid=(experts, slabs),
         in_specs=[
             rows_spec,
@@ -141,6 +141,10 @@
     )(received, gate_up, down_proj)
 
 
+def in_hbm(parts):
+    return [pltpu.with_memory_space_constraint(part, pltpu.HBM) for part in parts]
+
+
 def shard_of(place_ref, step, flip, lines):
     line = lax.rem(place_ref[0] - step + lines, lines)
     return line * 2 + (place_ref[1] + flip) % 2
@@ -154,10 +158,10 @@
     rows, place_ref, tables_ref, residual_ref, coarse_ref, fine_ref, gain_ref, *rest
 ):
     parts, (packed_ref, hidden_ref, held, slices, sems) = rest[:8], rest[8:]
-    lines, padded, columns = held.shape[1:]
+    lines, _, columns = held.shape[1:]
     copies = []
     for i, part in enumerate(parts):
-        copy = pltpu.make_async_copy(part.at[:, :, pl.ds(0, columns)], held.at[i], sems.at[i])
+        copy = pltpu.make_async_copy(part, held.at[i], sems.at[i])
         copy.start()
         copies.append(copy)
     table = tables_ref[...]
@@ -194,7 +198,7 @@
             jax.ShapeDtypeStruct((tok_count, 4 * columns), BF16),
             jax.ShapeDtypeStruct((width, tok_count), BF16),
         ),
-        in_specs=[SMEM] + [VMEM] * 5 + [ANY] * 8,
+        in_specs=[SMEM] + [VMEM] * 5 + [HBM] * 8,
         out_specs=(VMEM, VMEM),
         scratch_shapes=[
             pltpu.VMEM((8, lines, padded, columns), BF16),
@@ -203,23 +207,17 @@
         ],
         compiler_params=pltpu.CompilerParams(vmem_limit_bytes=40 << 20),
         name="qkv",
-    )(place, tables, residual, coarse, fine, gain, *parts)
+    )(place, tables, residual, coarse, fine, gain, *in_hbm(parts))
 
 
 def attention_kernel(
     place_ref, sink_ref, packed_ref, halo_ref, hidden_ref, *rest
 ):
     parts, (out_ref, held, mixed, total_ref, sems) = rest[:8], rest[8:]
-    lines, padded, columns = held.shape[1:]
-    depth = mixed.shape[2]
-    fold = columns // depth
-    quarter_rows = out_ref.shape[0] // 4
-    first_column = parts[0].shape[2] - columns
+    lines, quarter_rows, depth = held.shape[1:]
     copies = []
     for i, part in enumerate(parts):
-        copy = pltpu.make_async_copy(
-            part.at[:, :, pl.ds(first_column, columns)], held.at[i], sems.at[i]
-        )
+        copy = pltpu.make_async_copy(part, held.at[i], sems.at[i])
         copy.start()
         copies.append(copy)
     tok_count = packed_ref.shape[0]
@@ -279,42 +277,38 @@
             ].astype(BF16)
 
     for pair in range(4):
-        totals = [jnp.zeros((padded, tok_count), F32) for _ in range(fold)]
+        total = jnp.zeros((quarter_rows, tok_count), F32)
         for flip in range(2):
             copies[pair * 2 + flip].wait()
             for step in range(lines):
-                against = mixed[shard_of(place_ref, step, flip, lines)]
-                for i in range(fold):
-                    totals[i] += lax.dot_general(
-                        held[pair * 2 + flip, step, :, i * depth : (i + 1) * depth],
-                        against,
-                        (((1,), (1,)), ((), ())),
-                        preferred_element_type=F32,
-                    )
+                total += lax.dot_general(
+                    held[pair * 2 + flip, step],
+                    mixed[shard_of(place_ref, step, flip, lines)],
+                    (((1,), (1,)), ((), ())),
+                    preferred_element_type=F32,
+                )
         start = quarter_of(place_ref, pair % 2, pair // 2) * quarter_rows
-        for i in range(fold):
-            count = min(padded, quarter_rows - i * padded)
-            total_ref[pl.ds(pl.multiple_of(start + i * padded, 8), count), :] = totals[i][:count]
+        total_ref[pl.ds(pl.multiple_of(start, 8), quarter_rows), :] = total
     out_ref[...] = (hidden_ref[...].astype(F32) + total_ref[...]).astype(BF16)
 
 
-def attend_and_project(place, sinks, packed, halo, hidden_t, parts, columns, depth):
+def attend_and_project(place, sinks, packed, halo, hidden_t, parts):
     width, tok_count = hidden_t.shape
-    lines, padded = parts[0].shape[:2]
+    lines, quarter_rows, depth = parts[0].shape
     return pl.pallas_call(
         attention_kernel,
         out_shape=jax.ShapeDtypeStruct((width, tok_count), BF16),
-        in_specs=[SMEM] * 2 + [VMEM] * 3 + [ANY] * 8,
+        in_specs=[SMEM] * 2 + [VMEM] * 3 + [HBM] * 8,
         out_specs=VMEM,
         scratch_shapes=[
-            pltpu.VMEM((8, lines, padded, columns), BF16),
+            pltpu.VMEM((8, lines, quarter_rows, depth), BF16),
             pltpu.VMEM((2 * lines, tok_count, depth), BF16),
             pltpu.VMEM((width, tok_count), F32),
             pltpu.SemaphoreType.DMA((8,)),
         ],
         compiler_params=pltpu.CompilerParams(vmem_limit_bytes=40 << 20),
         name="attention",
-    )(place, sinks, packed, halo, hidden_t, *parts)
+    )(place, sinks, packed, halo, hidden_t, *in_hbm(parts))
 
 
 def place_of():
@@ -324,19 +318,21 @@
     ).astype(jnp.int32)
 
 
-def shard_block(qkv_proj, out_proj):
+def own_quarters(qkv_proj, out_proj):
     rows, qkv_width = qkv_proj.shape
-    depth, width = out_proj.shape
     quarter = lax.axis_index("groups") % 2 * 2 + lax.axis_index("pipe")
-    qw, ow = qkv_width // 4, width // 4
-    padded = rows + -rows % 8
+    qw, ow = qkv_width // 4, out_proj.shape[1] // 4
     mine_qkv = lax.dynamic_slice_in_dim(qkv_proj, quarter * qw, qw, 1)
     mine_out = lax.dynamic_slice_in_dim(out_proj.T, quarter * ow, ow, 0)
-    pieces = [jnp.pad(mine_qkv, ((0, padded - rows), (0, 0)))]
-    for first in range(0, ow, padded):
-        piece = mine_out[first : first + padded]
-        pieces.append(jnp.pad(piece, ((0, padded - piece.shape[0]), (0, 0))))
-    return jnp.concatenate(pieces, axis=1)
+    return jnp.pad(mine_qkv, ((0, -rows % 8), (0, 0))), mine_out
+
+
+def along_lines(block, seq_count):
+    blocks = [block]
+    for k in range(1, seq_count // 2):
+        pairs = [(i, (i + 2 * k) % seq_count) for i in range(seq_count)]
+        blocks.append(lax.ppermute(block, "seq", pairs))
+    return blocks
 
 
 def fused_body(
@@ -346,29 +342,38 @@
     tok_count, width = tokens.shape[1:]
     per_device = gate_up.shape[0]
     rows, qkv_width = qkv_proj.shape
-    depth = out_proj.shape[0]
     tokens_t, routes_t, scale_t = tokens[0].T, routes[0].T, route_weights[0].T
-    block = shard_block(qkv_proj, out_proj)
-    column = jnp.stack(neighbour_relay(block, seq_count))
-    other = swapped(column, "seq")
-    parts = [column, other, swapped(column, "groups"), swapped(other, "groups")]
-    parts += [swapped(part, "pipe") for part in parts]
+    mine_qkv, mine_out = own_quarters(qkv_proj, out_proj)
+    qkv_lines = along_lines(mine_qkv, seq_count)
 
     table = dispatch(tokens_t, routes_t, moe_gain.reshape(1, width))
     outgoing = table.reshape(seq_count, per_device // 2, CAP, width)
     received = lax.all_to_all(outgoing, "seq", split_axis=0, concat_axis=0, tiled=True)
+
+    qkv_lines, mine_out = lax.optimization_barrier((qkv_lines, mine_out))
+    qkv_own = jnp.stack(qkv_lines)
+    qkv_mate = swapped(qkv_own, "seq")
+    out_lines = along_lines(mine_out, seq_count)
+    qkv_parts = [qkv_own, qkv_mate, swapped(qkv_own, "groups"), swapped(qkv_mate, "groups")]
+    residual, coarse, fine = returns(tokens_t, routes_t, scale_t)
+    received, residual, coarse, fine = lax.optimization_barrier((received, residual, coarse, fine))
+
     finished = run_experts(received, gate_up, down_proj)
+    out_own = jnp.stack(out_lines)
+    out_mate = swapped(out_own, "seq")
     summed = lax.all_to_all(finished, "seq", split_axis=0, concat_axis=0, tiled=True)
+    qkv_parts += [swapped(part, "pipe") for part in qkv_parts]
+    out_parts = [out_own, out_mate, swapped(out_own, "groups"), swapped(out_mate, "groups")]
+    out_parts += [swapped(part, "pipe") for part in out_parts]
+
     summed = summed.reshape(E * CAP, width)
-    residual, coarse, fine = returns(tokens_t, routes_t, scale_t)
     place = place_of()
     packed, hidden_t = project_qkv(
-        place, summed, residual, coarse, fine, attn_gain.reshape(1, width), parts, rows, qkv_width // 4
+        place, summed, residual, coarse, fine, attn_gain.reshape(1, width), qkv_parts, rows, qkv_width // 4
     )
     query_width = QUERY_HEADS * HEAD_SIZE
     halo = halo_exchange(packed[tok_count - WINDOW_SPAN :, query_width:])
-    columns = block.shape[1] - qkv_width // 4
-    out_t = attend_and_project(place, jnp.exp(sinks), packed, halo, hidden_t, parts, columns, depth)
+    out_t = attend_and_project(place, jnp.exp(sinks), packed, halo, hidden_t, out_parts)
     return out_t.T[None]
 
 
@@ -452,7 +457,7 @@
 
 
 def expert_layer(local, route_rows, route_scale, moe_gain, gate_up, down_proj):
-    tok_count, width = local.shape
+    _, width = local.shape
     seq_count = lax.axis_size("seq")
     per_device = gate_up.shape[0]
     normed = rms_scale(local, moe_gain)
@@ -554,7 +559,7 @@
         )
     qkv_full, out_full = gather_weights(qkv_proj, out_proj)
     hidden = expert_layer(tokens[0], routes[0], route_weights[0], moe_gain, gate_up, down_proj)
-    tok_count, width = hidden.shape
+    tok_count, _ = hidden.shape
     normed = rms_scale(hidden, attn_gain)
     seq_index = lax.axis_index("seq")
     pipe_index = lax.axis_index("pipe")

time: 226 us -> 269 us (1.19)
  waiting for transfers between devices: 130 us -> 184 us
  starting transfers between devices: 48.5 us -> 35.4 us
    all_to_all x1, waiting for transfers between devices: 0.01 us -> 51.7 us  [fused_body(): lax.all_to_all(outgoing, 'seq', split_axis=0, concat_axis=0, tiled=True)]
    ppermute x6, waiting for transfers between devices: 54.7 us -> 76.8 us  [along_lines(): blocks.append(lax.ppermute(block, 'seq', pairs))]
    ppermute x7 -> x14, waiting for transfers between devices: 72.5 us -> 52.4 us  [swapped(): lax.ppermute(value, axis, [(i, i ^ 1) for i in range(lax.axis_size(axis))])]
    ppermute x6, starting transfers between devices: 29.1 us -> 11.9 us  [along_lines(): blocks.append(lax.ppermute(block, 'seq', pairs))]
    ppermute x7 -> x14, starting transfers between devices: 4.28 us -> 9.05 us  [swapped(): lax.ppermute(value, axis, [(i, i ^ 1) for i in range(lax.axis_size(axis))])]
  transfers between devices with their start and end apart: 16 -> 23, of which waited for: 8 -> 10; matrix products, arithmetic and copies ran while one was open for 1% -> 2% of each run, Pallas kernels for 10% -> 3%
where the time goes in v2:
time: 269 us; the launch traced here: 266 us
  waiting for transfers between devices  184 us (68%)
  Pallas kernels  37.8 us (14%)
  starting transfers between devices  35.4 us (13%)
  local copies, waits for them, and re-layouts  6.41 us (2%)
    ppermute x6, waiting for transfers between devices, along_lines(): blocks.append(lax.ppermute(block, 'seq', pairs))  76.8 us
    ppermute x14, waiting for transfers between devices, swapped(): lax.ppermute(value, axis, [(i, i ^ 1) for i in range(lax.axis_size(axis))])  52.4 us
    all_to_all x1, waiting for transfers between devices, fused_body(): lax.all_to_all(outgoing, 'seq', split_axis=0, concat_axis=0, tiled=True)  51.7 us
    pallas_call x1, Pallas kernels, run_experts(): pl.pallas_call(experts_kernel, out_shape=pltpu.HBM(received.shape, BF16),...  17.2 us
    ppermute x6, starting transfers between devices, along_lines(): blocks.append(lax.ppermute(block, 'seq', pairs))  11.9 us
    ppermute x14, starting transfers between devices, swapped(): lax.ppermute(value, axis, [(i, i ^ 1) for i in range(lax.axis_size(axis))])  9.05 us
    pallas_call x1, Pallas kernels, attend_and_project(): pl.pallas_call(attention_kernel, out_shape=jax.ShapeDtypeStruct((width, t...  7.99 us
    all_to_all x1, starting transfers between devices, fused_body(): lax.all_to_all(outgoing, 'seq', split_axis=0, concat_axis=0, tiled=True)  7.31 us
  transfers between devices with their start and end apart: 23, of which 10 were waited for; matrix products, arithmetic and copies ran while one was open for 2% of the time, Pallas kernels for 3%

profile of v2, /device:TPU:0, one launch (start us, length us, event | category | flops | bytes accessed | tf_op | source)
XLA Modules:
  0.0 265.9 jit_solution(2344997840309422147)
XLA Ops:
  0.0 1.4 reshape.12.gain_ref
  1.4 3.7 %dispatch.1 = bf16[16,48,1440]{2,1,0:T(8,128)(2,1)} custom-call(bf16[1440,128]{1,0:T(8,128)(2,1)} %bitcast.30, s32[4,128]{1,0:T(4,128)} %bitcast.36, f32[1,1440]{1,0:T(1,128)} %reshape.12.gain_ref), custom_call_target="tpu_custom_call" | custom-call | tf_op jit(solution)/shard_map/dispatch/pallas_call | solution.py:58
  5.1 7.3 %all-to-all-start = ((bf16[8,2,48,1440]{3,2,1,0:T(8,128)(2,1)}), bf16[8,2,48,1440]{3,2,1,0:T(8,128)(2,1)S(1)}, u32[]{:S(2)}, u32[]{:S(2)}) async-start(bf16[8,2,48,1440]{3,2,1,0:T(8,128)(2,1)} %bitcast.29), calls=%async_computation | async-start | bytes 4718592 | tf_op jit(solution)/shard_map/all_to_all | solution.py:351
  12.4 2.1 returns.1
  14.5 51.7 %all-to-all-done.rows_ref = bf16[8,2,48,1440]{3,2,1,0:T(8,128)(2,1)S(1)} async-done(((bf16[8,2,48,1440]{3,2,1,0:T(8,128)(2,1)}), bf16[8,2,48,1440]{3,2,1,0:T(8,128)(2,1)S(1)}, u32[]{:S(2)}, u32[]{:S(2)}) %all-to-all-start) | async-done | bytes 2211872 | tf_op jit(solution)/shard_map/all_to_all | solution.py:351
  66.3 17.2 %experts.1 = bf16[8,2,48,1440]{3,2,1,0:T(8,128)(2,1)} custom-call(bf16[8,2,48,1440]{3,2,1,0:T(8,128)(2,1)S(1)} %all-to-all-done.rows_ref, bf16[4,1440,1440]{2,1,0:T(8,128)(2,1)} %gate_up_ref.1, bf16[4,720,1440]{2,1,0:T(8,128)(2,1)} %down_ref.1), custom_call_target="tpu_custom_call" | custom-call | tf_op jit(solution)/shard_map/experts/pallas_call | solution.py:128
  83.4 3.6 %all-to-all-start.1 = ((bf16[8,2,48,1440]{3,2,1,0:T(8,128)(2,1)}), bf16[8,2,48,1440]{3,2,1,0:T(8,128)(2,1)S(1)}, u32[]{:S(2)}, u32[]{:S(2)}) async-start(bf16[8,2,48,1440]{3,2,1,0:T(8,128)(2,1)} %experts.1), calls=%async_computation.1 | async-start | bytes 4718592 | tf_op jit(solution)/shard_map/all_to_all | solution.py:364
  87.1 0.0 copy-start.10
  87.1 0.7 pad.4
  87.8 2.0 collective-permute-start
  89.8 2.4 collective-permute-start.1
  92.2 1.5 collective-permute-start.2
  93.7 0.9 dynamic-slice_bitcast_fusion
  94.6 41.2 %collective-permute-done = bf16[184,640]{1,0:T(8,128)(2,1)} collective-permute-done((bf16[184,640]{1,0:T(8,128)(2,1)}, bf16[184,640]{1,0:T(8,128)(2,1)}, u32[]{:S(2)}, u32[]{:S(2)}) %collective-permute-start) | collective-permute-done | bytes 235552 | tf_op jit(solution)/shard_map/ppermute | solution.py:334
  135.8 21.7 %collective-permute-done.1 = bf16[184,640]{1,0:T(8,128)(2,1)} collective-permute-done((bf16[184,640]{1,0:T(8,128)(2,1)}, bf16[184,640]{1,0:T(8,128)(2,1)}, u32[]{:S(2)}, u32[]{:S(2)}) %collective-permute-start.1) | collective-permute-done | bytes 235552 | tf_op jit(solution)/shard_map/ppermute | solution.py:334
  157.5 1.4 pad_maximum_fusion.rest_0_
  159.0 1.3 collective-permute-start.3
  160.3 5.5 %collective-permute-start.13 = (bf16[360,256]{1,0:T(8,128)(2,1)S(1)}, bf16[360,256]{1,0:T(8,128)(2,1)S(1)}, u32[]{:S(2)}, u32[]{:S(2)}) collective-permute-start(bf16[360,256]{1,0:T(8,128)(2,1)S(1)} %dynamic-slice_bitcast_fusion), channel_id=1, source_target_pairs={{0,12},{2,14},{4,0},{6,2},{8,4},{10,6},{12,8},{14,10},{1,13},{3,15... | collective-permute-start | bytes 552968 | tf_op jit(solution)/shard_map/ppermute | solution.py:334
  165.8 0.6 collective-permute-start.12
  166.4 0.0 collective-permute-start.11
  166.4 1.5 collective-permute-start.4
  167.9 3.0 %collective-permute-done.13 = bf16[360,256]{1,0:T(8,128)(2,1)S(1)} collective-permute-done((bf16[360,256]{1,0:T(8,128)(2,1)S(1)}, bf16[360,256]{1,0:T(8,128)(2,1)S(1)}, u32[]{:S(2)}, u32[]{:S(2)}) %collective-permute-start.13) | collective-permute-done | bytes 184352 | tf_op jit(solution)/shard_map/ppermute | solution.py:334
  170.9 10.8 %collective-permute-done.12 = bf16[360,256]{1,0:T(8,128)(2,1)S(1)} collective-permute-done((bf16[360,256]{1,0:T(8,128)(2,1)S(1)}, bf16[360,256]{1,0:T(8,128)(2,1)S(1)}, u32[]{:S(2)}, u32[]{:S(2)}) %collective-permute-start.12) | collective-permute-done | bytes 184352 | tf_op jit(solution)/shard_map/ppermute | solution.py:334
  181.7 0.0 collective-permute-done.11
  181.7 1.0 pad_maximum_fusion.1.rest_0_
  182.7 0.6 collective-permute-start.14
  183.3 1.5 collective-permute-start.15
  184.8 0.0 collective-permute-done.3.rest_1_
  184.8 0.5 collective-permute-start.5
  185.3 15.1 %collective-permute-done.14.rest_1_ = bf16[4,360,256]{2,1,0:T(8,128)(2,1)} collective-permute-done((bf16[4,360,256]{2,1,0:T(8,128)(2,1)}, bf16[4,360,256]{2,1,0:T(8,128)(2,1)}, u32[]{:S(2)}, u32[]{:S(2)}) %collective-permute-start.14) | collective-permute-done | bytes 737312 | tf_op jit(solution)/shard_map/ppermute | solution.py:381
  200.4 0.5 collective-permute-start.8
  200.9 5.1 %collective-permute-done.15.rest_2_ = bf16[4,360,256]{2,1,0:T(8,128)(2,1)} collective-permute-done((bf16[4,360,256]{2,1,0:T(8,128)(2,1)}, bf16[4,360,256]{2,1,0:T(8,128)(2,1)}, u32[]{:S(2)}, u32[]{:S(2)}) %collective-permute-start.15) | collective-permute-done | bytes 737312 | tf_op jit(solution)/shard_map/ppermute | solution.py:381
  206.0 1.5 collective-permute-start.16
  207.5 18.7 %collective-permute-done.5.rest_3_ = bf16[4,184,640]{2,1,0:T(8,128)(2,1)} collective-permute-done((bf16[4,184,640]{2,1,0:T(8,128)(2,1)S(1)}, bf16[4,184,640]{2,1,0:T(8,128)(2,1)}, u32[]{:S(2)}, u32[]{:S(2)}) %collective-permute-start.5) | collective-permute-done | bytes 942112 | tf_op jit(solution)/shard_map/ppermute | solution.py:381
  226.2 0.6 collective-permute-start.17
  226.8 13.4 %collective-permute-done.16.rest_3_ = bf16[4,360,256]{2,1,0:T(8,128)(2,1)} collective-permute-done((bf16[4,360,256]{2,1,0:T(8,128)(2,1)}, bf16[4,360,256]{2,1,0:T(8,128)(2,1)}, u32[]{:S(2)}, u32[]{:S(2)}) %collective-permute-start.16) | collective-permute-done | bytes 737312 | tf_op jit(solution)/shard_map/ppermute | solution.py:381
  240.2 0.0 collective-permute-start.18
  240.3 0.6 collective-permute-start.19
  240.8 0.5 copy-done.8
  241.3 0.9 copy-done.9
  242.2 0.5 collective-permute-start.20
  242.7 0.1 pad_add_fusion.place_ref
  242.8 1.0 copy-done.1
  243.8 0.9 copy-done.3
  244.8 6.8 %qkv.1 = (bf16[128,2560]{1,0:T(8,128)(2,1)S(1)}, bf16[1440,128]{1,0:T(8,128)(2,1)S(1)}) custom-call(s32[4]{0:T(128)S(1)} %pad_add_fusion.place_ref, bf16[768,1440]{1,0:T(8,128)(2,1)S(1)} %bitcast.28, bf16[128,1440]{1,0:T(8,128)(2,1)S(1)} %copy-done.1, bf16[128,768]{1,0:T(8,128)(2,1)S(1)} %copy-done.2, bf16[128,768]{1,0:T(8,128)(2,1)S(1)} %copy-done.3, ...), custom_call_target="tpu_custom_call" | custom-call | tf_op jit(solution)/shard_map/qkv/pallas_call | solution.py:195
  251.6 3.5 %collective-permute-start.10 = (bf16[128,512]{1,0:T(8,128)(2,1)S(1)}, bf16[128,512]{1,0:T(8,128)(2,1)S(1)}, u32[]{:S(2)}, u32[]{:S(2)}) collective-permute-start(bf16[128,512]{1,0:T(8,128)(2,1)S(1)} %slice.3), channel_id=1, source_target_pairs={{0,2},{2,4},{4,6},{6,8},{8,10},{10,12},{12,14},{14,1},{1,3},{3,5},... | collective-permute-start | bytes 393224 | tf_op jit(solution)/shard_map/ppermute | solution.py:532
  255.1 2.7 collective-permute-done.10.halo_ref
  257.8 8.0 %attention.1 = bf16[1440,128]{1,0:T(8,128)(2,1)} custom-call(s32[4]{0:T(128)S(1)} %pad_add_fusion.place_ref, f32[32]{0:T(128)S(1)} %exp.3.sink_ref, bf16[128,2560]{1,0:T(8,128)(2,1)S(1)} %get-tuple-element.30.packed_ref, bf16[128,512]{1,0:T(8,128)(2,1)S(1)} %collective-permute-done.10.halo_ref, bf16[1440,128]{1,0:T(8,128)(2,1)S(1)} %get-tuple-element.31.hidden_ref, ...), custom_call_target="tpu_custom_call" | custom-call | tf_op jit(solution)/shard_map/attention/pallas_call | solution.py:298
  (37 shorter events, 0.1 us)
Async XLA Ops:
  0.0 87.1 %copy-start = (bf16[180,2560]{1,0:T(8,128)(2,1)S(1)}, bf16[180,2560]{1,0:T(8,128)(2,1)}, u32[]{:S(2)}) copy-start(bf16[180,2560]{1,0:T(8,128)(2,1)} %param.17) | copy-start | bytes 2764804
  5.1 61.2 %all-to-all-start = ((bf16[8,2,48,1440]{3,2,1,0:T(8,128)(2,1)}), bf16[8,2,48,1440]{3,2,1,0:T(8,128)(2,1)S(1)}, u32[]{:S(2)}, u32[]{:S(2)}) async-start(bf16[8,2,48,1440]{3,2,1,0:T(8,128)(2,1)} %bitcast.29), calls=%async_computation | async-start | bytes 4718592 | tf_op jit(solution)/shard_map/all_to_all | solution.py:351
  83.4 159.4 %all-to-all-start.1 = ((bf16[8,2,48,1440]{3,2,1,0:T(8,128)(2,1)}), bf16[8,2,48,1440]{3,2,1,0:T(8,128)(2,1)S(1)}, u32[]{:S(2)}, u32[]{:S(2)}) async-start(bf16[8,2,48,1440]{3,2,1,0:T(8,128)(2,1)} %experts.1), calls=%async_computation.1 | async-start | bytes 4718592 | tf_op jit(solution)/shard_map/all_to_all | solution.py:364
  87.1 155.7 %copy-start.10 = (f32[1440]{0:T(1024)S(1)}, f32[1440]{0:T(1024)}, u32[]{:S(2)}) copy-start(f32[1440]{0:T(1024)} %param.16) | copy-start | bytes 17284
  87.1 155.8 %copy-start.2 = (bf16[128,768]{1,0:T(8,128)(2,1)S(1)}, bf16[128,768]{1,0:T(8,128)(2,1)}, u32[]{:S(2)}) copy-start(bf16[128,768]{1,0:T(8,128)(2,1)} %get-tuple-element.24.coarse_ref) | copy-start | bytes 589828
  87.8 48.0 %collective-permute-start = (bf16[184,640]{1,0:T(8,128)(2,1)}, bf16[184,640]{1,0:T(8,128)(2,1)}, u32[]{:S(2)}, u32[]{:S(2)}) collective-permute-start(bf16[184,640]{1,0:T(8,128)(2,1)} %pad.4), channel_id=1, source_target_pairs={{0,4},{2,6},{4,8},{6,10},{8,12},{10,14},{12,0},{14,2},{1,5},{3,7},... | collective-permute-start | bytes 706568 | tf_op jit(solution)/shard_map/ppermute | solution.py:334
  89.8 67.7 %collective-permute-start.1 = (bf16[184,640]{1,0:T(8,128)(2,1)}, bf16[184,640]{1,0:T(8,128)(2,1)}, u32[]{:S(2)}, u32[]{:S(2)}) collective-permute-start(bf16[184,640]{1,0:T(8,128)(2,1)} %pad.4), channel_id=1, source_target_pairs={{0,8},{2,10},{4,12},{6,14},{8,0},{10,2},{12,4},{14,6},{1,9},{3,11}... | collective-permute-start | bytes 706568 | tf_op jit(solution)/shard_map/ppermute | solution.py:334
  92.2 65.3 %collective-permute-start.2 = (bf16[184,640]{1,0:T(8,128)(2,1)}, bf16[184,640]{1,0:T(8,128)(2,1)}, u32[]{:S(2)}, u32[]{:S(2)}) collective-permute-start(bf16[184,640]{1,0:T(8,128)(2,1)} %pad.4), channel_id=1, source_target_pairs={{0,12},{2,14},{4,0},{6,2},{8,4},{10,6},{12,8},{14,10},{1,13},{3,15... | collective-permute-start | bytes 706568 | tf_op jit(solution)/shard_map/ppermute | solution.py:334
  159.0 26.3 %copy-start.4 = (bf16[4,184,640]{2,1,0:T(8,128)(2,1)}, bf16[4,184,640]{2,1,0:T(8,128)(2,1)S(1)}, u32[]{:S(2)}) copy-start(bf16[4,184,640]{2,1,0:T(8,128)(2,1)S(1)} %pad_maximum_fusion.rest_0_) | copy-start | bytes 2826244
  159.0 25.8 %collective-permute-start.3 = (bf16[4,184,640]{2,1,0:T(8,128)(2,1)S(1)}, bf16[4,184,640]{2,1,0:T(8,128)(2,1)S(1)}, u32[]{:S(2)}, u32[]{:S(2)}) collective-permute-start(bf16[4,184,640]{2,1,0:T(8,128)(2,1)S(1)} %pad_maximum_fusion.rest_0_), channel_id=1, source_target_pairs={{0,2},{2,0},{4,6},{6,4},{8,10},{10,8},{12,14},{14,12},{1,3},{3,1},... | collective-permute-start | bytes 2826248 | tf_op jit(solution)/shard_map/ppermute | solution.py:381
  160.3 10.6 %collective-permute-start.13 = (bf16[360,256]{1,0:T(8,128)(2,1)S(1)}, bf16[360,256]{1,0:T(8,128)(2,1)S(1)}, u32[]{:S(2)}, u32[]{:S(2)}) collective-permute-start(bf16[360,256]{1,0:T(8,128)(2,1)S(1)} %dynamic-slice_bitcast_fusion), channel_id=1, source_target_pairs={{0,12},{2,14},{4,0},{6,2},{8,4},{10,6},{12,8},{14,10},{1,13},{3,15... | collective-permute-start | bytes 552968 | tf_op jit(solution)/shard_map/ppermute | solution.py:334
  165.8 15.9 %collective-permute-start.12 = (bf16[360,256]{1,0:T(8,128)(2,1)S(1)}, bf16[360,256]{1,0:T(8,128)(2,1)S(1)}, u32[]{:S(2)}, u32[]{:S(2)}) collective-permute-start(bf16[360,256]{1,0:T(8,128)(2,1)S(1)} %dynamic-slice_bitcast_fusion), channel_id=1, source_target_pairs={{0,8},{2,10},{4,12},{6,14},{8,0},{10,2},{12,4},{14,6},{1,9},{3,11}... | collective-permute-start | bytes 552968 | tf_op jit(solution)/shard_map/ppermute | solution.py:334
  166.4 15.4 %collective-permute-start.11 = (bf16[360,256]{1,0:T(8,128)(2,1)S(1)}, bf16[360,256]{1,0:T(8,128)(2,1)S(1)}, u32[]{:S(2)}, u32[]{:S(2)}) collective-permute-start(bf16[360,256]{1,0:T(8,128)(2,1)S(1)} %dynamic-slice_bitcast_fusion), channel_id=1, source_target_pairs={{0,4},{2,6},{4,8},{6,10},{8,12},{10,14},{12,0},{14,2},{1,5},{3,7},... | collective-permute-start | bytes 552968 | tf_op jit(solution)/shard_map/ppermute | solution.py:334
  166.4 34.0 %collective-permute-start.4 = (bf16[4,184,640]{2,1,0:T(8,128)(2,1)S(1)}, bf16[4,184,640]{2,1,0:T(8,128)(2,1)S(1)}, u32[]{:S(2)}, u32[]{:S(2)}) collective-permute-start(bf16[4,184,640]{2,1,0:T(8,128)(2,1)S(1)} %pad_maximum_fusion.rest_0_), channel_id=1, source_target_pairs={{0,16},{16,0},{1,17},{17,1},{2,18},{18,2},{3,19},{19,3},{4,20},{20... | collective-permute-start | bytes 2826248 | tf_op jit(solution)/shard_map/ppermute | solution.py:381
  182.7 17.7 %collective-permute-start.14 = (bf16[4,360,256]{2,1,0:T(8,128)(2,1)}, bf16[4,360,256]{2,1,0:T(8,128)(2,1)}, u32[]{:S(2)}, u32[]{:S(2)}) collective-permute-start(bf16[4,360,256]{2,1,0:T(8,128)(2,1)} %pad_maximum_fusion.1.rest_0_), channel_id=1, source_target_pairs={{0,2},{2,0},{4,6},{6,4},{8,10},{10,8},{12,14},{14,12},{1,3},{3,1},... | collective-permute-start | bytes 2211848 | tf_op jit(solution)/shard_map/ppermute | solution.py:381
  183.3 22.8 %collective-permute-start.15 = (bf16[4,360,256]{2,1,0:T(8,128)(2,1)}, bf16[4,360,256]{2,1,0:T(8,128)(2,1)}, u32[]{:S(2)}, u32[]{:S(2)}) collective-permute-start(bf16[4,360,256]{2,1,0:T(8,128)(2,1)} %pad_maximum_fusion.1.rest_0_), channel_id=1, source_target_pairs={{0,16},{16,0},{1,17},{17,1},{2,18},{18,2},{3,19},{19,3},{4,20},{20... | collective-permute-start | bytes 2211848 | tf_op jit(solution)/shard_map/ppermute | solution.py:381
  184.8 41.5 %copy-start.5 = (bf16[4,184,640]{2,1,0:T(8,128)(2,1)}, bf16[4,184,640]{2,1,0:T(8,128)(2,1)S(1)}, u32[]{:S(2)}) copy-start(bf16[4,184,640]{2,1,0:T(8,128)(2,1)S(1)} %collective-permute-done.3.rest_1_) | copy-start | bytes 2826244
  184.8 41.5 %collective-permute-start.5 = (bf16[4,184,640]{2,1,0:T(8,128)(2,1)S(1)}, bf16[4,184,640]{2,1,0:T(8,128)(2,1)}, u32[]{:S(2)}, u32[]{:S(2)}) collective-permute-start(bf16[4,184,640]{2,1,0:T(8,128)(2,1)S(1)} %collective-permute-done.3.rest_1_), channel_id=1, source_target_pairs={{0,16},{16,0},{1,17},{17,1},{2,18},{18,2},{3,19},{19,3},{4,20},{20... | collective-permute-start | bytes 2826248 | tf_op jit(solution)/shard_map/ppermute | solution.py:381
  185.3 40.9 %collective-permute-start.6 = (bf16[4,184,640]{2,1,0:T(8,128)(2,1)S(1)}, bf16[4,184,640]{2,1,0:T(8,128)(2,1)S(1)}, u32[]{:S(2)}, u32[]{:S(2)}) collective-permute-start(bf16[4,184,640]{2,1,0:T(8,128)(2,1)S(1)} %pad_maximum_fusion.rest_0_), channel_id=1, source_target_pairs={{0,1},{1,0},{2,3},{3,2},{4,5},{5,4},{6,7},{7,6},{8,9},{9,8},{10,11... | collective-permute-start | bytes 2826248 | tf_op jit(solution)/shard_map/ppermute | solution.py:381
  200.4 39.8 %collective-permute-start.7 = (bf16[4,184,640]{2,1,0:T(8,128)(2,1)S(1)}, bf16[4,184,640]{2,1,0:T(8,128)(2,1)S(1)}, u32[]{:S(2)}, u32[]{:S(2)}) collective-permute-start(bf16[4,184,640]{2,1,0:T(8,128)(2,1)S(1)} %collective-permute-done.3.rest_1_), channel_id=1, source_target_pairs={{0,1},{1,0},{2,3},{3,2},{4,5},{5,4},{6,7},{7,6},{8,9},{9,8},{10,11... | collective-permute-start | bytes 2826248 | tf_op jit(solution)/shard_map/ppermute | solution.py:381
  200.4 39.8 %copy-start.6 = (bf16[4,184,640]{2,1,0:T(8,128)(2,1)}, bf16[4,184,640]{2,1,0:T(8,128)(2,1)S(1)}, u32[]{:S(2)}) copy-start(bf16[4,184,640]{2,1,0:T(8,128)(2,1)S(1)} %collective-permute-done.4.rest_2_) | copy-start | bytes 2826244
  200.4 40.4 %collective-permute-start.8 = (bf16[4,184,640]{2,1,0:T(8,128)(2,1)S(1)}, bf16[4,184,640]{2,1,0:T(8,128)(2,1)S(1)}, u32[]{:S(2)}, u32[]{:S(2)}) collective-permute-start(bf16[4,184,640]{2,1,0:T(8,128)(2,1)S(1)} %collective-permute-done.4.rest_2_), channel_id=1, source_target_pairs={{0,1},{1,0},{2,3},{3,2},{4,5},{5,4},{6,7},{7,6},{8,9},{9,8},{10,11... | collective-permute-start | bytes 2826248 | tf_op jit(solution)/shard_map/ppermute | solution.py:381
  206.0 34.2 %collective-permute-start.16 = (bf16[4,360,256]{2,1,0:T(8,128)(2,1)}, bf16[4,360,256]{2,1,0:T(8,128)(2,1)}, u32[]{:S(2)}, u32[]{:S(2)}) collective-permute-start(bf16[4,360,256]{2,1,0:T(8,128)(2,1)} %collective-permute-done.14.rest_1_), channel_id=1, source_target_pairs={{0,16},{16,0},{1,17},{17,1},{2,18},{18,2},{3,19},{19,3},{4,20},{20... | collective-permute-start | bytes 2211848 | tf_op jit(solution)/shard_map/ppermute | solution.py:381
  226.2 16.6 %collective-permute-start.9 = (bf16[4,184,640]{2,1,0:T(8,128)(2,1)}, bf16[4,184,640]{2,1,0:T(8,128)(2,1)}, u32[]{:S(2)}, u32[]{:S(2)}) collective-permute-start(bf16[4,184,640]{2,1,0:T(8,128)(2,1)} %collective-permute-done.5.rest_3_), channel_id=1, source_target_pairs={{0,1},{1,0},{2,3},{3,2},{4,5},{5,4},{6,7},{7,6},{8,9},{9,8},{10,11... | collective-permute-start | bytes 2826248 | tf_op jit(solution)/shard_map/ppermute | solution.py:381
  226.2 14.6 %copy-start.7 = (bf16[4,184,640]{2,1,0:T(8,128)(2,1)}, bf16[4,184,640]{2,1,0:T(8,128)(2,1)S(1)}, u32[]{:S(2)}) copy-start(bf16[4,184,640]{2,1,0:T(8,128)(2,1)S(1)} %collective-permute-done.6.rest_4_) | copy-start | bytes 2826244
  226.2 28.8 %collective-permute-start.17 = (bf16[4,360,256]{2,1,0:T(8,128)(2,1)}, bf16[4,360,256]{2,1,0:T(8,128)(2,1)}, u32[]{:S(2)}, u32[]{:S(2)}) collective-permute-start(bf16[4,360,256]{2,1,0:T(8,128)(2,1)} %pad_maximum_fusion.1.rest_0_), channel_id=1, source_target_pairs={{0,1},{1,0},{2,3},{3,2},{4,5},{5,4},{6,7},{7,6},{8,9},{9,8},{10,11... | collective-permute-start | bytes 2211848 | tf_op jit(solution)/shard_map/ppermute | solution.py:381
  240.2 14.9 %collective-permute-start.18 = (bf16[4,360,256]{2,1,0:T(8,128)(2,1)}, bf16[4,360,256]{2,1,0:T(8,128)(2,1)}, u32[]{:S(2)}, u32[]{:S(2)}) collective-permute-start(bf16[4,360,256]{2,1,0:T(8,128)(2,1)} %collective-permute-done.14.rest_1_), channel_id=1, source_target_pairs={{0,1},{1,0},{2,3},{3,2},{4,5},{5,4},{6,7},{7,6},{8,9},{9,8},{10,11... | collective-permute-start | bytes 2211848 | tf_op jit(solution)/shard_map/ppermute | solution.py:381
  240.2 1.0 copy-start.8
  240.3 14.8 %collective-permute-start.19 = (bf16[4,360,256]{2,1,0:T(8,128)(2,1)}, bf16[4,360,256]{2,1,0:T(8,128)(2,1)}, u32[]{:S(2)}, u32[]{:S(2)}) collective-permute-start(bf16[4,360,256]{2,1,0:T(8,128)(2,1)} %collective-permute-done.15.rest_2_), channel_id=1, source_target_pairs={{0,1},{1,0},{2,3},{3,2},{4,5},{5,4},{6,7},{7,6},{8,9},{9,8},{10,11... | collective-permute-start | bytes 2211848 | tf_op jit(solution)/shard_map/ppermute | solution.py:381
  241.3 0.9 copy-start.9
  242.2 12.9 %collective-permute-start.20 = (bf16[4,360,256]{2,1,0:T(8,128)(2,1)}, bf16[4,360,256]{2,1,0:T(8,128)(2,1)}, u32[]{:S(2)}, u32[]{:S(2)}) collective-permute-start(bf16[4,360,256]{2,1,0:T(8,128)(2,1)} %collective-permute-done.16.rest_3_), channel_id=1, source_target_pairs={{0,1},{1,0},{2,3},{3,2},{4,5},{5,4},{6,7},{7,6},{8,9},{9,8},{10,11... | collective-permute-start | bytes 2211848 | tf_op jit(solution)/shard_map/ppermute | solution.py:381
  242.8 1.0 copy-start.1
  243.8 0.9 copy-start.3
  244.8 10.3 %copy-start.11 = (f32[32]{0:T(128)S(1)}, f32[32]{0:T(128)}, u32[]{:S(2)}) copy-start(f32[32]{0:T(128)} %param.18) | copy-start | bytes 388
  251.6 6.2 %collective-permute-start.10 = (bf16[128,512]{1,0:T(8,128)(2,1)S(1)}, bf16[128,512]{1,0:T(8,128)(2,1)S(1)}, u32[]{:S(2)}, u32[]{:S(2)}) collective-permute-start(bf16[128,512]{1,0:T(8,128)(2,1)S(1)} %slice.3), channel_id=1, source_target_pairs={{0,2},{2,4},{4,6},{6,8},{8,10},{10,12},{12,14},{14,1},{1,3},{3,5},... | collective-permute-start | bytes 393224 | tf_op jit(solution)/shard_map/ppermute | solution.py:532

commit v3 on v2

--- a/solution.py
+++ b/solution.py
@@ -41,26 +41,31 @@
     return flags, jnp.where(flags > 0.0, rank, -1.0)
 
 
-def dispatch_kernel(tokens_ref, routes_ref, gain_ref, table_ref):
-    tok_count = tokens_ref.shape[1]
+def slot_lanes(width):
+    spare = -width % 128
+    return spare if spare >= E else spare + 128
+
+
+def prepare_kernel(tokens_ref, routes_ref, gain_ref, block_ref):
+    width, tok_count = tokens_ref.shape
     value = tokens_ref[...].astype(F32).T
     mean_square = jnp.mean(value * value, axis=-1, keepdims=True)
-    normed = (value * lax.rsqrt(mean_square + eps) * gain_ref[...]).astype(BF16)
+    normed = value * lax.rsqrt(mean_square + eps) * gain_ref[...][None, :]
+    block_ref[:, :width] = normed.astype(BF16)
     _, rank = route_slots(routes_ref)
-    slot = lax.broadcasted_iota(jnp.int32, (CAP, tok_count), 0).astype(F32)
-    for expert in range(E):
-        select = jnp.where(slot == rank[expert : expert + 1, :], 1.0, 0.0).astype(BF16)
-        table_ref[expert] = jnp.dot(select, normed, preferred_element_type=F32).astype(BF16)
-
-
-def dispatch(tokens_t, routes_t, gain):
-    width = tokens_t.shape[0]
+    spare = block_ref.shape[1] - width
+    unused = jnp.full((spare - E, tok_count), -1.0, F32)
+    block_ref[:, width:] = jnp.concatenate([rank, unused], axis=0).T.astype(BF16)
+
+
+def prepare(tokens_t, routes_t, gain):
+    width, tok_count = tokens_t.shape
     return pl.pallas_call(
-        dispatch_kernel,
-        out_shape=jax.ShapeDtypeStruct((E, CAP, width), BF16),
+        prepare_kernel,
+        out_shape=jax.ShapeDtypeStruct((tok_count, width + slot_lanes(width)), BF16),
         in_specs=[VMEM] * 3,
         out_specs=VMEM,
-        name="dispatch",
+        name="prepare",
     )(tokens_t, routes_t, gain)
 
 
@@ -98,11 +103,26 @@
     )(tokens_t, routes_t, scale_t)
 
 
-def experts_kernel(rows_ref, gate_up_ref, down_ref, out_ref, total_ref):
-    slab = pl.program_id(1)
-    blocks, cap, width = rows_ref.shape
-    rows = rows_ref[...].reshape(blocks * cap, width)
-    projected = jnp.dot(rows, gate_up_ref[...], preferred_element_type=F32)
+def experts_kernel(lines, place_ref, *refs):
+    blocks = refs[: 2 * lines]
+    gate_up_ref, down_ref, out_ref, picked, slots, total_ref = refs[2 * lines :]
+    expert, slab = pl.program_id(0), pl.program_id(1)
+    experts, _, width = picked.shape
+    tok_count, _ = blocks[0].shape
+
+    @pl.when((expert == 0) & (slab == 0))
+    def _():
+        place = shard_of(place_ref, 0, 0, lines) * experts
+        slot = lax.broadcasted_iota(jnp.int32, (CAP, tok_count), 0).astype(F32)
+        for i, block in enumerate(blocks):
+            slots[i] = block[:, width:].astype(F32).T
+            select = [slot == slots[i, pl.ds(place + e, 1), :] for e in range(experts)]
+            select = jnp.where(jnp.concatenate(select, axis=0), 1.0, 0.0).astype(BF16)
+            rows = jnp.dot(select, block[:, :width], preferred_element_type=F32).astype(BF16)
+            for e in range(experts):
+                picked[e, i * CAP : (i + 1) * CAP, :] = rows[e * CAP : (e + 1) * CAP]
+
+    projected = jnp.dot(picked[expert], gate_up_ref[...], preferred_element_type=F32)
     gate_part = projected[:, :HALF]
     up_part = projected[:, HALF:]
     hidden = (gate_part * jax.nn.sigmoid(1.702 * gate_part) * (up_part + 1.0)).astype(BF16)
@@ -118,35 +138,63 @@
 
     @pl.when(slab == pl.num_programs(1) - 1)
     def _():
-        out_ref[...] = total_ref[...].astype(BF16).reshape(blocks, cap, width)
-
-
-def run_experts(received, gate_up, down_proj):
-    seq_count, experts, cap, width = received.shape
-    slabs = gate_up.shape[0] // experts
-    rows_spec = pl.BlockSpec((seq_count, None, cap, width), lambda e, k: (0, e, 0, 0))
+        for i in range(2 * lines):
+            owner = shard_of(place_ref, i // 2, i % 2, lines)
+            out_ref[owner] = total_ref[i * CAP : (i + 1) * CAP].astype(BF16)
+
+
+def run_experts(place, blocks, gate_up, down_proj):
+    seq_count = len(blocks)
+    tok_count, sent = blocks[0].shape
+    per_device, width, gate_width = gate_up.shape
+    slabs = 2
+    experts = per_device // slabs
     return pl.pallas_call(
-        experts_kernel,
-        out_shape=pltpu.HBM(received.shape, BF16),
+        functools.partial(experts_kernel, seq_count // 2),
+        out_shape=pltpu.HBM((seq_count, experts, CAP, width), BF16),
         grid=(experts, slabs),
-        in_specs=[
-            rows_spec,
-            pl.BlockSpec((None, width, gate_up.shape[2]), lambda e, k: (e * slabs + k, 0, 0)),
+        in_specs=[SMEM]
+        + [pl.BlockSpec((tok_count, sent), lambda e, k: (0, 0))] * seq_count
+        + [
+            pl.BlockSpec((None, width, gate_width), lambda e, k: (e * slabs + k, 0, 0)),
             pl.BlockSpec((None, down_proj.shape[1], width), lambda e, k: (e * slabs + k, 0, 0)),
         ],
-        out_specs=rows_spec,
-        scratch_shapes=[pltpu.VMEM((seq_count * cap, width), F32)],
+        out_specs=pl.BlockSpec((seq_count, None, CAP, width), lambda e, k: (0, e, 0, 0)),
+        scratch_shapes=[
+            pltpu.VMEM((experts, seq_count * CAP, width), BF16),
+            pltpu.VMEM((seq_count, sent - width, tok_count), F32),
+            pltpu.VMEM((seq_count * CAP, width), F32),
+        ],
         compiler_params=pltpu.CompilerParams(vmem_limit_bytes=48 << 20),
         name="experts",
-    )(received, gate_up, down_proj)
+    )(place, *blocks, gate_up, down_proj)
 
 
 def in_hbm(parts):
     return [pltpu.with_memory_space_constraint(part, pltpu.HBM) for part in parts]
 
 
+def start_copies(parts, held, sems):
+    half = held.shape[1] // 2
+    copies = []
+    for i, part in enumerate(parts):
+        target = held.at[i // 2, pl.ds(i % 2 * half, half)]
+        copy = pltpu.make_async_copy(part, target, sems.at[i])
+        copy.start()
+        copies.append(copy)
+    return [copies[i : i + 2] for i in range(0, len(copies), 2)]
+
+
+def block_step(slot, lines):
+    half = lines // 2
+    return slot % half * 2 + slot // half
+
+
 def shard_of(place_ref, step, flip, lines):
-    line = lax.rem(place_ref[0] - step + lines, lines)
+    line, bit = 0, 1
+    while bit < lines:
+        line += (place_ref[0] // bit + step // bit) % 2 * bit
+        bit *= 2
     return line * 2 + (place_ref[1] + flip) % 2
 
 
@@ -157,13 +205,9 @@
 def qkv_kernel(
     rows, place_ref, tables_ref, residual_ref, coarse_ref, fine_ref, gain_ref, *rest
 ):
-    parts, (packed_ref, hidden_ref, held, slices, sems) = rest[:8], rest[8:]
+    parts, (packed_ref, hidden_ref, held, slices, sems) = rest[:16], rest[16:]
     lines, _, columns = held.shape[1:]
-    copies = []
-    for i, part in enumerate(parts):
-        copy = pltpu.make_async_copy(part, held.at[i], sems.at[i])
-        copy.start()
-        copies.append(copy)
+    copies = start_copies(parts, held, sems)
     table = tables_ref[...]
     mixed = jnp.dot(coarse_ref[...], table, preferred_element_type=F32)
     mixed += jnp.dot(fine_ref[...], table, preferred_element_type=F32)
@@ -171,17 +215,18 @@
     value = hidden.astype(F32)
     hidden_ref[...] = value.T.astype(BF16)
     mean_square = jnp.mean(value * value, axis=-1, keepdims=True)
-    normed = value * lax.rsqrt(mean_square + eps) * gain_ref[...]
+    normed = value * lax.rsqrt(mean_square + eps) * gain_ref[...][None, :]
     slices[...] = jnp.zeros_like(slices)
     for s in range(2 * lines):
         slices[s, :, :rows] = normed[:, s * rows : (s + 1) * rows].astype(BF16)
     for pair in range(4):
         total = jnp.zeros((value.shape[0], columns), F32)
         for flip in range(2):
-            copies[pair * 2 + flip].wait()
+            for copy in copies[pair * 2 + flip]:
+                copy.wait()
             for step in range(lines):
                 total += jnp.dot(
-                    slices[shard_of(place_ref, step, flip, lines)],
+                    slices[shard_of(place_ref, block_step(step, lines), flip, lines)],
                     held[pair * 2 + flip, step],
                     preferred_element_type=F32,
                 )
@@ -191,19 +236,19 @@
 
 def project_qkv(place, tables, residual, coarse, fine, gain, parts, rows, columns):
     tok_count, width = residual.shape
-    lines, padded = parts[0].shape[:2]
+    lines, padded = 2 * parts[0].shape[0], parts[0].shape[1]
     return pl.pallas_call(
         functools.partial(qkv_kernel, rows),
         out_shape=(
             jax.ShapeDtypeStruct((tok_count, 4 * columns), BF16),
             jax.ShapeDtypeStruct((width, tok_count), BF16),
         ),
-        in_specs=[SMEM] + [VMEM] * 5 + [HBM] * 8,
+        in_specs=[SMEM] + [VMEM] * 5 + [HBM] * 16,
         out_specs=(VMEM, VMEM),
         scratch_shapes=[
             pltpu.VMEM((8, lines, padded, columns), BF16),
             pltpu.VMEM((2 * lines, tok_count, padded), BF16),
-            pltpu.SemaphoreType.DMA((8,)),
+            pltpu.SemaphoreType.DMA((16,)),
         ],
         compiler_params=pltpu.CompilerParams(vmem_limit_bytes=40 << 20),
         name="qkv",
@@ -213,13 +258,9 @@
 def attention_kernel(
     place_ref, sink_ref, packed_ref, halo_ref, hidden_ref, *rest
 ):
-    parts, (out_ref, held, mixed, total_ref, sems) = rest[:8], rest[8:]
+    parts, (out_ref, held, mixed, total_ref, sems) = rest[:16], rest[16:]
     lines, quarter_rows, depth = held.shape[1:]
-    copies = []
-    for i, part in enumerate(parts):
-        copy = pltpu.make_async_copy(part, held.at[i], sems.at[i])
-        copy.start()
-        copies.append(copy)
+    copies = start_copies(parts, held, sems)
     tok_count = packed_ref.shape[0]
     pair_width = 2 * HEAD_SIZE
     query_width = QUERY_HEADS * HEAD_SIZE
@@ -279,11 +320,12 @@
     for pair in range(4):
         total = jnp.zeros((quarter_rows, tok_count), F32)
         for flip in range(2):
-            copies[pair * 2 + flip].wait()
+            for copy in copies[pair * 2 + flip]:
+                copy.wait()
             for step in range(lines):
                 total += lax.dot_general(
                     held[pair * 2 + flip, step],
-                    mixed[shard_of(place_ref, step, flip, lines)],
+                    mixed[shard_of(place_ref, block_step(step, lines), flip, lines)],
                     (((1,), (1,)), ((), ())),
                     preferred_element_type=F32,
                 )
@@ -294,17 +336,18 @@
 
 def attend_and_project(place, sinks, packed, halo, hidden_t, parts):
     width, tok_count = hidden_t.shape
-    lines, quarter_rows, depth = parts[0].shape
+    half, quarter_rows, depth = parts[0].shape
+    lines = 2 * half
     return pl.pallas_call(
         attention_kernel,
         out_shape=jax.ShapeDtypeStruct((width, tok_count), BF16),
-        in_specs=[SMEM] * 2 + [VMEM] * 3 + [HBM] * 8,
+        in_specs=[SMEM] * 2 + [VMEM] * 3 + [HBM] * 16,
         out_specs=VMEM,
         scratch_shapes=[
             pltpu.VMEM((8, lines, quarter_rows, depth), BF16),
             pltpu.VMEM((2 * lines, tok_count, depth), BF16),
             pltpu.VMEM((width, tok_count), F32),
-            pltpu.SemaphoreType.DMA((8,)),
+            pltpu.SemaphoreType.DMA((16,)),
         ],
         compiler_params=pltpu.CompilerParams(vmem_limit_bytes=40 << 20),
         name="attention",
@@ -327,12 +370,34 @@
     return jnp.pad(mine_qkv, ((0, -rows % 8), (0, 0))), mine_out
 
 
-def along_lines(block, seq_count):
-    blocks = [block]
-    for k in range(1, seq_count // 2):
-        pairs = [(i, (i + 2 * k) % seq_count) for i in range(seq_count)]
-        blocks.append(lax.ppermute(block, "seq", pairs))
-    return blocks
+def flipped(value, bit):
+    count = lax.axis_size("seq")
+    return lax.ppermute(value, "seq", [(i, i ^ bit * 2) for i in range(count)])
+
+
+def far_blocks(block, lines):
+    bit = lines // 2
+    found = {0: block}
+    while bit > 1:
+        for step in list(found):
+            found[step + bit] = flipped(found[step], bit)
+        bit //= 2
+    return [found[step] for step in range(0, lines, 2)]
+
+
+def gather_quarters(mine, lines):
+    even = jnp.stack(far_blocks(mine, lines))
+    odd = flipped(even, 1)
+    parts = []
+    even_mate, even_across = swapped(even, "seq"), swapped(even, "groups")
+    odd_mate, odd_across = swapped(odd, "seq"), swapped(odd, "groups")
+    even_last = swapped(even_mate, "groups")
+    odd_last = swapped(odd_mate, "groups")
+    parts = [even, odd, even_mate, odd_mate, even_across, odd_across, even_last, odd_last]
+    beside = []
+    for part in parts:
+        beside.append(swapped(part, "pipe"))
+    return parts + beside
 
 
 def fused_body(
@@ -340,36 +405,29 @@
 ):
     seq_count = lax.axis_size("seq")
     tok_count, width = tokens.shape[1:]
-    per_device = gate_up.shape[0]
     rows, qkv_width = qkv_proj.shape
     tokens_t, routes_t, scale_t = tokens[0].T, routes[0].T, route_weights[0].T
+    place = place_of()
+
+    block = prepare(tokens_t, routes_t, moe_gain)
+    lines = seq_count // 2
+    evens = far_blocks(block, lines)
+    blocks = []
+    for even in evens:
+        odd = flipped(even, 1)
+        for value in (even, odd):
+            blocks += [value, swapped(value, "seq")]
     mine_qkv, mine_out = own_quarters(qkv_proj, out_proj)
-    qkv_lines = along_lines(mine_qkv, seq_count)
-
-    table = dispatch(tokens_t, routes_t, moe_gain.reshape(1, width))
-    outgoing = table.reshape(seq_count, per_device // 2, CAP, width)
-    received = lax.all_to_all(outgoing, "seq", split_axis=0, concat_axis=0, tiled=True)
-
-    qkv_lines, mine_out = lax.optimization_barrier((qkv_lines, mine_out))
-    qkv_own = jnp.stack(qkv_lines)
-    qkv_mate = swapped(qkv_own, "seq")
-    out_lines = along_lines(mine_out, seq_count)
-    qkv_parts = [qkv_own, qkv_mate, swapped(qkv_own, "groups"), swapped(qkv_mate, "groups")]
+    qkv_parts = gather_quarters(mine_qkv, lines)
+    out_parts = gather_quarters(mine_out, lines)
+
+    finished = run_experts(place, blocks, gate_up, down_proj)
+    summed = lax.all_to_all(finished, "seq", split_axis=0, concat_axis=0, tiled=True)
     residual, coarse, fine = returns(tokens_t, routes_t, scale_t)
-    received, residual, coarse, fine = lax.optimization_barrier((received, residual, coarse, fine))
-
-    finished = run_experts(received, gate_up, down_proj)
-    out_own = jnp.stack(out_lines)
-    out_mate = swapped(out_own, "seq")
-    summed = lax.all_to_all(finished, "seq", split_axis=0, concat_axis=0, tiled=True)
-    qkv_parts += [swapped(part, "pipe") for part in qkv_parts]
-    out_parts = [out_own, out_mate, swapped(out_own, "groups"), swapped(out_mate, "groups")]
-    out_parts += [swapped(part, "pipe") for part in out_parts]
 
     summed = summed.reshape(E * CAP, width)
-    place = place_of()
     packed, hidden_t = project_qkv(
-        place, summed, residual, coarse, fine, attn_gain.reshape(1, width), qkv_parts, rows, qkv_width // 4
+        place, summed, residual, coarse, fine, attn_gain, qkv_parts, rows, qkv_width // 4
     )
     query_width = QUERY_HEADS * HEAD_SIZE
     halo = halo_exchange(packed[tok_count - WINDOW_SPAN :, query_width:])

time: 269 us -> 264 us (0.981)
  waiting for transfers between devices: 184 us -> 175 us
  starting transfers between devices: 35.4 us -> 40.8 us
    all_to_all x1 -> x0, waiting for transfers between devices: 51.7 us -> none  [fused_body(): lax.all_to_all(outgoing, 'seq', split_axis=0, concat_axis=0, tiled=True)]
    ppermute x14 -> x32, waiting for transfers between devices: 52.4 us -> 74.2 us  [swapped(): lax.ppermute(value, axis, [(i, i ^ 1) for i in range(lax.axis_size(axis))])]
    ppermute x6 -> x7, waiting for transfers between devices: 76.8 us -> 98.1 us  [flipped(): return lax.ppermute(value, 'seq', [(i, i ^ bit * 2) for i in range(count)])]
    ppermute x14 -> x32, starting transfers between devices: 9.05 us -> 20.2 us  [swapped(): lax.ppermute(value, axis, [(i, i ^ 1) for i in range(lax.axis_size(axis))])]
    all_to_all x1 -> x0, starting transfers between devices: 7.31 us -> none  [fused_body(): lax.all_to_all(outgoing, 'seq', split_axis=0, concat_axis=0, tiled=True)]
    ppermute x6 -> x7, starting transfers between devices: 11.9 us -> 11.4 us  [flipped(): return lax.ppermute(value, 'seq', [(i, i ^ bit * 2) for i in range(count)])]
  transfers between devices with their start and end apart: 23 -> 41, of which waited for: 10 -> 17; matrix products, arithmetic and copies ran while one was open for 2% -> 1% of each run, Pallas kernels for 3% -> 3%
where the time goes in v3:
time: 264 us; the launch traced here: 261 us
  waiting for transfers between devices  175 us (66%)
  starting transfers between devices  40.8 us (15%)
  Pallas kernels  37.3 us (14%)
  local copies, waits for them, and re-layouts  6.28 us (2%)
    ppermute x7, waiting for transfers between devices, flipped(): return lax.ppermute(value, 'seq', [(i, i ^ bit * 2) for i in range(count)])  98.1 us
    ppermute x32, waiting for transfers between devices, swapped(): lax.ppermute(value, axis, [(i, i ^ 1) for i in range(lax.axis_size(axis))])  74.2 us
    ppermute x32, starting transfers between devices, swapped(): lax.ppermute(value, axis, [(i, i ^ 1) for i in range(lax.axis_size(axis))])  20.2 us
    pallas_call x1, Pallas kernels, run_experts(): pl.pallas_call(functools.partial(experts_kernel, seq_count // 2), out_sha...  18 us
    ppermute x7, starting transfers between devices, flipped(): return lax.ppermute(value, 'seq', [(i, i ^ bit * 2) for i in range(count)])  11.4 us
    pallas_call x1, Pallas kernels, attend_and_project(): pl.pallas_call(attention_kernel, out_shape=jax.ShapeDtypeStruct((width, t...  8.17 us
    pallas_call x1, Pallas kernels, project_qkv(): pl.pallas_call(functools.partial(qkv_kernel, rows), out_shape=(jax.ShapeD...  6.85 us
    all_to_all x1, starting transfers between devices, fused_body(): lax.all_to_all(finished, 'seq', split_axis=0, concat_axis=0, tiled=True)  5.63 us
  transfers between devices with their start and end apart: 41, of which 17 were waited for; matrix products, arithmetic and copies ran while one was open for 1% of the time, Pallas kernels for 3%

profile of v3, /device:TPU:0, one launch (start us, length us, event | category | flops | bytes accessed | tf_op | source)
XLA Modules:
  0.0 260.9 jit_solution(10276308063268992381)
XLA Ops:
  0.0 2.2 prepare.1.refs_0_
  2.2 4.1 %collective-permute-start.3 = (bf16[128,1536]{1,0:T(8,128)(2,1)}, bf16[128,1536]{1,0:T(8,128)(2,1)S(1)}, u32[]{:S(2)}, u32[]{:S(2)}) collective-permute-start(bf16[128,1536]{1,0:T(8,128)(2,1)} %prepare.1.refs_0_), channel_id=1, source_target_pairs={{0,8},{2,10},{4,12},{6,14},{8,0},{10,2},{12,4},{14,6},{1,9},{3,11}... | collective-permute-start | bytes 1179656 | tf_op jit(solution)/shard_map/ppermute | solution.py:375
  6.3 1.6 collective-permute-start.1
  7.8 16.3 %collective-permute-done.3.refs_4_ = bf16[128,1536]{1,0:T(8,128)(2,1)S(1)} collective-permute-done((bf16[128,1536]{1,0:T(8,128)(2,1)}, bf16[128,1536]{1,0:T(8,128)(2,1)S(1)}, u32[]{:S(2)}, u32[]{:S(2)}) %collective-permute-start.3) | collective-permute-done | bytes 393248 | tf_op jit(solution)/shard_map/ppermute | solution.py:375
  24.1 0.7 collective-permute-start.5
  24.8 1.5 collective-permute-start
  26.9 1.5 collective-permute-start.2
  28.4 5.9 %collective-permute-done.5.refs_6_ = bf16[128,1536]{1,0:T(8,128)(2,1)S(1)} collective-permute-done((bf16[128,1536]{1,0:T(8,128)(2,1)S(1)}, bf16[128,1536]{1,0:T(8,128)(2,1)S(1)}, u32[]{:S(2)}, u32[]{:S(2)}) %collective-permute-start.5) | collective-permute-done | bytes 393248 | tf_op jit(solution)/shard_map/ppermute | solution.py:375
  34.3 1.3 collective-permute-start.6
  35.7 1.3 collective-permute-done.refs_1_
  37.0 8.4 %collective-permute-done.4.refs_5_ = bf16[128,1536]{1,0:T(8,128)(2,1)S(1)} collective-permute-done((bf16[128,1536]{1,0:T(8,128)(2,1)S(1)}, bf16[128,1536]{1,0:T(8,128)(2,1)S(1)}, u32[]{:S(2)}, u32[]{:S(2)}) %collective-permute-start.4) | collective-permute-done | bytes 393248 | tf_op jit(solution)/shard_map/ppermute | solution.py:439
  45.5 8.4 %collective-permute-done.2.refs_3_ = bf16[128,1536]{1,0:T(8,128)(2,1)S(1)} collective-permute-done((bf16[128,1536]{1,0:T(8,128)(2,1)S(1)}, bf16[128,1536]{1,0:T(8,128)(2,1)S(1)}, u32[]{:S(2)}, u32[]{:S(2)}) %collective-permute-start.2) | collective-permute-done | bytes 393248 | tf_op jit(solution)/shard_map/ppermute | solution.py:439
  53.9 7.3 %collective-permute-done.6.refs_7_ = bf16[128,1536]{1,0:T(8,128)(2,1)} collective-permute-done((bf16[128,1536]{1,0:T(8,128)(2,1)S(1)}, bf16[128,1536]{1,0:T(8,128)(2,1)}, u32[]{:S(2)}, u32[]{:S(2)}) %collective-permute-start.6) | collective-permute-done | bytes 393248 | tf_op jit(solution)/shard_map/ppermute | solution.py:439
  61.2 1.0 copy-done.1
  62.2 18.0 %experts.1 = bf16[8,2,48,1440]{3,2,1,0:T(8,128)(2,1)} custom-call(s32[4]{0:T(128)S(1)} %pad_add_fusion.place_ref, bf16[128,1536]{1,0:T(8,128)(2,1)S(1)} %copy-done.1, bf16[128,1536]{1,0:T(8,128)(2,1)S(1)} %collective-permute-done.refs_1_, bf16[128,1536]{1,0:T(8,128)(2,1)S(1)} %collective-permute-done.1.refs_2_, ...), custom_call_target="tpu_custom_call" | custom-call | tf_op jit(solution)/shard_map/experts/pallas_call | solution.py:152
  80.2 5.6 %all-to-all-start = ((bf16[8,2,48,1440]{3,2,1,0:T(8,128)(2,1)}), bf16[8,2,48,1440]{3,2,1,0:T(8,128)(2,1)S(1)}, u32[]{:S(2)}, u32[]{:S(2)}) async-start(bf16[8,2,48,1440]{3,2,1,0:T(8,128)(2,1)} %experts.1), calls=%async_computation | async-start | bytes 4718592 | tf_op jit(solution)/shard_map/all_to_all | solution.py:425
  85.8 1.6 dynamic-slice_bitcast_fusion
  87.4 2.9 %collective-permute-start.24 = (bf16[360,256]{1,0:T(8,128)(2,1)}, bf16[360,256]{1,0:T(8,128)(2,1)}, u32[]{:S(2)}, u32[]{:S(2)}) collective-permute-start(bf16[360,256]{1,0:T(8,128)(2,1)} %get-tuple-element.16), channel_id=1, source_target_pairs={{0,8},{2,10},{4,12},{6,14},{8,0},{10,2},{12,4},{14,6},{1,9},{3,11}... | collective-permute-start | bytes 552968 | tf_op jit(solution)/shard_map/ppermute | solution.py:375
  90.5 63.7 %collective-permute-done.24 = bf16[360,256]{1,0:T(8,128)(2,1)} collective-permute-done((bf16[360,256]{1,0:T(8,128)(2,1)}, bf16[360,256]{1,0:T(8,128)(2,1)}, u32[]{:S(2)}, u32[]{:S(2)}) %collective-permute-start.24) | collective-permute-done | bytes 184352 | tf_op jit(solution)/shard_map/ppermute | solution.py:375
  154.2 1.0 pad_maximum_fusion.1.rest_0_
  155.3 1.5 collective-permute-start.28
  156.9 2.0 collective-permute-start.8
  158.9 7.8 %collective-permute-done.25.rest_1_ = bf16[2,360,256]{2,1,0:T(8,128)(2,1)S(1)} collective-permute-done((bf16[2,360,256]{2,1,0:T(8,128)(2,1)S(1)}, bf16[2,360,256]{2,1,0:T(8,128)(2,1)S(1)}, u32[]{:S(2)}, u32[]{:S(2)}) %collective-permute-start.25) | collective-permute-done | bytes 368672 | tf_op jit(solution)/shard_map/ppermute | solution.py:375
  166.7 1.5 collective-permute-start.11
  168.3 2.0 collective-permute-start.27
  170.3 4.4 %collective-permute-done.8.rest_1_ = bf16[2,184,640]{2,1,0:T(8,128)(2,1)S(1)} collective-permute-done((bf16[2,184,640]{2,1,0:T(8,128)(2,1)S(1)}, bf16[2,184,640]{2,1,0:T(8,128)(2,1)S(1)}, u32[]{:S(2)}, u32[]{:S(2)}) %collective-permute-start.8) | collective-permute-done | bytes 471072 | tf_op jit(solution)/shard_map/ppermute | solution.py:375
  174.7 1.5 collective-permute-start.29
  176.2 4.1 %collective-permute-done.9.rest_2_ = bf16[2,184,640]{2,1,0:T(8,128)(2,1)S(1)} collective-permute-done((bf16[2,184,640]{2,1,0:T(8,128)(2,1)S(1)}, bf16[2,184,640]{2,1,0:T(8,128)(2,1)S(1)}, u32[]{:S(2)}, u32[]{:S(2)}) %collective-permute-start.9) | collective-permute-done | bytes 471072 | tf_op jit(solution)/shard_map/ppermute | solution.py:439
  180.4 1.5 collective-permute-start.12
  181.9 0.6 collective-permute-start.30
  182.5 5.8 %collective-permute-done.27.rest_3_ = bf16[2,360,256]{2,1,0:T(8,128)(2,1)} collective-permute-done((bf16[2,360,256]{2,1,0:T(8,128)(2,1)S(1)}, bf16[2,360,256]{2,1,0:T(8,128)(2,1)}, u32[]{:S(2)}, u32[]{:S(2)}) %collective-permute-start.27) | collective-permute-done | bytes 368672 | tf_op jit(solution)/shard_map/ppermute | solution.py:439
  188.9 15.1 %collective-permute-done.30.rest_6_ = bf16[2,360,256]{2,1,0:T(8,128)(2,1)} collective-permute-done((bf16[2,360,256]{2,1,0:T(8,128)(2,1)S(1)}, bf16[2,360,256]{2,1,0:T(8,128)(2,1)}, u32[]{:S(2)}, u32[]{:S(2)}) %collective-permute-start.30) | collective-permute-done | bytes 368672 | tf_op jit(solution)/shard_map/ppermute | solution.py:439
  203.9 1.5 collective-permute-start.13
  206.1 0.5 collective-permute-start.14
  206.6 11.0 %collective-permute-done.13.rest_6_ = bf16[2,184,640]{2,1,0:T(8,128)(2,1)S(1)} collective-permute-done((bf16[2,184,640]{2,1,0:T(8,128)(2,1)S(1)}, bf16[2,184,640]{2,1,0:T(8,128)(2,1)S(1)}, u32[]{:S(2)}, u32[]{:S(2)}) %collective-permute-start.13) | collective-permute-done | bytes 471072 | tf_op jit(solution)/shard_map/ppermute | solution.py:439
  217.6 1.5 collective-permute-start.31
  219.9 7.8 %collective-permute-done.14.rest_7_ = bf16[2,184,640]{2,1,0:T(8,128)(2,1)S(1)} collective-permute-done((bf16[2,184,640]{2,1,0:T(8,128)(2,1)S(1)}, bf16[2,184,640]{2,1,0:T(8,128)(2,1)S(1)}, u32[]{:S(2)}, u32[]{:S(2)}) %collective-permute-start.14) | collective-permute-done | bytes 471072 | tf_op jit(solution)/shard_map/ppermute | solution.py:439
  227.7 4.7 %collective-permute-done.31.rest_7_ = bf16[2,360,256]{2,1,0:T(8,128)(2,1)} collective-permute-done((bf16[2,360,256]{2,1,0:T(8,128)(2,1)}, bf16[2,360,256]{2,1,0:T(8,128)(2,1)}, u32[]{:S(2)}, u32[]{:S(2)}) %collective-permute-start.31) | collective-permute-done | bytes 368672 | tf_op jit(solution)/shard_map/ppermute | solution.py:439
  232.4 0.6 collective-permute-start.35
  233.9 0.5 copy-done.22
  234.4 2.1 returns.1
  236.5 1.0 copy-done.2
  237.5 0.9 copy-done.3
  238.4 0.9 copy-done.4
  239.3 6.9 %qkv.1 = (bf16[128,2560]{1,0:T(8,128)(2,1)S(1)}, bf16[1440,128]{1,0:T(8,128)(2,1)S(1)}) custom-call(s32[4]{0:T(128)S(1)} %pad_add_fusion.place_ref, bf16[768,1440]{1,0:T(8,128)(2,1)S(1)} %bitcast.26, bf16[128,1440]{1,0:T(8,128)(2,1)S(1)} %copy-done.2, bf16[128,768]{1,0:T(8,128)(2,1)S(1)} %copy-done.3, bf16[128,768]{1,0:T(8,128)(2,1)S(1)} %copy-done.4, ...), custom_call_target="tpu_custom_call" | custom-call | tf_op jit(solution)/shard_map/qkv/pallas_call | solution.py:240
  246.2 3.5 %collective-permute-start.23 = (bf16[128,512]{1,0:T(8,128)(2,1)S(1)}, bf16[128,512]{1,0:T(8,128)(2,1)S(1)}, u32[]{:S(2)}, u32[]{:S(2)}) collective-permute-start(bf16[128,512]{1,0:T(8,128)(2,1)S(1)} %slice.3), channel_id=1, source_target_pairs={{0,2},{2,4},{4,6},{6,8},{8,10},{10,12},{12,14},{14,1},{1,3},{3,5},... | collective-permute-start | bytes 393224 | tf_op jit(solution)/shard_map/ppermute | solution.py:590
  249.8 2.7 %collective-permute-done.23.halo_ref = bf16[128,512]{1,0:T(8,128)(2,1)S(1)} collective-permute-done((bf16[128,512]{1,0:T(8,128)(2,1)S(1)}, bf16[128,512]{1,0:T(8,128)(2,1)S(1)}, u32[]{:S(2)}, u32[]{:S(2)}) %collective-permute-start.23) | collective-permute-done | bytes 131104 | tf_op jit(solution)/shard_map/ppermute | solution.py:590
  252.5 8.2 %attention.1 = bf16[1440,128]{1,0:T(8,128)(2,1)} custom-call(s32[4]{0:T(128)S(1)} %pad_add_fusion.place_ref, f32[32]{0:T(128)S(1)} %exp.3.sink_ref, bf16[128,2560]{1,0:T(8,128)(2,1)S(1)} %get-tuple-element.13.packed_ref, bf16[128,512]{1,0:T(8,128)(2,1)S(1)} %collective-permute-done.23.halo_ref, bf16[1440,128]{1,0:T(8,128)(2,1)S(1)} %get-tuple-element.14.hidden_ref, ...), custom_call_target="tpu_custom_call" | custom-call | tf_op jit(solution)/shard_map/attention/pallas_call | solution.py:341
  (101 shorter events, 3.9 us)
Async XLA Ops:
  0.0 90.4 %copy-start = (bf16[180,2560]{1,0:T(8,128)(2,1)S(1)}, bf16[180,2560]{1,0:T(8,128)(2,1)}, u32[]{:S(2)}) copy-start(bf16[180,2560]{1,0:T(8,128)(2,1)} %param.17) | copy-start | bytes 2764804
  2.2 21.9 %collective-permute-start.3 = (bf16[128,1536]{1,0:T(8,128)(2,1)}, bf16[128,1536]{1,0:T(8,128)(2,1)S(1)}, u32[]{:S(2)}, u32[]{:S(2)}) collective-permute-start(bf16[128,1536]{1,0:T(8,128)(2,1)} %prepare.1.refs_0_), channel_id=1, source_target_pairs={{0,8},{2,10},{4,12},{6,14},{8,0},{10,2},{12,4},{14,6},{1,9},{3,11}... | collective-permute-start | bytes 1179656 | tf_op jit(solution)/shard_map/ppermute | solution.py:375
  6.3 20.6 %collective-permute-start.1 = (bf16[128,1536]{1,0:T(8,128)(2,1)}, bf16[128,1536]{1,0:T(8,128)(2,1)S(1)}, u32[]{:S(2)}, u32[]{:S(2)}) collective-permute-start(bf16[128,1536]{1,0:T(8,128)(2,1)} %prepare.1.refs_0_), channel_id=1, source_target_pairs={{0,4},{2,6},{4,0},{6,2},{8,12},{10,14},{12,8},{14,10},{1,5},{3,7},... | collective-permute-start | bytes 1179656 | tf_op jit(solution)/shard_map/ppermute | solution.py:375
  24.1 10.2 %collective-permute-start.5 = (bf16[128,1536]{1,0:T(8,128)(2,1)S(1)}, bf16[128,1536]{1,0:T(8,128)(2,1)S(1)}, u32[]{:S(2)}, u32[]{:S(2)}) collective-permute-start(bf16[128,1536]{1,0:T(8,128)(2,1)S(1)} %collective-permute-done.3.refs_4_), channel_id=1, source_target_pairs={{0,4},{2,6},{4,0},{6,2},{8,12},{10,14},{12,8},{14,10},{1,5},{3,7},... | collective-permute-start | bytes 1179656 | tf_op jit(solution)/shard_map/ppermute | solution.py:375
  24.8 12.2 %collective-permute-start = (bf16[128,1536]{1,0:T(8,128)(2,1)}, bf16[128,1536]{1,0:T(8,128)(2,1)S(1)}, u32[]{:S(2)}, u32[]{:S(2)}) collective-permute-start(bf16[128,1536]{1,0:T(8,128)(2,1)} %prepare.1.refs_0_), channel_id=1, source_target_pairs={{0,2},{2,0},{4,6},{6,4},{8,10},{10,8},{12,14},{14,12},{1,3},{3,1},... | collective-permute-start | bytes 1179656 | tf_op jit(solution)/shard_map/ppermute | solution.py:439
  26.4 19.1 %collective-permute-start.4 = (bf16[128,1536]{1,0:T(8,128)(2,1)S(1)}, bf16[128,1536]{1,0:T(8,128)(2,1)S(1)}, u32[]{:S(2)}, u32[]{:S(2)}) collective-permute-start(bf16[128,1536]{1,0:T(8,128)(2,1)S(1)} %collective-permute-done.3.refs_4_), channel_id=1, source_target_pairs={{0,2},{2,0},{4,6},{6,4},{8,10},{10,8},{12,14},{14,12},{1,3},{3,1},... | collective-permute-start | bytes 1179656 | tf_op jit(solution)/shard_map/ppermute | solution.py:439
  26.9 27.0 %collective-permute-start.2 = (bf16[128,1536]{1,0:T(8,128)(2,1)S(1)}, bf16[128,1536]{1,0:T(8,128)(2,1)S(1)}, u32[]{:S(2)}, u32[]{:S(2)}) collective-permute-start(bf16[128,1536]{1,0:T(8,128)(2,1)S(1)} %collective-permute-done.1.refs_2_), channel_id=1, source_target_pairs={{0,2},{2,0},{4,6},{6,4},{8,10},{10,8},{12,14},{14,12},{1,3},{3,1},... | collective-permute-start | bytes 1179656 | tf_op jit(solution)/shard_map/ppermute | solution.py:439
  34.3 26.9 %collective-permute-start.6 = (bf16[128,1536]{1,0:T(8,128)(2,1)S(1)}, bf16[128,1536]{1,0:T(8,128)(2,1)}, u32[]{:S(2)}, u32[]{:S(2)}) collective-permute-start(bf16[128,1536]{1,0:T(8,128)(2,1)S(1)} %collective-permute-done.5.refs_6_), channel_id=1, source_target_pairs={{0,2},{2,0},{4,6},{6,4},{8,10},{10,8},{12,14},{14,12},{1,3},{3,1},... | collective-permute-start | bytes 1179656 | tf_op jit(solution)/shard_map/ppermute | solution.py:439
  62.2 174.3 %copy-start.5 = (f32[1440]{0:T(1024)S(1)}, f32[1440]{0:T(1024)}, u32[]{:S(2)}) copy-start(f32[1440]{0:T(1024)} %gain_ref.3) | copy-start | bytes 17284
  80.2 169.6 %copy-start.26 = (f32[32]{0:T(128)S(1)}, f32[32]{0:T(128)}, u32[]{:S(2)}) copy-start(f32[32]{0:T(128)} %param.18) | copy-start | bytes 388
  80.2 156.3 %all-to-all-start = ((bf16[8,2,48,1440]{3,2,1,0:T(8,128)(2,1)}), bf16[8,2,48,1440]{3,2,1,0:T(8,128)(2,1)S(1)}, u32[]{:S(2)}, u32[]{:S(2)}) async-start(bf16[8,2,48,1440]{3,2,1,0:T(8,128)(2,1)} %experts.1), calls=%async_computation | async-start | bytes 4718592 | tf_op jit(solution)/shard_map/all_to_all | solution.py:425
  87.4 66.8 %collective-permute-start.24 = (bf16[360,256]{1,0:T(8,128)(2,1)}, bf16[360,256]{1,0:T(8,128)(2,1)}, u32[]{:S(2)}, u32[]{:S(2)}) collective-permute-start(bf16[360,256]{1,0:T(8,128)(2,1)} %get-tuple-element.16), channel_id=1, source_target_pairs={{0,8},{2,10},{4,12},{6,14},{8,0},{10,2},{12,4},{14,6},{1,9},{3,11}... | collective-permute-start | bytes 552968 | tf_op jit(solution)/shard_map/ppermute | solution.py:375
  90.4 66.4 %collective-permute-start.7 = (bf16[184,640]{1,0:T(8,128)(2,1)S(1)}, bf16[184,640]{1,0:T(8,128)(2,1)S(1)}, u32[]{:S(2)}, u32[]{:S(2)}) collective-permute-start(bf16[184,640]{1,0:T(8,128)(2,1)S(1)} %get-tuple-element.18), channel_id=1, source_target_pairs={{0,8},{2,10},{4,12},{6,14},{8,0},{10,2},{12,4},{14,6},{1,9},{3,11}... | collective-permute-start | bytes 706568 | tf_op jit(solution)/shard_map/ppermute | solution.py:375
  155.2 11.5 %collective-permute-start.25 = (bf16[2,360,256]{2,1,0:T(8,128)(2,1)S(1)}, bf16[2,360,256]{2,1,0:T(8,128)(2,1)S(1)}, u32[]{:S(2)}, u32[]{:S(2)}) collective-permute-start(bf16[2,360,256]{2,1,0:T(8,128)(2,1)S(1)} %pad_maximum_fusion.1.rest_0_), channel_id=1, source_target_pairs={{0,4},{2,6},{4,0},{6,2},{8,12},{10,14},{12,8},{14,10},{1,5},{3,7},... | collective-permute-start | bytes 1105928 | tf_op jit(solution)/shard_map/ppermute | solution.py:375
  155.2 11.5 %collective-permute-start.26 = (bf16[2,360,256]{2,1,0:T(8,128)(2,1)S(1)}, bf16[2,360,256]{2,1,0:T(8,128)(2,1)S(1)}, u32[]{:S(2)}, u32[]{:S(2)}) collective-permute-start(bf16[2,360,256]{2,1,0:T(8,128)(2,1)S(1)} %pad_maximum_fusion.1.rest_0_), channel_id=1, source_target_pairs={{0,2},{2,0},{4,6},{6,4},{8,10},{10,8},{12,14},{14,12},{1,3},{3,1},... | collective-permute-start | bytes 1105928 | tf_op jit(solution)/shard_map/ppermute | solution.py:439
  155.3 12.9 %collective-permute-start.28 = (bf16[2,360,256]{2,1,0:T(8,128)(2,1)S(1)}, bf16[2,360,256]{2,1,0:T(8,128)(2,1)}, u32[]{:S(2)}, u32[]{:S(2)}) collective-permute-start(bf16[2,360,256]{2,1,0:T(8,128)(2,1)S(1)} %pad_maximum_fusion.1.rest_0_), channel_id=1, source_target_pairs={{0,16},{16,0},{1,17},{17,1},{2,18},{18,2},{3,19},{19,3},{4,20},{20... | collective-permute-start | bytes 1105928 | tf_op jit(solution)/shard_map/ppermute | solution.py:439
  156.9 17.8 %collective-permute-start.8 = (bf16[2,184,640]{2,1,0:T(8,128)(2,1)S(1)}, bf16[2,184,640]{2,1,0:T(8,128)(2,1)S(1)}, u32[]{:S(2)}, u32[]{:S(2)}) collective-permute-start(bf16[2,184,640]{2,1,0:T(8,128)(2,1)S(1)} %pad_maximum_fusion.rest_0_), channel_id=1, source_target_pairs={{0,4},{2,6},{4,0},{6,2},{8,12},{10,14},{12,8},{14,10},{1,5},{3,7},... | collective-permute-start | bytes 1413128 | tf_op jit(solution)/shard_map/ppermute | solution.py:375
  158.9 9.3 %collective-permute-start.32 = (bf16[2,360,256]{2,1,0:T(8,128)(2,1)S(1)}, bf16[2,360,256]{2,1,0:T(8,128)(2,1)S(1)}, u32[]{:S(2)}, u32[]{:S(2)}) collective-permute-start(bf16[2,360,256]{2,1,0:T(8,128)(2,1)S(1)} %pad_maximum_fusion.1.rest_0_), channel_id=1, source_target_pairs={{0,1},{1,0},{2,3},{3,2},{4,5},{5,4},{6,7},{7,6},{8,9},{9,8},{10,11... | collective-permute-start | bytes 1105928 | tf_op jit(solution)/shard_map/ppermute | solution.py:439
  166.7 67.0 %copy-start.23 = (bf16[2,360,256]{2,1,0:T(8,128)(2,1)}, bf16[2,360,256]{2,1,0:T(8,128)(2,1)S(1)}, u32[]{:S(2)}) copy-start(bf16[2,360,256]{2,1,0:T(8,128)(2,1)S(1)} %collective-permute-done.25.rest_1_) | copy-start | bytes 1105924
  166.7 13.7 %collective-permute-start.9 = (bf16[2,184,640]{2,1,0:T(8,128)(2,1)S(1)}, bf16[2,184,640]{2,1,0:T(8,128)(2,1)S(1)}, u32[]{:S(2)}, u32[]{:S(2)}) collective-permute-start(bf16[2,184,640]{2,1,0:T(8,128)(2,1)S(1)} %pad_maximum_fusion.rest_0_), channel_id=1, source_target_pairs={{0,2},{2,0},{4,6},{6,4},{8,10},{10,8},{12,14},{14,12},{1,3},{3,1},... | collective-permute-start | bytes 1413128 | tf_op jit(solution)/shard_map/ppermute | solution.py:439
  166.7 67.0 %copy-start.24 = (bf16[2,360,256]{2,1,0:T(8,128)(2,1)}, bf16[2,360,256]{2,1,0:T(8,128)(2,1)S(1)}, u32[]{:S(2)}) copy-start(bf16[2,360,256]{2,1,0:T(8,128)(2,1)S(1)} %collective-permute-done.26.rest_2_) | copy-start | bytes 1105924
  166.7 13.7 %collective-permute-start.11 = (bf16[2,184,640]{2,1,0:T(8,128)(2,1)S(1)}, bf16[2,184,640]{2,1,0:T(8,128)(2,1)S(1)}, u32[]{:S(2)}, u32[]{:S(2)}) collective-permute-start(bf16[2,184,640]{2,1,0:T(8,128)(2,1)S(1)} %pad_maximum_fusion.rest_0_), channel_id=1, source_target_pairs={{0,16},{16,0},{1,17},{17,1},{2,18},{18,2},{3,19},{19,3},{4,20},{20... | collective-permute-start | bytes 1413128 | tf_op jit(solution)/shard_map/ppermute | solution.py:439
  168.3 13.7 %collective-permute-start.15 = (bf16[2,184,640]{2,1,0:T(8,128)(2,1)S(1)}, bf16[2,184,640]{2,1,0:T(8,128)(2,1)S(1)}, u32[]{:S(2)}, u32[]{:S(2)}) collective-permute-start(bf16[2,184,640]{2,1,0:T(8,128)(2,1)S(1)} %pad_maximum_fusion.rest_0_), channel_id=1, source_target_pairs={{0,1},{1,0},{2,3},{3,2},{4,5},{5,4},{6,7},{7,6},{8,9},{9,8},{10,11... | collective-permute-start | bytes 1413128 | tf_op jit(solution)/shard_map/ppermute | solution.py:439
  168.3 20.1 %collective-permute-start.27 = (bf16[2,360,256]{2,1,0:T(8,128)(2,1)S(1)}, bf16[2,360,256]{2,1,0:T(8,128)(2,1)}, u32[]{:S(2)}, u32[]{:S(2)}) collective-permute-start(bf16[2,360,256]{2,1,0:T(8,128)(2,1)S(1)} %collective-permute-done.25.rest_1_), channel_id=1, source_target_pairs={{0,2},{2,0},{4,6},{6,4},{8,10},{10,8},{12,14},{14,12},{1,3},{3,1},... | collective-permute-start | bytes 1105928 | tf_op jit(solution)/shard_map/ppermute | solution.py:439
  174.7 13.7 %collective-permute-start.29 = (bf16[2,360,256]{2,1,0:T(8,128)(2,1)S(1)}, bf16[2,360,256]{2,1,0:T(8,128)(2,1)}, u32[]{:S(2)}, u32[]{:S(2)}) collective-permute-start(bf16[2,360,256]{2,1,0:T(8,128)(2,1)S(1)} %collective-permute-done.25.rest_1_), channel_id=1, source_target_pairs={{0,16},{16,0},{1,17},{17,1},{2,18},{18,2},{3,19},{19,3},{4,20},{20... | collective-permute-start | bytes 1105928 | tf_op jit(solution)/shard_map/ppermute | solution.py:439
  180.3 38.8 %copy-start.9 = (bf16[2,184,640]{2,1,0:T(8,128)(2,1)}, bf16[2,184,640]{2,1,0:T(8,128)(2,1)S(1)}, u32[]{:S(2)}) copy-start(bf16[2,184,640]{2,1,0:T(8,128)(2,1)S(1)} %collective-permute-done.9.rest_2_) | copy-start | bytes 1413124
  180.3 25.6 %collective-permute-start.10 = (bf16[2,184,640]{2,1,0:T(8,128)(2,1)S(1)}, bf16[2,184,640]{2,1,0:T(8,128)(2,1)S(1)}, u32[]{:S(2)}, u32[]{:S(2)}) collective-permute-start(bf16[2,184,640]{2,1,0:T(8,128)(2,1)S(1)} %collective-permute-done.8.rest_1_), channel_id=1, source_target_pairs={{0,2},{2,0},{4,6},{6,4},{8,10},{10,8},{12,14},{14,12},{1,3},{3,1},... | collective-permute-start | bytes 1413128 | tf_op jit(solution)/shard_map/ppermute | solution.py:439
  180.4 38.8 %copy-start.10 = (bf16[2,184,640]{2,1,0:T(8,128)(2,1)}, bf16[2,184,640]{2,1,0:T(8,128)(2,1)S(1)}, u32[]{:S(2)}) copy-start(bf16[2,184,640]{2,1,0:T(8,128)(2,1)S(1)} %collective-permute-done.11.rest_4_) | copy-start | bytes 1413124
  180.4 25.6 %collective-permute-start.12 = (bf16[2,184,640]{2,1,0:T(8,128)(2,1)S(1)}, bf16[2,184,640]{2,1,0:T(8,128)(2,1)S(1)}, u32[]{:S(2)}, u32[]{:S(2)}) collective-permute-start(bf16[2,184,640]{2,1,0:T(8,128)(2,1)S(1)} %collective-permute-done.8.rest_1_), channel_id=1, source_target_pairs={{0,16},{16,0},{1,17},{17,1},{2,18},{18,2},{3,19},{19,3},{4,20},{20... | collective-permute-start | bytes 1413128 | tf_op jit(solution)/shard_map/ppermute | solution.py:439
  181.9 22.0 %collective-permute-start.30 = (bf16[2,360,256]{2,1,0:T(8,128)(2,1)S(1)}, bf16[2,360,256]{2,1,0:T(8,128)(2,1)}, u32[]{:S(2)}, u32[]{:S(2)}) collective-permute-start(bf16[2,360,256]{2,1,0:T(8,128)(2,1)S(1)} %collective-permute-done.26.rest_2_), channel_id=1, source_target_pairs={{0,16},{16,0},{1,17},{17,1},{2,18},{18,2},{3,19},{19,3},{4,20},{20... | collective-permute-start | bytes 1105928 | tf_op jit(solution)/shard_map/ppermute | solution.py:439
  188.4 17.1 %collective-permute-start.33 = (bf16[2,360,256]{2,1,0:T(8,128)(2,1)S(1)}, bf16[2,360,256]{2,1,0:T(8,128)(2,1)}, u32[]{:S(2)}, u32[]{:S(2)}) collective-permute-start(bf16[2,360,256]{2,1,0:T(8,128)(2,1)S(1)} %collective-permute-done.25.rest_1_), channel_id=1, source_target_pairs={{0,1},{1,0},{2,3},{3,2},{4,5},{5,4},{6,7},{7,6},{8,9},{9,8},{10,11... | collective-permute-start | bytes 1105928 | tf_op jit(solution)/shard_map/ppermute | solution.py:439
  188.4 17.0 %collective-permute-start.34 = (bf16[2,360,256]{2,1,0:T(8,128)(2,1)S(1)}, bf16[2,360,256]{2,1,0:T(8,128)(2,1)}, u32[]{:S(2)}, u32[]{:S(2)}) collective-permute-start(bf16[2,360,256]{2,1,0:T(8,128)(2,1)S(1)} %collective-permute-done.26.rest_2_), channel_id=1, source_target_pairs={{0,1},{1,0},{2,3},{3,2},{4,5},{5,4},{6,7},{7,6},{8,9},{9,8},{10,11... | collective-permute-start | bytes 1105928 | tf_op jit(solution)/shard_map/ppermute | solution.py:439
  203.9 13.7 %collective-permute-start.13 = (bf16[2,184,640]{2,1,0:T(8,128)(2,1)S(1)}, bf16[2,184,640]{2,1,0:T(8,128)(2,1)S(1)}, u32[]{:S(2)}, u32[]{:S(2)}) collective-permute-start(bf16[2,184,640]{2,1,0:T(8,128)(2,1)S(1)} %collective-permute-done.9.rest_2_), channel_id=1, source_target_pairs={{0,16},{16,0},{1,17},{17,1},{2,18},{18,2},{3,19},{19,3},{4,20},{20... | collective-permute-start | bytes 1413128 | tf_op jit(solution)/shard_map/ppermute | solution.py:439
  205.4 13.7 %collective-permute-start.16 = (bf16[2,184,640]{2,1,0:T(8,128)(2,1)S(1)}, bf16[2,184,640]{2,1,0:T(8,128)(2,1)S(1)}, u32[]{:S(2)}, u32[]{:S(2)}) collective-permute-start(bf16[2,184,640]{2,1,0:T(8,128)(2,1)S(1)} %collective-permute-done.8.rest_1_), channel_id=1, source_target_pairs={{0,1},{1,0},{2,3},{3,2},{4,5},{5,4},{6,7},{7,6},{8,9},{9,8},{10,11... | collective-permute-start | bytes 1413128 | tf_op jit(solution)/shard_map/ppermute | solution.py:439
  205.5 13.7 %collective-permute-start.17 = (bf16[2,184,640]{2,1,0:T(8,128)(2,1)S(1)}, bf16[2,184,640]{2,1,0:T(8,128)(2,1)S(1)}, u32[]{:S(2)}, u32[]{:S(2)}) collective-permute-start(bf16[2,184,640]{2,1,0:T(8,128)(2,1)S(1)} %collective-permute-done.9.rest_2_), channel_id=1, source_target_pairs={{0,1},{1,0},{2,3},{3,2},{4,5},{5,4},{6,7},{7,6},{8,9},{9,8},{10,11... | collective-permute-start | bytes 1413128 | tf_op jit(solution)/shard_map/ppermute | solution.py:439
  206.0 13.8 %collective-permute-start.19 = (bf16[2,184,640]{2,1,0:T(8,128)(2,1)S(1)}, bf16[2,184,640]{2,1,0:T(8,128)(2,1)S(1)}, u32[]{:S(2)}, u32[]{:S(2)}) collective-permute-start(bf16[2,184,640]{2,1,0:T(8,128)(2,1)S(1)} %collective-permute-done.11.rest_4_), channel_id=1, source_target_pairs={{0,1},{1,0},{2,3},{3,2},{4,5},{5,4},{6,7},{7,6},{8,9},{9,8},{10,11... | collective-permute-start | bytes 1413128 | tf_op jit(solution)/shard_map/ppermute | solution.py:439
  206.1 21.6 %collective-permute-start.14 = (bf16[2,184,640]{2,1,0:T(8,128)(2,1)S(1)}, bf16[2,184,640]{2,1,0:T(8,128)(2,1)S(1)}, u32[]{:S(2)}, u32[]{:S(2)}) collective-permute-start(bf16[2,184,640]{2,1,0:T(8,128)(2,1)S(1)} %collective-permute-done.10.rest_3_), channel_id=1, source_target_pairs={{0,16},{16,0},{1,17},{17,1},{2,18},{18,2},{3,19},{19,3},{4,20},{20... | collective-permute-start | bytes 1413128 | tf_op jit(solution)/shard_map/ppermute | solution.py:439
  217.6 14.8 %collective-permute-start.31 = (bf16[2,360,256]{2,1,0:T(8,128)(2,1)}, bf16[2,360,256]{2,1,0:T(8,128)(2,1)}, u32[]{:S(2)}, u32[]{:S(2)}) collective-permute-start(bf16[2,360,256]{2,1,0:T(8,128)(2,1)} %collective-permute-done.27.rest_3_), channel_id=1, source_target_pairs={{0,16},{16,0},{1,17},{17,1},{2,18},{18,2},{3,19},{19,3},{4,20},{20... | collective-permute-start | bytes 1105928 | tf_op jit(solution)/shard_map/ppermute | solution.py:439
  219.1 13.3 %collective-permute-start.18 = (bf16[2,184,640]{2,1,0:T(8,128)(2,1)S(1)}, bf16[2,184,640]{2,1,0:T(8,128)(2,1)S(1)}, u32[]{:S(2)}, u32[]{:S(2)}) collective-permute-start(bf16[2,184,640]{2,1,0:T(8,128)(2,1)S(1)} %collective-permute-done.10.rest_3_), channel_id=1, source_target_pairs={{0,1},{1,0},{2,3},{3,2},{4,5},{5,4},{6,7},{7,6},{8,9},{9,8},{10,11... | collective-permute-start | bytes 1413128 | tf_op jit(solution)/shard_map/ppermute | solution.py:439
  219.2 13.7 %collective-permute-start.20 = (bf16[2,184,640]{2,1,0:T(8,128)(2,1)S(1)}, bf16[2,184,640]{2,1,0:T(8,128)(2,1)S(1)}, u32[]{:S(2)}, u32[]{:S(2)}) collective-permute-start(bf16[2,184,640]{2,1,0:T(8,128)(2,1)S(1)} %collective-permute-done.12.rest_5_), channel_id=1, source_target_pairs={{0,1},{1,0},{2,3},{3,2},{4,5},{5,4},{6,7},{7,6},{8,9},{9,8},{10,11... | collective-permute-start | bytes 1413128 | tf_op jit(solution)/shard_map/ppermute | solution.py:439
  219.8 13.3 %collective-permute-start.21 = (bf16[2,184,640]{2,1,0:T(8,128)(2,1)S(1)}, bf16[2,184,640]{2,1,0:T(8,128)(2,1)S(1)}, u32[]{:S(2)}, u32[]{:S(2)}) collective-permute-start(bf16[2,184,640]{2,1,0:T(8,128)(2,1)S(1)} %collective-permute-done.13.rest_6_), channel_id=1, source_target_pairs={{0,1},{1,0},{2,3},{3,2},{4,5},{5,4},{6,7},{7,6},{8,9},{9,8},{10,11... | collective-permute-start | bytes 1413128 | tf_op jit(solution)/shard_map/ppermute | solution.py:439
  227.7 5.9 %collective-permute-start.22 = (bf16[2,184,640]{2,1,0:T(8,128)(2,1)S(1)}, bf16[2,184,640]{2,1,0:T(8,128)(2,1)S(1)}, u32[]{:S(2)}, u32[]{:S(2)}) collective-permute-start(bf16[2,184,640]{2,1,0:T(8,128)(2,1)S(1)} %collective-permute-done.14.rest_7_), channel_id=1, source_target_pairs={{0,1},{1,0},{2,3},{3,2},{4,5},{5,4},{6,7},{7,6},{8,9},{9,8},{10,11... | collective-permute-start | bytes 1413128 | tf_op jit(solution)/shard_map/ppermute | solution.py:439
  232.4 13.9 %collective-permute-start.36 = (bf16[2,360,256]{2,1,0:T(8,128)(2,1)}, bf16[2,360,256]{2,1,0:T(8,128)(2,1)}, u32[]{:S(2)}, u32[]{:S(2)}) collective-permute-start(bf16[2,360,256]{2,1,0:T(8,128)(2,1)} %collective-permute-done.28.rest_4_), channel_id=1, source_target_pairs={{0,1},{1,0},{2,3},{3,2},{4,5},{5,4},{6,7},{7,6},{8,9},{9,8},{10,11... | collective-permute-start | bytes 1105928 | tf_op jit(solution)/shard_map/ppermute | solution.py:439
  232.4 17.4 %collective-permute-start.35 = (bf16[2,360,256]{2,1,0:T(8,128)(2,1)}, bf16[2,360,256]{2,1,0:T(8,128)(2,1)}, u32[]{:S(2)}, u32[]{:S(2)}) collective-permute-start(bf16[2,360,256]{2,1,0:T(8,128)(2,1)} %collective-permute-done.27.rest_3_), channel_id=1, source_target_pairs={{0,1},{1,0},{2,3},{3,2},{4,5},{5,4},{6,7},{7,6},{8,9},{9,8},{10,11... | collective-permute-start | bytes 1105928 | tf_op jit(solution)/shard_map/ppermute | solution.py:439
  233.0 16.8 %collective-permute-start.37 = (bf16[2,360,256]{2,1,0:T(8,128)(2,1)}, bf16[2,360,256]{2,1,0:T(8,128)(2,1)}, u32[]{:S(2)}, u32[]{:S(2)}) collective-permute-start(bf16[2,360,256]{2,1,0:T(8,128)(2,1)} %collective-permute-done.29.rest_5_), channel_id=1, source_target_pairs={{0,1},{1,0},{2,3},{3,2},{4,5},{5,4},{6,7},{7,6},{8,9},{9,8},{10,11... | collective-permute-start | bytes 1105928 | tf_op jit(solution)/shard_map/ppermute | solution.py:439
  233.1 16.7 %collective-permute-start.38 = (bf16[2,360,256]{2,1,0:T(8,128)(2,1)}, bf16[2,360,256]{2,1,0:T(8,128)(2,1)}, u32[]{:S(2)}, u32[]{:S(2)}) collective-permute-start(bf16[2,360,256]{2,1,0:T(8,128)(2,1)} %collective-permute-done.30.rest_6_), channel_id=1, source_target_pairs={{0,1},{1,0},{2,3},{3,2},{4,5},{5,4},{6,7},{7,6},{8,9},{9,8},{10,11... | collective-permute-start | bytes 1105928 | tf_op jit(solution)/shard_map/ppermute | solution.py:439
  233.6 16.2 %collective-permute-start.39 = (bf16[2,360,256]{2,1,0:T(8,128)(2,1)}, bf16[2,360,256]{2,1,0:T(8,128)(2,1)}, u32[]{:S(2)}, u32[]{:S(2)}) collective-permute-start(bf16[2,360,256]{2,1,0:T(8,128)(2,1)} %collective-permute-done.31.rest_7_), channel_id=1, source_target_pairs={{0,1},{1,0},{2,3},{3,2},{4,5},{5,4},{6,7},{7,6},{8,9},{9,8},{10,11... | collective-permute-start | bytes 1105928 | tf_op jit(solution)/shard_map/ppermute | solution.py:439
  246.2 6.3 %collective-permute-start.23 = (bf16[128,512]{1,0:T(8,128)(2,1)S(1)}, bf16[128,512]{1,0:T(8,128)(2,1)S(1)}, u32[]{:S(2)}, u32[]{:S(2)}) collective-permute-start(bf16[128,512]{1,0:T(8,128)(2,1)S(1)} %slice.3), channel_id=1, source_target_pairs={{0,2},{2,4},{4,6},{6,8},{8,10},{10,12},{12,14},{14,1},{1,3},{3,5},... | collective-permute-start | bytes 393224 | tf_op jit(solution)/shard_map/ppermute | solution.py:590
  (20 other events, 226.0 us)

commit v4 on v3

--- a/solution.py
+++ b/solution.py
@@ -62,7 +62,7 @@
     width, tok_count = tokens_t.shape
     return pl.pallas_call(
         prepare_kernel,
-        out_shape=jax.ShapeDtypeStruct((tok_count, width + slot_lanes(width)), BF16),
+        out_shape=pltpu.HBM((tok_count, width + slot_lanes(width)), BF16),
         in_specs=[VMEM] * 3,
         out_specs=VMEM,
         name="prepare",
@@ -93,9 +93,9 @@
     return pl.pallas_call(
         returns_kernel,
         out_shape=(
-            jax.ShapeDtypeStruct((tok_count, width), BF16),
-            jax.ShapeDtypeStruct((tok_count, E * CAP), BF16),
-            jax.ShapeDtypeStruct((tok_count, E * CAP), BF16),
+            pltpu.VMEM((tok_count, width), BF16),
+            pltpu.VMEM((tok_count, E * CAP), BF16),
+            pltpu.VMEM((tok_count, E * CAP), BF16),
         ),
         in_specs=[VMEM] * 3,
         out_specs=(VMEM,) * 3,
@@ -165,21 +165,22 @@
             pltpu.VMEM((seq_count, sent - width, tok_count), F32),
             pltpu.VMEM((seq_count * CAP, width), F32),
         ],
-        compiler_params=pltpu.CompilerParams(vmem_limit_bytes=48 << 20),
+        compiler_params=pltpu.CompilerParams(vmem_limit_bytes=40 << 20),
         name="experts",
-    )(place, *blocks, gate_up, down_proj)
+    )(place, *blocks, *in_hbm([gate_up, down_proj]))
 
 
 def in_hbm(parts):
     return [pltpu.with_memory_space_constraint(part, pltpu.HBM) for part in parts]
 
 
-def start_copies(parts, held, sems):
+def start_copies(parts, held, sems, first):
     half = held.shape[1] // 2
     copies = []
     for i, part in enumerate(parts):
         target = held.at[i // 2, pl.ds(i % 2 * half, half)]
-        copy = pltpu.make_async_copy(part, target, sems.at[i])
+        source = part.at[:, :, pl.ds(first, held.shape[3])]
+        copy = pltpu.make_async_copy(source, target, sems.at[i])
         copy.start()
         copies.append(copy)
     return [copies[i : i + 2] for i in range(0, len(copies), 2)]
@@ -202,25 +203,10 @@
     return (place_ref[2] + group_flip) % 2 * 2 + (place_ref[3] + pipe_flip) % 2
 
 
-def qkv_kernel(
-    rows, place_ref, tables_ref, residual_ref, coarse_ref, fine_ref, gain_ref, *rest
-):
-    parts, (packed_ref, hidden_ref, held, slices, sems) = rest[:16], rest[16:]
-    lines, _, columns = held.shape[1:]
-    copies = start_copies(parts, held, sems)
-    table = tables_ref[...]
-    mixed = jnp.dot(coarse_ref[...], table, preferred_element_type=F32)
-    mixed += jnp.dot(fine_ref[...], table, preferred_element_type=F32)
-    hidden = (residual_ref[...].astype(F32) + mixed).astype(BF16)
-    value = hidden.astype(F32)
-    hidden_ref[...] = value.T.astype(BF16)
-    mean_square = jnp.mean(value * value, axis=-1, keepdims=True)
-    normed = value * lax.rsqrt(mean_square + eps) * gain_ref[...][None, :]
-    slices[...] = jnp.zeros_like(slices)
-    for s in range(2 * lines):
-        slices[s, :, :rows] = normed[:, s * rows : (s + 1) * rows].astype(BF16)
+def columns_of(held, slices, place_ref, copies, lines, columns, out_ref):
+    tok_count = slices.shape[1]
     for pair in range(4):
-        total = jnp.zeros((value.shape[0], columns), F32)
+        total = jnp.zeros((tok_count, columns), F32)
         for flip in range(2):
             for copy in copies[pair * 2 + flip]:
                 copy.wait()
@@ -231,39 +217,81 @@
                     preferred_element_type=F32,
                 )
         start = quarter_of(place_ref, pair % 2, pair // 2) * columns
-        packed_ref[:, pl.ds(pl.multiple_of(start, 128), columns)] = total.astype(BF16)
-
-
-def project_qkv(place, tables, residual, coarse, fine, gain, parts, rows, columns):
+        out_ref[:, pl.ds(pl.multiple_of(start, 128), columns)] = total.astype(BF16)
+
+
+def pairs_kernel(
+    rows, place_ref, tables_ref, residual_ref, coarse_ref, fine_ref, gain_ref, *rest
+):
+    parts, (pairs_ref, slices, hidden_ref, held, sems) = rest[:16], rest[16:]
+    lines, _, columns = held.shape[1:]
+    copies = start_copies(parts, held, sems, parts[0].shape[2] - columns)
+    table = tables_ref[...]
+    mixed = jnp.dot(coarse_ref[...], table, preferred_element_type=F32)
+    mixed += jnp.dot(fine_ref[...], table, preferred_element_type=F32)
+    hidden = (residual_ref[...].astype(F32) + mixed).astype(BF16)
+    value = hidden.astype(F32)
+    mean_square = jnp.mean(value * value, axis=-1, keepdims=True)
+    normed = (value * lax.rsqrt(mean_square + eps) * gain_ref[...][None, :]).astype(BF16)
+    slices[...] = jnp.zeros_like(slices)
+    for s in range(2 * lines):
+        slices[s, :, :rows] = normed[:, s * rows : (s + 1) * rows]
+    columns_of(held, slices, place_ref, copies, lines, columns, pairs_ref)
+    hidden_ref[...] = value.T.astype(BF16)
+
+
+def project_pairs(place, tables, residual, coarse, fine, gain, parts, rows, columns):
     tok_count, width = residual.shape
     lines, padded = 2 * parts[0].shape[0], parts[0].shape[1]
     return pl.pallas_call(
-        functools.partial(qkv_kernel, rows),
+        functools.partial(pairs_kernel, rows),
         out_shape=(
             jax.ShapeDtypeStruct((tok_count, 4 * columns), BF16),
+            jax.ShapeDtypeStruct((2 * lines, tok_count, padded), BF16),
             jax.ShapeDtypeStruct((width, tok_count), BF16),
         ),
         in_specs=[SMEM] + [VMEM] * 5 + [HBM] * 16,
-        out_specs=(VMEM, VMEM),
+        out_specs=(VMEM,) * 3,
         scratch_shapes=[
             pltpu.VMEM((8, lines, padded, columns), BF16),
-            pltpu.VMEM((2 * lines, tok_count, padded), BF16),
             pltpu.SemaphoreType.DMA((16,)),
         ],
-        compiler_params=pltpu.CompilerParams(vmem_limit_bytes=40 << 20),
-        name="qkv",
+        compiler_params=pltpu.CompilerParams(vmem_limit_bytes=20 << 20),
+        name="pairs",
     )(place, tables, residual, coarse, fine, gain, *in_hbm(parts))
 
 
+def queries_kernel(place_ref, slices, *rest):
+    parts, (queries_ref, held, sems) = rest[:16], rest[16:]
+    lines, _, columns = held.shape[1:]
+    copies = start_copies(parts, held, sems, 0)
+    columns_of(held, slices, place_ref, copies, lines, columns, queries_ref)
+
+
+def project_queries(place, slices, parts, columns):
+    count, tok_count, padded = slices.shape
+    return pl.pallas_call(
+        queries_kernel,
+        out_shape=jax.ShapeDtypeStruct((tok_count, 4 * columns), BF16),
+        in_specs=[SMEM, VMEM] + [HBM] * 16,
+        out_specs=VMEM,
+        scratch_shapes=[
+            pltpu.VMEM((8, count // 2, padded, columns), BF16),
+            pltpu.SemaphoreType.DMA((16,)),
+        ],
+        compiler_params=pltpu.CompilerParams(vmem_limit_bytes=20 << 20),
+        name="queries",
+    )(place, slices, *in_hbm(parts))
+
+
 def attention_kernel(
-    place_ref, sink_ref, packed_ref, halo_ref, hidden_ref, *rest
+    place_ref, sink_ref, packed_ref, pairs_ref, halo_ref, hidden_ref, *rest
 ):
     parts, (out_ref, held, mixed, total_ref, sems) = rest[:16], rest[16:]
     lines, quarter_rows, depth = held.shape[1:]
-    copies = start_copies(parts, held, sems)
+    copies = start_copies(parts, held, sems, 0)
     tok_count = packed_ref.shape[0]
     pair_width = 2 * HEAD_SIZE
-    query_width = QUERY_HEADS * HEAD_SIZE
     kv_width = KEY_VALUE_HEADS * HEAD_SIZE
     query_groups = QUERY_HEADS // KEY_VALUE_HEADS
     span = halo_ref.shape[0]
@@ -277,10 +305,10 @@
     left = lax.broadcasted_iota(jnp.int32, (extent, pair_width), 1) < HEAD_SIZE
     scale = float(HEAD_SIZE) ** (-0.5)
 
-    def sides(start, head):
+    def sides(start, head, factor):
         lanes = pl.ds(start + head // 2 * pair_width, pair_width)
-        own = packed_ref[:, query_width + start + head // 2 * pair_width :][:, :pair_width]
-        both = jnp.concatenate([halo_ref[:, lanes], own], axis=0).astype(F32)
+        both = jnp.concatenate([halo_ref[:, lanes], pairs_ref[:, lanes]], axis=0)
+        both = both.astype(F32) * factor
         turned = pltpu.roll(both, HEAD_SIZE, 1)
         low, high = (both, turned) if head % 2 == 0 else (turned, both)
         low = jnp.where(left, low, 0.0).astype(BF16)
@@ -289,7 +317,7 @@
 
     pairs = query_groups // 2
     for head in range(KEY_VALUE_HEADS):
-        keys, values = sides(0, head), sides(kv_width, head)
+        keys, values = sides(0, head, scale), sides(kv_width, head, 1.0)
         base = head * pairs * pair_width
         stacked = jnp.concatenate(
             [packed_ref[:, base + j * pair_width : base + (j + 1) * pair_width] for j in range(pairs)],
@@ -302,11 +330,11 @@
             )
             probs = []
             for j in range(pairs):
-                piece = scores[j * tok_count : (j + 1) * tok_count] * scale
+                piece = scores[j * tok_count : (j + 1) * tok_count]
                 weights = jnp.where(allowed, jnp.exp(piece), 0.0)
                 sink = sink_ref[head * query_groups + 2 * j + side]
                 sums = jnp.sum(weights, axis=-1, keepdims=True) + sink
-                probs.append((weights / sums).astype(BF16))
+                probs.append((weights * (1.0 / sums)).astype(BF16))
             part = jnp.dot(
                 jnp.concatenate(probs, axis=0), values[side], preferred_element_type=F32
             )
@@ -334,14 +362,14 @@
     out_ref[...] = (hidden_ref[...].astype(F32) + total_ref[...]).astype(BF16)
 
 
-def attend_and_project(place, sinks, packed, halo, hidden_t, parts):
+def attend_and_project(place, sinks, queries, pairs, halo, hidden_t, parts):
     width, tok_count = hidden_t.shape
     half, quarter_rows, depth = parts[0].shape
     lines = 2 * half
     return pl.pallas_call(
         attention_kernel,
         out_shape=jax.ShapeDtypeStruct((width, tok_count), BF16),
-        in_specs=[SMEM] * 2 + [VMEM] * 3 + [HBM] * 16,
+        in_specs=[SMEM] * 2 + [VMEM] * 4 + [HBM] * 16,
         out_specs=VMEM,
         scratch_shapes=[
             pltpu.VMEM((8, lines, quarter_rows, depth), BF16),
@@ -349,9 +377,9 @@
             pltpu.VMEM((width, tok_count), F32),
             pltpu.SemaphoreType.DMA((16,)),
         ],
-        compiler_params=pltpu.CompilerParams(vmem_limit_bytes=40 << 20),
+        compiler_params=pltpu.CompilerParams(vmem_limit_bytes=24 << 20),
         name="attention",
-    )(place, sinks, packed, halo, hidden_t, *in_hbm(parts))
+    )(place, sinks, queries, pairs, halo, hidden_t, *in_hbm(parts))
 
 
 def place_of():
@@ -364,8 +392,11 @@
 def own_quarters(qkv_proj, out_proj):
     rows, qkv_width = qkv_proj.shape
     quarter = lax.axis_index("groups") % 2 * 2 + lax.axis_index("pipe")
-    qw, ow = qkv_width // 4, out_proj.shape[1] // 4
-    mine_qkv = lax.dynamic_slice_in_dim(qkv_proj, quarter * qw, qw, 1)
+    query_width = QUERY_HEADS * HEAD_SIZE
+    qw, pw, ow = query_width // 4, (qkv_width - query_width) // 4, out_proj.shape[1] // 4
+    mine_queries = lax.dynamic_slice_in_dim(qkv_proj, quarter * qw, qw, 1)
+    mine_pairs = lax.dynamic_slice_in_dim(qkv_proj, query_width + quarter * pw, pw, 1)
+    mine_qkv = jnp.concatenate([mine_queries, mine_pairs], axis=1)
     mine_out = lax.dynamic_slice_in_dim(out_proj.T, quarter * ow, ow, 0)
     return jnp.pad(mine_qkv, ((0, -rows % 8), (0, 0))), mine_out
 
@@ -385,19 +416,16 @@
     return [found[step] for step in range(0, lines, 2)]
 
 
-def gather_quarters(mine, lines):
-    even = jnp.stack(far_blocks(mine, lines))
+def gather_quarters(mine, lines, last_axis):
+    far = far_blocks(mine, lines)
+    even = jnp.stack(far)
     odd = flipped(even, 1)
-    parts = []
     even_mate, even_across = swapped(even, "seq"), swapped(even, "groups")
     odd_mate, odd_across = swapped(odd, "seq"), swapped(odd, "groups")
     even_last = swapped(even_mate, "groups")
-    odd_last = swapped(odd_mate, "groups")
+    odd_last = swapped(odd_across if last_axis == "seq" else odd_mate, last_axis)
     parts = [even, odd, even_mate, odd_mate, even_across, odd_across, even_last, odd_last]
-    beside = []
-    for part in parts:
-        beside.append(swapped(part, "pipe"))
-    return parts + beside
+    return parts + [swapped(part, "pipe") for part in parts]
 
 
 def fused_body(
@@ -418,20 +446,21 @@
         for value in (even, odd):
             blocks += [value, swapped(value, "seq")]
     mine_qkv, mine_out = own_quarters(qkv_proj, out_proj)
-    qkv_parts = gather_quarters(mine_qkv, lines)
-    out_parts = gather_quarters(mine_out, lines)
-
-    finished = run_experts(place, blocks, gate_up, down_proj)
+    qkv_parts = gather_quarters(mine_qkv, lines, "groups")
+    out_parts = gather_quarters(mine_out, lines, "seq")
+
+    finished = run_experts(place, in_hbm(blocks[:1]) + blocks[1:], gate_up, down_proj)
     summed = lax.all_to_all(finished, "seq", split_axis=0, concat_axis=0, tiled=True)
     residual, coarse, fine = returns(tokens_t, routes_t, scale_t)
 
     summed = summed.reshape(E * CAP, width)
-    packed, hidden_t = project_qkv(
-        place, summed, residual, coarse, fine, attn_gain, qkv_parts, rows, qkv_width // 4
-    )
     query_width = QUERY_HEADS * HEAD_SIZE
-    halo = halo_exchange(packed[tok_count - WINDOW_SPAN :, query_width:])
-    out_t = attend_and_project(place, jnp.exp(sinks), packed, halo, hidden_t, out_parts)
+    pairs, slices, hidden_t = project_pairs(
+        place, summed, residual, coarse, fine, attn_gain, qkv_parts, rows, (qkv_width - query_width) // 4
+    )
+    halo = halo_exchange(pairs[tok_count - WINDOW_SPAN :])
+    queries = project_queries(place, slices, qkv_parts, query_width // 4)
+    out_t = attend_and_project(place, jnp.exp(sinks), queries, pairs, halo, hidden_t, out_parts)
     return out_t.T[None]
 
 

time: 264 us -> 252 us (0.955)
  waiting for transfers between devices: 175 us -> 170 us
  local copies, waits for them, and re-layouts: 6.28 us -> 1.63 us
  starting transfers between devices: 40.8 us -> 37.4 us
    ppermute x32, waiting for transfers between devices: 74.2 us -> 68.2 us  [swapped(): lax.ppermute(value, axis, [(i, i ^ 1) for i in range(lax.axis_size(axis))])]
    unnamed x54 -> x46, local copies, waits for them, and re-layouts: 4.59 us -> 0.65 us
    ppermute x7, waiting for transfers between devices: 98.1 us -> 101 us  [flipped(): return lax.ppermute(value, 'seq', [(i, i ^ bit * 2) for i in range(count)])]
    ppermute x1, waiting for transfers between devices: 2.73 us -> 0.01 us  [halo_exchange(): lax.ppermute(pairs, ('seq', 'pipe'), list(zip(order[:-1], order[1:])))]
    pallas_call x3 -> x4, Pallas kernels: 11.1 us -> 12.8 us  [the longest x1 5.58 us: project_pairs(): pl.pallas_call(functools.partial(pairs_kernel, rows), out_shape=(jax.Shap...]
  transfers between devices with their start and end apart: 41 -> 41, of which waited for: 17 -> 17; matrix products, arithmetic and copies ran while one was open for 1% -> 0% of each run, Pallas kernels for 3% -> 4%
where the time goes in v4:
time: 252 us; the launch traced here: 249 us
  waiting for transfers between devices  170 us (67%)
  Pallas kernels  39.2 us (16%)
  starting transfers between devices  37.4 us (15%)
    ppermute x7, waiting for transfers between devices, flipped(): return lax.ppermute(value, 'seq', [(i, i ^ bit * 2) for i in range(count)])  101 us
    ppermute x32, waiting for transfers between devices, swapped(): lax.ppermute(value, axis, [(i, i ^ 1) for i in range(lax.axis_size(axis))])  68.2 us
    ppermute x32, starting transfers between devices, swapped(): lax.ppermute(value, axis, [(i, i ^ 1) for i in range(lax.axis_size(axis))])  19.6 us
    pallas_call x1, Pallas kernels, run_experts(): pl.pallas_call(functools.partial(experts_kernel, seq_count // 2), out_sha...  18.2 us
    ppermute x7, starting transfers between devices, flipped(): return lax.ppermute(value, 'seq', [(i, i ^ bit * 2) for i in range(count)])  10.6 us
    pallas_call x1, Pallas kernels, attend_and_project(): pl.pallas_call(attention_kernel, out_shape=jax.ShapeDtypeStruct((width, t...  8.19 us
    all_to_all x1, starting transfers between devices, fused_body(): lax.all_to_all(finished, 'seq', split_axis=0, concat_axis=0, tiled=True)  5.64 us
    pallas_call x1, Pallas kernels, project_pairs(): pl.pallas_call(functools.partial(pairs_kernel, rows), out_shape=(jax.Shap...  5.58 us
  transfers between devices with their start and end apart: 41, of which 17 were waited for; matrix products, arithmetic and copies ran while one was open for 0% of the time, Pallas kernels for 4%

profile of v4, /device:TPU:0, one launch (start us, length us, event | category | flops | bytes accessed | tf_op | source)
XLA Modules:
  0.0 248.7 jit_solution(4304116878489973429)
XLA Ops:
  0.0 2.2 prepare.1.refs_0_
  2.2 4.1 %collective-permute-start.3 = (bf16[128,1536]{1,0:T(8,128)(2,1)}, bf16[128,1536]{1,0:T(8,128)(2,1)S(1)}, u32[]{:S(2)}, u32[]{:S(2)}) collective-permute-start(bf16[128,1536]{1,0:T(8,128)(2,1)} %prepare.1.refs_0_), channel_id=1, source_target_pairs={{0,8},{2,10},{4,12},{6,14},{8,0},{10,2},{12,4},{14,6},{1,9},{3,11}... | collective-permute-start | bytes 1179656 | tf_op jit(solution)/shard_map/ppermute | solution.py:406
  6.3 1.6 collective-permute-start.1
  7.8 16.3 %collective-permute-done.3.refs_4_ = bf16[128,1536]{1,0:T(8,128)(2,1)S(1)} collective-permute-done((bf16[128,1536]{1,0:T(8,128)(2,1)}, bf16[128,1536]{1,0:T(8,128)(2,1)S(1)}, u32[]{:S(2)}, u32[]{:S(2)}) %collective-permute-start.3) | collective-permute-done | bytes 393248 | tf_op jit(solution)/shard_map/ppermute | solution.py:406
  24.1 0.7 collective-permute-start.5
  24.8 1.5 collective-permute-start
  26.4 0.5 collective-permute-start.4
  26.9 1.5 collective-permute-start.2
  28.4 5.9 %collective-permute-done.5.refs_6_ = bf16[128,1536]{1,0:T(8,128)(2,1)S(1)} collective-permute-done((bf16[128,1536]{1,0:T(8,128)(2,1)S(1)}, bf16[128,1536]{1,0:T(8,128)(2,1)S(1)}, u32[]{:S(2)}, u32[]{:S(2)}) %collective-permute-start.5) | collective-permute-done | bytes 393248 | tf_op jit(solution)/shard_map/ppermute | solution.py:406
  34.3 1.3 collective-permute-start.6
  35.7 1.3 collective-permute-done.refs_1_
  37.0 8.4 %collective-permute-done.4.refs_5_ = bf16[128,1536]{1,0:T(8,128)(2,1)S(1)} collective-permute-done((bf16[128,1536]{1,0:T(8,128)(2,1)S(1)}, bf16[128,1536]{1,0:T(8,128)(2,1)S(1)}, u32[]{:S(2)}, u32[]{:S(2)}) %collective-permute-start.4) | collective-permute-done | bytes 393248 | tf_op jit(solution)/shard_map/ppermute | solution.py:468
  45.5 8.4 %collective-permute-done.2.refs_3_ = bf16[128,1536]{1,0:T(8,128)(2,1)S(1)} collective-permute-done((bf16[128,1536]{1,0:T(8,128)(2,1)S(1)}, bf16[128,1536]{1,0:T(8,128)(2,1)S(1)}, u32[]{:S(2)}, u32[]{:S(2)}) %collective-permute-start.2) | collective-permute-done | bytes 393248 | tf_op jit(solution)/shard_map/ppermute | solution.py:468
  53.9 7.3 %collective-permute-done.6.refs_7_ = bf16[128,1536]{1,0:T(8,128)(2,1)} collective-permute-done((bf16[128,1536]{1,0:T(8,128)(2,1)S(1)}, bf16[128,1536]{1,0:T(8,128)(2,1)}, u32[]{:S(2)}, u32[]{:S(2)}) %collective-permute-start.6) | collective-permute-done | bytes 393248 | tf_op jit(solution)/shard_map/ppermute | solution.py:468
  61.2 18.2 %experts.1 = bf16[8,2,48,1440]{3,2,1,0:T(8,128)(2,1)} custom-call(s32[4]{0:T(128)S(1)} %pad_add_fusion.place_ref, bf16[128,1536]{1,0:T(8,128)(2,1)} %prepare.1.refs_0_, bf16[128,1536]{1,0:T(8,128)(2,1)S(1)} %collective-permute-done.refs_1_, bf16[128,1536]{1,0:T(8,128)(2,1)S(1)} %collective-permute-done.1.refs_2_, ...), custom_call_target="tpu_custom_call" | custom-call | tf_op jit(solution)/shard_map/experts/pallas_call | solution.py:152
  79.4 5.6 %all-to-all-start = ((bf16[8,2,48,1440]{3,2,1,0:T(8,128)(2,1)}), bf16[8,2,48,1440]{3,2,1,0:T(8,128)(2,1)}, u32[]{:S(2)}, u32[]{:S(2)}) async-start(bf16[8,2,48,1440]{3,2,1,0:T(8,128)(2,1)} %experts.1), calls=%async_computation | async-start | bytes 4718592 | tf_op jit(solution)/shard_map/all_to_all | solution.py:453
  85.0 0.9 dynamic-slice_bitcast_fusion
  85.9 3.0 %collective-permute-start.24 = (bf16[360,256]{1,0:T(8,128)(2,1)S(1)}, bf16[360,256]{1,0:T(8,128)(2,1)S(1)}, u32[]{:S(2)}, u32[]{:S(2)}) collective-permute-start(bf16[360,256]{1,0:T(8,128)(2,1)S(1)} %get-tuple-element.18), channel_id=1, source_target_pairs={{0,8},{2,10},{4,12},{6,14},{8,0},{10,2},{12,4},{14,6},{1,9},{3,11}... | collective-permute-start | bytes 552968 | tf_op jit(solution)/shard_map/ppermute | solution.py:406
  89.1 64.1 %collective-permute-done.24 = bf16[360,256]{1,0:T(8,128)(2,1)S(1)} collective-permute-done((bf16[360,256]{1,0:T(8,128)(2,1)S(1)}, bf16[360,256]{1,0:T(8,128)(2,1)S(1)}, u32[]{:S(2)}, u32[]{:S(2)}) %collective-permute-start.24) | collective-permute-done | bytes 184352 | tf_op jit(solution)/shard_map/ppermute | solution.py:406
  153.5 1.5 collective-permute-start.28
  155.0 1.0 collective-permute-done.7
  156.1 1.0 collective-permute-start.8
  157.1 7.8 %collective-permute-done.25.rest_1_ = bf16[2,360,256]{2,1,0:T(8,128)(2,1)S(1)} collective-permute-done((bf16[2,360,256]{2,1,0:T(8,128)(2,1)S(1)}, bf16[2,360,256]{2,1,0:T(8,128)(2,1)S(1)}, u32[]{:S(2)}, u32[]{:S(2)}) %collective-permute-start.25) | collective-permute-done | bytes 368672 | tf_op jit(solution)/shard_map/ppermute | solution.py:406
  164.8 0.5 collective-permute-start.9
  165.4 1.5 collective-permute-start.11
  166.9 0.6 collective-permute-start.29
  167.5 6.4 %collective-permute-done.8.rest_1_ = bf16[2,184,640]{2,1,0:T(8,128)(2,1)S(1)} collective-permute-done((bf16[2,184,640]{2,1,0:T(8,128)(2,1)S(1)}, bf16[2,184,640]{2,1,0:T(8,128)(2,1)S(1)}, u32[]{:S(2)}, u32[]{:S(2)}) %collective-permute-start.8) | collective-permute-done | bytes 471072 | tf_op jit(solution)/shard_map/ppermute | solution.py:406
  173.9 1.5 collective-permute-start.27
  175.4 0.9 collective-permute-done.9.rest_2_
  176.2 1.7 collective-permute-start.10
  178.0 1.0 collective-permute-done.11.rest_4_
  179.0 1.5 collective-permute-start.12
  180.5 0.5 collective-permute-start.30
  181.0 6.0 %collective-permute-done.29.rest_5_ = bf16[2,360,256]{2,1,0:T(8,128)(2,1)} collective-permute-done((bf16[2,360,256]{2,1,0:T(8,128)(2,1)S(1)}, bf16[2,360,256]{2,1,0:T(8,128)(2,1)}, u32[]{:S(2)}, u32[]{:S(2)}) %collective-permute-start.29) | collective-permute-done | bytes 368672 | tf_op jit(solution)/shard_map/ppermute | solution.py:468
  187.0 0.5 collective-permute-start.34
  187.5 16.2 %collective-permute-done.30.rest_6_ = bf16[2,360,256]{2,1,0:T(8,128)(2,1)} collective-permute-done((bf16[2,360,256]{2,1,0:T(8,128)(2,1)S(1)}, bf16[2,360,256]{2,1,0:T(8,128)(2,1)}, u32[]{:S(2)}, u32[]{:S(2)}) %collective-permute-start.30) | collective-permute-done | bytes 368672 | tf_op jit(solution)/shard_map/ppermute | solution.py:468
  203.7 1.5 collective-permute-start.13
  205.2 0.5 collective-permute-start.17
  205.8 0.5 collective-permute-start.14
  206.3 11.0 %collective-permute-done.13.rest_6_ = bf16[2,184,640]{2,1,0:T(8,128)(2,1)S(1)} collective-permute-done((bf16[2,184,640]{2,1,0:T(8,128)(2,1)S(1)}, bf16[2,184,640]{2,1,0:T(8,128)(2,1)S(1)}, u32[]{:S(2)}, u32[]{:S(2)}) %collective-permute-start.13) | collective-permute-done | bytes 471072 | tf_op jit(solution)/shard_map/ppermute | solution.py:468
  218.3 6.9 %collective-permute-done.14.rest_7_ = bf16[2,184,640]{2,1,0:T(8,128)(2,1)S(1)} collective-permute-done((bf16[2,184,640]{2,1,0:T(8,128)(2,1)S(1)}, bf16[2,184,640]{2,1,0:T(8,128)(2,1)S(1)}, u32[]{:S(2)}, u32[]{:S(2)}) %collective-permute-start.14) | collective-permute-done | bytes 471072 | tf_op jit(solution)/shard_map/ppermute | solution.py:468
  226.4 0.7 collective-permute-done.22.rest_15_
  227.3 0.6 copy-done.17
  227.9 1.3 returns.1
  229.3 5.6 %pairs.1 = (bf16[128,512]{1,0:T(8,128)(2,1)S(1)}, bf16[8,128,184]{2,1,0:T(8,128)(2,1)S(1)}, bf16[1440,128]{1,0:T(8,128)(2,1)S(1)}) custom-call(s32[4]{0:T(128)S(1)} %pad_add_fusion.place_ref, bf16[768,1440]{1,0:T(8,128)(2,1)} %bitcast.8.tables_ref, bf16[128,1440]{1,0:T(8,128)(2,1)S(1)} %get-tuple-element.11.residual_ref, ...), custom_call_target="tpu_custom_call" | custom-call | tf_op jit(solution)/shard_map/pairs/pallas_call | solution.py:246
  234.9 1.6 collective-permute-start.23
  236.5 3.8 %queries.1.packed_ref = bf16[128,2048]{1,0:T(8,128)(2,1)S(1)} custom-call(s32[4]{0:T(128)S(1)} %pad_add_fusion.place_ref, bf16[8,128,184]{2,1,0:T(8,128)(2,1)S(1)} %get-tuple-element.14.slices, bf16[2,184,640]{2,1,0:T(8,128)(2,1)} %copy-done.2, bf16[2,184,640]{2,1,0:T(8,128)(2,1)} %copy-done.3, bf16[2,184,640]{2,1,0:T(8,128)(2,1)} %copy-done.4, ...), custom_call_target="tpu_custom_call" | custom-call | tf_op jit(solution)/shard_map/queries/pallas_call | solution.py:273
  240.3 8.2 %attention.1 = bf16[1440,128]{1,0:T(8,128)(2,1)} custom-call(s32[4]{0:T(128)S(1)} %pad_add_fusion.place_ref, f32[32]{0:T(128)S(1)} %exp.3.sink_ref, bf16[128,2048]{1,0:T(8,128)(2,1)S(1)} %queries.1.packed_ref, bf16[128,512]{1,0:T(8,128)(2,1)S(1)} %get-tuple-element.15.pairs_ref, bf16[128,512]{1,0:T(8,128)(2,1)S(1)} %collective-permute-done.23.halo_ref, ...), custom_call_target="tpu_custom_call" | custom-call | tf_op jit(solution)/shard_map/attention/pallas_call | solution.py:369
  (94 shorter events, 2.9 us)
Async XLA Ops:
  0.0 88.9 %copy-start = (bf16[180,2560]{1,0:T(8,128)(2,1)S(1)}, bf16[180,2560]{1,0:T(8,128)(2,1)}, u32[]{:S(2)}) copy-start(bf16[180,2560]{1,0:T(8,128)(2,1)} %param.17) | copy-start | bytes 2764804
  2.2 21.9 %collective-permute-start.3 = (bf16[128,1536]{1,0:T(8,128)(2,1)}, bf16[128,1536]{1,0:T(8,128)(2,1)S(1)}, u32[]{:S(2)}, u32[]{:S(2)}) collective-permute-start(bf16[128,1536]{1,0:T(8,128)(2,1)} %prepare.1.refs_0_), channel_id=1, source_target_pairs={{0,8},{2,10},{4,12},{6,14},{8,0},{10,2},{12,4},{14,6},{1,9},{3,11}... | collective-permute-start | bytes 1179656 | tf_op jit(solution)/shard_map/ppermute | solution.py:406
  6.3 20.6 %collective-permute-start.1 = (bf16[128,1536]{1,0:T(8,128)(2,1)}, bf16[128,1536]{1,0:T(8,128)(2,1)S(1)}, u32[]{:S(2)}, u32[]{:S(2)}) collective-permute-start(bf16[128,1536]{1,0:T(8,128)(2,1)} %prepare.1.refs_0_), channel_id=1, source_target_pairs={{0,4},{2,6},{4,0},{6,2},{8,12},{10,14},{12,8},{14,10},{1,5},{3,7},... | collective-permute-start | bytes 1179656 | tf_op jit(solution)/shard_map/ppermute | solution.py:406
  24.1 10.2 %collective-permute-start.5 = (bf16[128,1536]{1,0:T(8,128)(2,1)S(1)}, bf16[128,1536]{1,0:T(8,128)(2,1)S(1)}, u32[]{:S(2)}, u32[]{:S(2)}) collective-permute-start(bf16[128,1536]{1,0:T(8,128)(2,1)S(1)} %collective-permute-done.3.refs_4_), channel_id=1, source_target_pairs={{0,4},{2,6},{4,0},{6,2},{8,12},{10,14},{12,8},{14,10},{1,5},{3,7},... | collective-permute-start | bytes 1179656 | tf_op jit(solution)/shard_map/ppermute | solution.py:406
  24.8 12.2 %collective-permute-start = (bf16[128,1536]{1,0:T(8,128)(2,1)}, bf16[128,1536]{1,0:T(8,128)(2,1)S(1)}, u32[]{:S(2)}, u32[]{:S(2)}) collective-permute-start(bf16[128,1536]{1,0:T(8,128)(2,1)} %prepare.1.refs_0_), channel_id=1, source_target_pairs={{0,2},{2,0},{4,6},{6,4},{8,10},{10,8},{12,14},{14,12},{1,3},{3,1},... | collective-permute-start | bytes 1179656 | tf_op jit(solution)/shard_map/ppermute | solution.py:468
  26.4 19.1 %collective-permute-start.4 = (bf16[128,1536]{1,0:T(8,128)(2,1)S(1)}, bf16[128,1536]{1,0:T(8,128)(2,1)S(1)}, u32[]{:S(2)}, u32[]{:S(2)}) collective-permute-start(bf16[128,1536]{1,0:T(8,128)(2,1)S(1)} %collective-permute-done.3.refs_4_), channel_id=1, source_target_pairs={{0,2},{2,0},{4,6},{6,4},{8,10},{10,8},{12,14},{14,12},{1,3},{3,1},... | collective-permute-start | bytes 1179656 | tf_op jit(solution)/shard_map/ppermute | solution.py:468
  26.9 27.0 %collective-permute-start.2 = (bf16[128,1536]{1,0:T(8,128)(2,1)S(1)}, bf16[128,1536]{1,0:T(8,128)(2,1)S(1)}, u32[]{:S(2)}, u32[]{:S(2)}) collective-permute-start(bf16[128,1536]{1,0:T(8,128)(2,1)S(1)} %collective-permute-done.1.refs_2_), channel_id=1, source_target_pairs={{0,2},{2,0},{4,6},{6,4},{8,10},{10,8},{12,14},{14,12},{1,3},{3,1},... | collective-permute-start | bytes 1179656 | tf_op jit(solution)/shard_map/ppermute | solution.py:468
  34.3 26.9 %collective-permute-start.6 = (bf16[128,1536]{1,0:T(8,128)(2,1)S(1)}, bf16[128,1536]{1,0:T(8,128)(2,1)}, u32[]{:S(2)}, u32[]{:S(2)}) collective-permute-start(bf16[128,1536]{1,0:T(8,128)(2,1)S(1)} %collective-permute-done.5.refs_6_), channel_id=1, source_target_pairs={{0,2},{2,0},{4,6},{6,4},{8,10},{10,8},{12,14},{14,12},{1,3},{3,1},... | collective-permute-start | bytes 1179656 | tf_op jit(solution)/shard_map/ppermute | solution.py:468
  35.7 193.5 %copy-start.1 = (f32[1440]{0:T(1024)S(1)}, f32[1440]{0:T(1024)}, u32[]{:S(2)}) copy-start(f32[1440]{0:T(1024)} %gain_ref.3) | copy-start | bytes 17284
  79.4 157.1 %copy-start.22 = (f32[32]{0:T(128)S(1)}, f32[32]{0:T(128)}, u32[]{:S(2)}) copy-start(f32[32]{0:T(128)} %param.18) | copy-start | bytes 388
  79.4 149.9 %all-to-all-start = ((bf16[8,2,48,1440]{3,2,1,0:T(8,128)(2,1)}), bf16[8,2,48,1440]{3,2,1,0:T(8,128)(2,1)}, u32[]{:S(2)}, u32[]{:S(2)}) async-start(bf16[8,2,48,1440]{3,2,1,0:T(8,128)(2,1)} %experts.1), calls=%async_computation | async-start | bytes 4718592 | tf_op jit(solution)/shard_map/all_to_all | solution.py:453
  85.9 67.3 %collective-permute-start.24 = (bf16[360,256]{1,0:T(8,128)(2,1)S(1)}, bf16[360,256]{1,0:T(8,128)(2,1)S(1)}, u32[]{:S(2)}, u32[]{:S(2)}) collective-permute-start(bf16[360,256]{1,0:T(8,128)(2,1)S(1)} %get-tuple-element.18), channel_id=1, source_target_pairs={{0,8},{2,10},{4,12},{6,14},{8,0},{10,2},{12,4},{14,6},{1,9},{3,11}... | collective-permute-start | bytes 552968 | tf_op jit(solution)/shard_map/ppermute | solution.py:406
  89.0 67.0 %collective-permute-start.7 = (bf16[184,640]{1,0:T(8,128)(2,1)S(1)}, bf16[184,640]{1,0:T(8,128)(2,1)S(1)}, u32[]{:S(2)}, u32[]{:S(2)}) collective-permute-start(bf16[184,640]{1,0:T(8,128)(2,1)S(1)} %get-tuple-element.20), channel_id=1, source_target_pairs={{0,8},{2,10},{4,12},{6,14},{8,0},{10,2},{12,4},{14,6},{1,9},{3,11}... | collective-permute-start | bytes 706568 | tf_op jit(solution)/shard_map/ppermute | solution.py:406
  153.3 86.9 %copy-start.18 = (bf16[2,360,256]{2,1,0:T(8,128)(2,1)}, bf16[2,360,256]{2,1,0:T(8,128)(2,1)S(1)}, u32[]{:S(2)}) copy-start(bf16[2,360,256]{2,1,0:T(8,128)(2,1)S(1)} %pad_maximum_fusion.1.rest_0_) | copy-start | bytes 1105924
  153.3 11.5 %collective-permute-start.25 = (bf16[2,360,256]{2,1,0:T(8,128)(2,1)S(1)}, bf16[2,360,256]{2,1,0:T(8,128)(2,1)S(1)}, u32[]{:S(2)}, u32[]{:S(2)}) collective-permute-start(bf16[2,360,256]{2,1,0:T(8,128)(2,1)S(1)} %pad_maximum_fusion.1.rest_0_), channel_id=1, source_target_pairs={{0,4},{2,6},{4,0},{6,2},{8,12},{10,14},{12,8},{14,10},{1,5},{3,7},... | collective-permute-start | bytes 1105928 | tf_op jit(solution)/shard_map/ppermute | solution.py:406
  153.4 12.0 %collective-permute-start.26 = (bf16[2,360,256]{2,1,0:T(8,128)(2,1)S(1)}, bf16[2,360,256]{2,1,0:T(8,128)(2,1)S(1)}, u32[]{:S(2)}, u32[]{:S(2)}) collective-permute-start(bf16[2,360,256]{2,1,0:T(8,128)(2,1)S(1)} %pad_maximum_fusion.1.rest_0_), channel_id=1, source_target_pairs={{0,2},{2,0},{4,6},{6,4},{8,10},{10,8},{12,14},{14,12},{1,3},{3,1},... | collective-permute-start | bytes 1105928 | tf_op jit(solution)/shard_map/ppermute | solution.py:468
  153.5 13.4 %collective-permute-start.28 = (bf16[2,360,256]{2,1,0:T(8,128)(2,1)S(1)}, bf16[2,360,256]{2,1,0:T(8,128)(2,1)}, u32[]{:S(2)}, u32[]{:S(2)}) collective-permute-start(bf16[2,360,256]{2,1,0:T(8,128)(2,1)S(1)} %pad_maximum_fusion.1.rest_0_), channel_id=1, source_target_pairs={{0,16},{16,0},{1,17},{17,1},{2,18},{18,2},{3,19},{19,3},{4,20},{20... | collective-permute-start | bytes 1105928 | tf_op jit(solution)/shard_map/ppermute | solution.py:468
  156.0 73.2 %copy-start.2 = (bf16[2,184,640]{2,1,0:T(8,128)(2,1)}, bf16[2,184,640]{2,1,0:T(8,128)(2,1)S(1)}, u32[]{:S(2)}) copy-start(bf16[2,184,640]{2,1,0:T(8,128)(2,1)S(1)} %pad_maximum_fusion.rest_0_) | copy-start | bytes 1413124
  156.1 17.8 %collective-permute-start.8 = (bf16[2,184,640]{2,1,0:T(8,128)(2,1)S(1)}, bf16[2,184,640]{2,1,0:T(8,128)(2,1)S(1)}, u32[]{:S(2)}, u32[]{:S(2)}) collective-permute-start(bf16[2,184,640]{2,1,0:T(8,128)(2,1)S(1)} %pad_maximum_fusion.rest_0_), channel_id=1, source_target_pairs={{0,4},{2,6},{4,0},{6,2},{8,12},{10,14},{12,8},{14,10},{1,5},{3,7},... | collective-permute-start | bytes 1413128 | tf_op jit(solution)/shard_map/ppermute | solution.py:406
  157.1 9.8 %collective-permute-start.32 = (bf16[2,360,256]{2,1,0:T(8,128)(2,1)S(1)}, bf16[2,360,256]{2,1,0:T(8,128)(2,1)S(1)}, u32[]{:S(2)}, u32[]{:S(2)}) collective-permute-start(bf16[2,360,256]{2,1,0:T(8,128)(2,1)S(1)} %pad_maximum_fusion.1.rest_0_), channel_id=1, source_target_pairs={{0,1},{1,0},{2,3},{3,2},{4,5},{5,4},{6,7},{7,6},{8,9},{9,8},{10,11... | collective-permute-start | bytes 1105928 | tf_op jit(solution)/shard_map/ppermute | solution.py:468
  164.8 62.4 %copy-start.19 = (bf16[2,360,256]{2,1,0:T(8,128)(2,1)}, bf16[2,360,256]{2,1,0:T(8,128)(2,1)S(1)}, u32[]{:S(2)}) copy-start(bf16[2,360,256]{2,1,0:T(8,128)(2,1)S(1)} %collective-permute-done.25.rest_1_) | copy-start | bytes 1105924
  164.8 11.4 %collective-permute-start.9 = (bf16[2,184,640]{2,1,0:T(8,128)(2,1)S(1)}, bf16[2,184,640]{2,1,0:T(8,128)(2,1)S(1)}, u32[]{:S(2)}, u32[]{:S(2)}) collective-permute-start(bf16[2,184,640]{2,1,0:T(8,128)(2,1)S(1)} %pad_maximum_fusion.rest_0_), channel_id=1, source_target_pairs={{0,2},{2,0},{4,6},{6,4},{8,10},{10,8},{12,14},{14,12},{1,3},{3,1},... | collective-permute-start | bytes 1413128 | tf_op jit(solution)/shard_map/ppermute | solution.py:468
  165.4 61.9 %copy-start.20 = (bf16[2,360,256]{2,1,0:T(8,128)(2,1)}, bf16[2,360,256]{2,1,0:T(8,128)(2,1)S(1)}, u32[]{:S(2)}) copy-start(bf16[2,360,256]{2,1,0:T(8,128)(2,1)S(1)} %collective-permute-done.26.rest_2_) | copy-start | bytes 1105924
  165.4 13.7 %collective-permute-start.11 = (bf16[2,184,640]{2,1,0:T(8,128)(2,1)S(1)}, bf16[2,184,640]{2,1,0:T(8,128)(2,1)S(1)}, u32[]{:S(2)}, u32[]{:S(2)}) collective-permute-start(bf16[2,184,640]{2,1,0:T(8,128)(2,1)S(1)} %pad_maximum_fusion.rest_0_), channel_id=1, source_target_pairs={{0,16},{16,0},{1,17},{17,1},{2,18},{18,2},{3,19},{19,3},{4,20},{20... | collective-permute-start | bytes 1413128 | tf_op jit(solution)/shard_map/ppermute | solution.py:468
  166.9 13.7 %collective-permute-start.15 = (bf16[2,184,640]{2,1,0:T(8,128)(2,1)S(1)}, bf16[2,184,640]{2,1,0:T(8,128)(2,1)S(1)}, u32[]{:S(2)}, u32[]{:S(2)}) collective-permute-start(bf16[2,184,640]{2,1,0:T(8,128)(2,1)S(1)} %pad_maximum_fusion.rest_0_), channel_id=1, source_target_pairs={{0,1},{1,0},{2,3},{3,2},{4,5},{5,4},{6,7},{7,6},{8,9},{9,8},{10,11... | collective-permute-start | bytes 1413128 | tf_op jit(solution)/shard_map/ppermute | solution.py:468
  166.9 20.1 %collective-permute-start.29 = (bf16[2,360,256]{2,1,0:T(8,128)(2,1)S(1)}, bf16[2,360,256]{2,1,0:T(8,128)(2,1)}, u32[]{:S(2)}, u32[]{:S(2)}) collective-permute-start(bf16[2,360,256]{2,1,0:T(8,128)(2,1)S(1)} %collective-permute-done.25.rest_1_), channel_id=1, source_target_pairs={{0,16},{16,0},{1,17},{17,1},{2,18},{18,2},{3,19},{19,3},{4,20},{20... | collective-permute-start | bytes 1105928 | tf_op jit(solution)/shard_map/ppermute | solution.py:468
  173.9 13.1 %collective-permute-start.27 = (bf16[2,360,256]{2,1,0:T(8,128)(2,1)S(1)}, bf16[2,360,256]{2,1,0:T(8,128)(2,1)}, u32[]{:S(2)}, u32[]{:S(2)}) collective-permute-start(bf16[2,360,256]{2,1,0:T(8,128)(2,1)S(1)} %collective-permute-done.25.rest_1_), channel_id=1, source_target_pairs={{0,2},{2,0},{4,6},{6,4},{8,10},{10,8},{12,14},{14,12},{1,3},{3,1},... | collective-permute-start | bytes 1105928 | tf_op jit(solution)/shard_map/ppermute | solution.py:468
  176.2 29.5 %collective-permute-start.10 = (bf16[2,184,640]{2,1,0:T(8,128)(2,1)S(1)}, bf16[2,184,640]{2,1,0:T(8,128)(2,1)S(1)}, u32[]{:S(2)}, u32[]{:S(2)}) collective-permute-start(bf16[2,184,640]{2,1,0:T(8,128)(2,1)S(1)} %collective-permute-done.8.rest_1_), channel_id=1, source_target_pairs={{0,2},{2,0},{4,6},{6,4},{8,10},{10,8},{12,14},{14,12},{1,3},{3,1},... | collective-permute-start | bytes 1413128 | tf_op jit(solution)/shard_map/ppermute | solution.py:468
  179.0 26.8 %collective-permute-start.12 = (bf16[2,184,640]{2,1,0:T(8,128)(2,1)S(1)}, bf16[2,184,640]{2,1,0:T(8,128)(2,1)S(1)}, u32[]{:S(2)}, u32[]{:S(2)}) collective-permute-start(bf16[2,184,640]{2,1,0:T(8,128)(2,1)S(1)} %collective-permute-done.8.rest_1_), channel_id=1, source_target_pairs={{0,16},{16,0},{1,17},{17,1},{2,18},{18,2},{3,19},{19,3},{4,20},{20... | collective-permute-start | bytes 1413128 | tf_op jit(solution)/shard_map/ppermute | solution.py:468
  180.5 23.2 %collective-permute-start.30 = (bf16[2,360,256]{2,1,0:T(8,128)(2,1)S(1)}, bf16[2,360,256]{2,1,0:T(8,128)(2,1)}, u32[]{:S(2)}, u32[]{:S(2)}) collective-permute-start(bf16[2,360,256]{2,1,0:T(8,128)(2,1)S(1)} %collective-permute-done.26.rest_2_), channel_id=1, source_target_pairs={{0,16},{16,0},{1,17},{17,1},{2,18},{18,2},{3,19},{19,3},{4,20},{20... | collective-permute-start | bytes 1105928 | tf_op jit(solution)/shard_map/ppermute | solution.py:468
  187.0 18.2 %collective-permute-start.33 = (bf16[2,360,256]{2,1,0:T(8,128)(2,1)S(1)}, bf16[2,360,256]{2,1,0:T(8,128)(2,1)}, u32[]{:S(2)}, u32[]{:S(2)}) collective-permute-start(bf16[2,360,256]{2,1,0:T(8,128)(2,1)S(1)} %collective-permute-done.25.rest_1_), channel_id=1, source_target_pairs={{0,1},{1,0},{2,3},{3,2},{4,5},{5,4},{6,7},{7,6},{8,9},{9,8},{10,11... | collective-permute-start | bytes 1105928 | tf_op jit(solution)/shard_map/ppermute | solution.py:468
  187.0 18.2 %collective-permute-start.34 = (bf16[2,360,256]{2,1,0:T(8,128)(2,1)S(1)}, bf16[2,360,256]{2,1,0:T(8,128)(2,1)}, u32[]{:S(2)}, u32[]{:S(2)}) collective-permute-start(bf16[2,360,256]{2,1,0:T(8,128)(2,1)S(1)} %collective-permute-done.26.rest_2_), channel_id=1, source_target_pairs={{0,1},{1,0},{2,3},{3,2},{4,5},{5,4},{6,7},{7,6},{8,9},{9,8},{10,11... | collective-permute-start | bytes 1105928 | tf_op jit(solution)/shard_map/ppermute | solution.py:468
  203.7 13.7 %collective-permute-start.13 = (bf16[2,184,640]{2,1,0:T(8,128)(2,1)S(1)}, bf16[2,184,640]{2,1,0:T(8,128)(2,1)S(1)}, u32[]{:S(2)}, u32[]{:S(2)}) collective-permute-start(bf16[2,184,640]{2,1,0:T(8,128)(2,1)S(1)} %collective-permute-done.9.rest_2_), channel_id=1, source_target_pairs={{0,16},{16,0},{1,17},{17,1},{2,18},{18,2},{3,19},{19,3},{4,20},{20... | collective-permute-start | bytes 1413128 | tf_op jit(solution)/shard_map/ppermute | solution.py:468
  205.2 12.5 %collective-permute-start.16 = (bf16[2,184,640]{2,1,0:T(8,128)(2,1)S(1)}, bf16[2,184,640]{2,1,0:T(8,128)(2,1)S(1)}, u32[]{:S(2)}, u32[]{:S(2)}) collective-permute-start(bf16[2,184,640]{2,1,0:T(8,128)(2,1)S(1)} %collective-permute-done.8.rest_1_), channel_id=1, source_target_pairs={{0,1},{1,0},{2,3},{3,2},{4,5},{5,4},{6,7},{7,6},{8,9},{9,8},{10,11... | collective-permute-start | bytes 1413128 | tf_op jit(solution)/shard_map/ppermute | solution.py:468
  205.2 12.5 %collective-permute-start.17 = (bf16[2,184,640]{2,1,0:T(8,128)(2,1)S(1)}, bf16[2,184,640]{2,1,0:T(8,128)(2,1)S(1)}, u32[]{:S(2)}, u32[]{:S(2)}) collective-permute-start(bf16[2,184,640]{2,1,0:T(8,128)(2,1)S(1)} %collective-permute-done.9.rest_2_), channel_id=1, source_target_pairs={{0,1},{1,0},{2,3},{3,2},{4,5},{5,4},{6,7},{7,6},{8,9},{9,8},{10,11... | collective-permute-start | bytes 1413128 | tf_op jit(solution)/shard_map/ppermute | solution.py:468
  205.7 12.5 %collective-permute-start.19 = (bf16[2,184,640]{2,1,0:T(8,128)(2,1)S(1)}, bf16[2,184,640]{2,1,0:T(8,128)(2,1)S(1)}, u32[]{:S(2)}, u32[]{:S(2)}) collective-permute-start(bf16[2,184,640]{2,1,0:T(8,128)(2,1)S(1)} %collective-permute-done.11.rest_4_), channel_id=1, source_target_pairs={{0,1},{1,0},{2,3},{3,2},{4,5},{5,4},{6,7},{7,6},{8,9},{9,8},{10,11... | collective-permute-start | bytes 1413128 | tf_op jit(solution)/shard_map/ppermute | solution.py:468
  205.8 19.5 %collective-permute-start.14 = (bf16[2,184,640]{2,1,0:T(8,128)(2,1)S(1)}, bf16[2,184,640]{2,1,0:T(8,128)(2,1)S(1)}, u32[]{:S(2)}, u32[]{:S(2)}) collective-permute-start(bf16[2,184,640]{2,1,0:T(8,128)(2,1)S(1)} %collective-permute-done.10.rest_3_), channel_id=1, source_target_pairs={{0,16},{16,0},{1,17},{17,1},{2,18},{18,2},{3,19},{19,3},{4,20},{20... | collective-permute-start | bytes 1413128 | tf_op jit(solution)/shard_map/ppermute | solution.py:468
  217.3 7.9 %collective-permute-start.31 = (bf16[2,360,256]{2,1,0:T(8,128)(2,1)}, bf16[2,360,256]{2,1,0:T(8,128)(2,1)}, u32[]{:S(2)}, u32[]{:S(2)}) collective-permute-start(bf16[2,360,256]{2,1,0:T(8,128)(2,1)} %collective-permute-done.29.rest_5_), channel_id=1, source_target_pairs={{0,2},{2,0},{4,6},{6,4},{8,10},{10,8},{12,14},{14,12},{1,3},{3,1},... | collective-permute-start | bytes 1105928 | tf_op jit(solution)/shard_map/ppermute | solution.py:468
  217.7 8.1 %collective-permute-start.18 = (bf16[2,184,640]{2,1,0:T(8,128)(2,1)S(1)}, bf16[2,184,640]{2,1,0:T(8,128)(2,1)S(1)}, u32[]{:S(2)}, u32[]{:S(2)}) collective-permute-start(bf16[2,184,640]{2,1,0:T(8,128)(2,1)S(1)} %collective-permute-done.10.rest_3_), channel_id=1, source_target_pairs={{0,1},{1,0},{2,3},{3,2},{4,5},{5,4},{6,7},{7,6},{8,9},{9,8},{10,11... | collective-permute-start | bytes 1413128 | tf_op jit(solution)/shard_map/ppermute | solution.py:468
  217.7 8.1 %collective-permute-start.20 = (bf16[2,184,640]{2,1,0:T(8,128)(2,1)S(1)}, bf16[2,184,640]{2,1,0:T(8,128)(2,1)S(1)}, u32[]{:S(2)}, u32[]{:S(2)}) collective-permute-start(bf16[2,184,640]{2,1,0:T(8,128)(2,1)S(1)} %collective-permute-done.12.rest_5_), channel_id=1, source_target_pairs={{0,1},{1,0},{2,3},{3,2},{4,5},{5,4},{6,7},{7,6},{8,9},{9,8},{10,11... | collective-permute-start | bytes 1413128 | tf_op jit(solution)/shard_map/ppermute | solution.py:468
  218.2 8.1 %collective-permute-start.21 = (bf16[2,184,640]{2,1,0:T(8,128)(2,1)S(1)}, bf16[2,184,640]{2,1,0:T(8,128)(2,1)S(1)}, u32[]{:S(2)}, u32[]{:S(2)}) collective-permute-start(bf16[2,184,640]{2,1,0:T(8,128)(2,1)S(1)} %collective-permute-done.13.rest_6_), channel_id=1, source_target_pairs={{0,1},{1,0},{2,3},{3,2},{4,5},{5,4},{6,7},{7,6},{8,9},{9,8},{10,11... | collective-permute-start | bytes 1413128 | tf_op jit(solution)/shard_map/ppermute | solution.py:468
  225.3 1.8 collective-permute-start.22
  225.3 9.6 %collective-permute-start.36 = (bf16[2,360,256]{2,1,0:T(8,128)(2,1)}, bf16[2,360,256]{2,1,0:T(8,128)(2,1)}, u32[]{:S(2)}, u32[]{:S(2)}) collective-permute-start(bf16[2,360,256]{2,1,0:T(8,128)(2,1)} %collective-permute-done.28.rest_4_), channel_id=1, source_target_pairs={{0,1},{1,0},{2,3},{3,2},{4,5},{5,4},{6,7},{7,6},{8,9},{9,8},{10,11... | collective-permute-start | bytes 1105928 | tf_op jit(solution)/shard_map/ppermute | solution.py:468
  225.8 14.5 %collective-permute-start.37 = (bf16[2,360,256]{2,1,0:T(8,128)(2,1)}, bf16[2,360,256]{2,1,0:T(8,128)(2,1)}, u32[]{:S(2)}, u32[]{:S(2)}) collective-permute-start(bf16[2,360,256]{2,1,0:T(8,128)(2,1)} %collective-permute-done.29.rest_5_), channel_id=1, source_target_pairs={{0,1},{1,0},{2,3},{3,2},{4,5},{5,4},{6,7},{7,6},{8,9},{9,8},{10,11... | collective-permute-start | bytes 1105928 | tf_op jit(solution)/shard_map/ppermute | solution.py:468
  225.9 14.4 %collective-permute-start.35 = (bf16[2,360,256]{2,1,0:T(8,128)(2,1)}, bf16[2,360,256]{2,1,0:T(8,128)(2,1)}, u32[]{:S(2)}, u32[]{:S(2)}) collective-permute-start(bf16[2,360,256]{2,1,0:T(8,128)(2,1)} %collective-permute-done.27.rest_3_), channel_id=1, source_target_pairs={{0,1},{1,0},{2,3},{3,2},{4,5},{5,4},{6,7},{7,6},{8,9},{9,8},{10,11... | collective-permute-start | bytes 1105928 | tf_op jit(solution)/shard_map/ppermute | solution.py:468
  226.3 14.0 %collective-permute-start.38 = (bf16[2,360,256]{2,1,0:T(8,128)(2,1)}, bf16[2,360,256]{2,1,0:T(8,128)(2,1)}, u32[]{:S(2)}, u32[]{:S(2)}) collective-permute-start(bf16[2,360,256]{2,1,0:T(8,128)(2,1)} %collective-permute-done.30.rest_6_), channel_id=1, source_target_pairs={{0,1},{1,0},{2,3},{3,2},{4,5},{5,4},{6,7},{7,6},{8,9},{9,8},{10,11... | collective-permute-start | bytes 1105928 | tf_op jit(solution)/shard_map/ppermute | solution.py:468
  227.1 13.2 %collective-permute-start.39 = (bf16[2,360,256]{2,1,0:T(8,128)(2,1)}, bf16[2,360,256]{2,1,0:T(8,128)(2,1)}, u32[]{:S(2)}, u32[]{:S(2)}) collective-permute-start(bf16[2,360,256]{2,1,0:T(8,128)(2,1)} %collective-permute-done.31.rest_7_), channel_id=1, source_target_pairs={{0,1},{1,0},{2,3},{3,2},{4,5},{5,4},{6,7},{7,6},{8,9},{9,8},{10,11... | collective-permute-start | bytes 1105928 | tf_op jit(solution)/shard_map/ppermute | solution.py:468
  234.9 5.4 %collective-permute-start.23 = (bf16[128,512]{1,0:T(8,128)(2,1)S(1)}, bf16[128,512]{1,0:T(8,128)(2,1)S(1)}, u32[]{:S(2)}, u32[]{:S(2)}) collective-permute-start(bf16[128,512]{1,0:T(8,128)(2,1)S(1)} %get-tuple-element.15.pairs_ref), channel_id=1, source_target_pairs={{0,2},{2,4},{4,6},{6,8},{8,10},{10,12},{12,14},{14,1},{1,3},{3,5},... | collective-permute-start | bytes 393224 | tf_op jit(solution)/shard_map/ppermute | solution.py:619
  (16 other events, 299.9 us)

commit v5 on v4

--- a/solution.py
+++ b/solution.py
@@ -62,7 +62,7 @@
     width, tok_count = tokens_t.shape
     return pl.pallas_call(
         prepare_kernel,
-        out_shape=pltpu.HBM((tok_count, width + slot_lanes(width)), BF16),
+        out_shape=jax.ShapeDtypeStruct((tok_count, width + slot_lanes(width)), BF16),
         in_specs=[VMEM] * 3,
         out_specs=VMEM,
         name="prepare",
@@ -103,71 +103,137 @@
     )(tokens_t, routes_t, scale_t)
 
 
+def fetch_kernel(gate_up_ref, down_ref, gate_up_out, down_out, sems):
+    copies = [
+        pltpu.make_async_copy(gate_up_ref.at[0], gate_up_out, sems.at[0]),
+        pltpu.make_async_copy(down_ref.at[0], down_out, sems.at[1]),
+    ]
+    for copy in copies:
+        copy.start()
+    for copy in copies:
+        copy.wait()
+
+
+def fetch_first(gate_up, down_proj):
+    return pl.pallas_call(
+        fetch_kernel,
+        out_shape=(pltpu.VMEM(gate_up.shape[1:], BF16), pltpu.VMEM(down_proj.shape[1:], BF16)),
+        in_specs=[HBM] * 2,
+        out_specs=(VMEM, VMEM),
+        scratch_shapes=[pltpu.SemaphoreType.DMA((2,))],
+        compiler_params=pltpu.CompilerParams(vmem_limit_bytes=4 << 20),
+        name="fetch",
+    )(gate_up, down_proj)
+
+
 def experts_kernel(lines, place_ref, *refs):
     blocks = refs[: 2 * lines]
-    gate_up_ref, down_ref, out_ref, picked, slots, total_ref = refs[2 * lines :]
-    expert, slab = pl.program_id(0), pl.program_id(1)
+    first_up, first_down, gate_up_ref, down_ref, out_ref = refs[2 * lines : 2 * lines + 5]
+    picked, slots, total_ref, ups, downs, results, sems = refs[2 * lines + 5 :]
     experts, _, width = picked.shape
+    per_device = gate_up_ref.shape[0]
+    slabs = per_device // experts
     tok_count, _ = blocks[0].shape
 
-    @pl.when((expert == 0) & (slab == 0))
-    def _():
-        place = shard_of(place_ref, 0, 0, lines) * experts
-        slot = lax.broadcasted_iota(jnp.int32, (CAP, tok_count), 0).astype(F32)
-        for i, block in enumerate(blocks):
-            slots[i] = block[:, width:].astype(F32).T
-            select = [slot == slots[i, pl.ds(place + e, 1), :] for e in range(experts)]
-            select = jnp.where(jnp.concatenate(select, axis=0), 1.0, 0.0).astype(BF16)
-            rows = jnp.dot(select, block[:, :width], preferred_element_type=F32).astype(BF16)
-            for e in range(experts):
-                picked[e, i * CAP : (i + 1) * CAP, :] = rows[e * CAP : (e + 1) * CAP]
-
-    projected = jnp.dot(picked[expert], gate_up_ref[...], preferred_element_type=F32)
-    gate_part = projected[:, :HALF]
-    up_part = projected[:, HALF:]
-    hidden = (gate_part * jax.nn.sigmoid(1.702 * gate_part) * (up_part + 1.0)).astype(BF16)
-    value = jnp.dot(hidden, down_ref[...], preferred_element_type=F32)
-
-    @pl.when(slab == 0)
-    def _():
-        total_ref[...] = value
-
-    @pl.when(slab > 0)
-    def _():
-        total_ref[...] += value
-
-    @pl.when(slab == pl.num_programs(1) - 1)
-    def _():
+    def weights(slab):
+        spot = slab % 2
+        return [
+            pltpu.make_async_copy(gate_up_ref.at[slab], ups.at[spot], sems.at[spot]),
+            pltpu.make_async_copy(down_ref.at[slab], downs.at[spot], sems.at[2 + spot]),
+        ]
+
+    def begin(slab):
+        if slab < per_device:
+            for copy in weights(slab):
+                copy.start()
+
+    begin(1)
+    begin(2)
+    place = shard_of(place_ref, 0, 0, lines) * experts
+    slot = lax.broadcasted_iota(jnp.int32, (CAP, tok_count), 0).astype(F32)
+    for i, block in enumerate(blocks):
+        slots[i] = block[:, width:].astype(F32).T
+        select = [slot == slots[i, pl.ds(place + e, 1), :] for e in range(experts)]
+        select = jnp.where(jnp.concatenate(select, axis=0), 1.0, 0.0).astype(BF16)
+        rows = jnp.dot(select, block[:, :width], preferred_element_type=F32).astype(BF16)
+        for e in range(experts):
+            picked[e, i * CAP : (i + 1) * CAP, :] = rows[e * CAP : (e + 1) * CAP]
+
+    sent_back = []
+    for slab in range(per_device):
+        expert, part = slab // slabs, slab % slabs
+        if slab == 0:
+            gate_up, down = first_up, first_down
+        else:
+            for copy in weights(slab):
+                copy.wait()
+            gate_up, down = ups.at[slab % 2], downs.at[slab % 2]
+        projected = jnp.dot(picked[expert], gate_up[...], preferred_element_type=F32)
+        gate_part = projected[:, :HALF]
+        up_part = projected[:, HALF:]
+        hidden = (gate_part * jax.nn.sigmoid(1.702 * gate_part) * (up_part + 1.0)).astype(BF16)
+        value = jnp.dot(hidden, down[...], preferred_element_type=F32)
+        if slab >= 1:
+            begin(slab + 2)
+        if part < slabs - 1:
+            total_ref[...] = value if part == 0 else total_ref[...] + value
+            continue
+        if part > 0:
+            value += total_ref[...]
         for i in range(2 * lines):
             owner = shard_of(place_ref, i // 2, i % 2, lines)
-            out_ref[owner] = total_ref[i * CAP : (i + 1) * CAP].astype(BF16)
-
-
-def run_experts(place, blocks, gate_up, down_proj):
+            results[expert, owner] = value[i * CAP : (i + 1) * CAP].astype(BF16)
+        copy = pltpu.make_async_copy(results.at[expert], out_ref.at[:, expert], sems.at[4 + expert])
+        copy.start()
+        sent_back.append(copy)
+    for copy in sent_back:
+        copy.wait()
+
+
+def run_experts(place, blocks, first, gate_up, down_proj):
     seq_count = len(blocks)
     tok_count, sent = blocks[0].shape
     per_device, width, gate_width = gate_up.shape
-    slabs = 2
-    experts = per_device // slabs
+    experts = per_device // 2
     return pl.pallas_call(
         functools.partial(experts_kernel, seq_count // 2),
         out_shape=pltpu.HBM((seq_count, experts, CAP, width), BF16),
-        grid=(experts, slabs),
-        in_specs=[SMEM]
-        + [pl.BlockSpec((tok_count, sent), lambda e, k: (0, 0))] * seq_count
-        + [
-            pl.BlockSpec((None, width, gate_width), lambda e, k: (e * slabs + k, 0, 0)),
-            pl.BlockSpec((None, down_proj.shape[1], width), lambda e, k: (e * slabs + k, 0, 0)),
-        ],
-        out_specs=pl.BlockSpec((seq_count, None, CAP, width), lambda e, k: (0, e, 0, 0)),
+        in_specs=[SMEM] + [VMEM] * (seq_count + 2) + [HBM] * 2,
+        out_specs=HBM,
         scratch_shapes=[
             pltpu.VMEM((experts, seq_count * CAP, width), BF16),
             pltpu.VMEM((seq_count, sent - width, tok_count), F32),
             pltpu.VMEM((seq_count * CAP, width), F32),
+            pltpu.VMEM((2, width, gate_width), BF16),
+            pltpu.VMEM((2, down_proj.shape[1], width), BF16),
+            pltpu.VMEM((experts, seq_count, CAP, width), BF16),
+            pltpu.SemaphoreType.DMA((4 + experts,)),
         ],
-        compiler_params=pltpu.CompilerParams(vmem_limit_bytes=40 << 20),
+        compiler_params=pltpu.CompilerParams(vmem_limit_bytes=36 << 20),
         name="experts",
-    )(place, *blocks, *in_hbm([gate_up, down_proj]))
+    )(place, *blocks, *first, gate_up, down_proj)
+
+
+def stack_kernel(*refs):
+    *parts, out_ref, sems = refs
+    copies = []
+    for i, part in enumerate(parts):
+        copy = pltpu.make_async_copy(part, out_ref.at[i], sems.at[i])
+        copy.start()
+        copies.append(copy)
+    for copy in copies:
+        copy.wait()
+
+
+def stacked(parts):
+    return pl.pallas_call(
+        stack_kernel,
+        out_shape=pltpu.HBM((len(parts),) + parts[0].shape, parts[0].dtype),
+        in_specs=[pl.BlockSpec(memory_space=pl.ANY)] * len(parts),
+        out_specs=HBM,
+        scratch_shapes=[pltpu.SemaphoreType.DMA((len(parts),))],
+        compiler_params=pltpu.CompilerParams(vmem_limit_bytes=1 << 20),
+    )(*parts)
 
 
 def in_hbm(parts):
@@ -295,14 +361,12 @@
     kv_width = KEY_VALUE_HEADS * HEAD_SIZE
     query_groups = QUERY_HEADS // KEY_VALUE_HEADS
     span = halo_ref.shape[0]
-    extent = span + tok_count
-    query_pos = lax.broadcasted_iota(jnp.int32, (tok_count, extent), 0) + span
-    key_pos = lax.broadcasted_iota(jnp.int32, (tok_count, extent), 1)
-    distance = query_pos - key_pos
+    query_pos = lax.broadcasted_iota(jnp.int32, (tok_count, span), 0)
+    key_pos = lax.broadcasted_iota(jnp.int32, (tok_count, span), 1)
+    inside = key_pos <= query_pos
     halo_valid = place_ref[0] + place_ref[1] + place_ref[3] > 0
-    first_key = jnp.where(halo_valid, 0, span)
-    allowed = (distance >= 0) & (distance < WINDOW_SPAN) & (key_pos >= first_key)
-    left = lax.broadcasted_iota(jnp.int32, (extent, pair_width), 1) < HEAD_SIZE
+    usable = key_pos < jnp.where(halo_valid, span, 0)
+    left = lax.broadcasted_iota(jnp.int32, (span + tok_count, pair_width), 1) < HEAD_SIZE
     scale = float(HEAD_SIZE) ** (-0.5)
 
     def sides(start, head, factor):
@@ -331,10 +395,14 @@
             probs = []
             for j in range(pairs):
                 piece = scores[j * tok_count : (j + 1) * tok_count]
-                weights = jnp.where(allowed, jnp.exp(piece), 0.0)
+                weights = jnp.exp(jnp.where(inside, piece[:, span:], piece[:, :span]))
+                weights = jnp.where(inside | usable, weights, 0.0)
                 sink = sink_ref[head * query_groups + 2 * j + side]
                 sums = jnp.sum(weights, axis=-1, keepdims=True) + sink
-                probs.append((weights * (1.0 / sums)).astype(BF16))
+                share = weights * (1.0 / sums)
+                ahead = jnp.where(inside, 0.0, share).astype(BF16)
+                own = jnp.where(inside, share, 0.0).astype(BF16)
+                probs.append(jnp.concatenate([ahead, own], axis=1))
             part = jnp.dot(
                 jnp.concatenate(probs, axis=0), values[side], preferred_element_type=F32
             )
@@ -418,7 +486,7 @@
 
 def gather_quarters(mine, lines, last_axis):
     far = far_blocks(mine, lines)
-    even = jnp.stack(far)
+    even = stacked(far)
     odd = flipped(even, 1)
     even_mate, even_across = swapped(even, "seq"), swapped(even, "groups")
     odd_mate, odd_across = swapped(odd, "seq"), swapped(odd, "groups")
@@ -446,10 +514,15 @@
         for value in (even, odd):
             blocks += [value, swapped(value, "seq")]
     mine_qkv, mine_out = own_quarters(qkv_proj, out_proj)
+    gate_up, down_proj, place, mine_qkv, mine_out = lax.optimization_barrier(
+        (gate_up, down_proj, place, mine_qkv, mine_out)
+    )
     qkv_parts = gather_quarters(mine_qkv, lines, "groups")
     out_parts = gather_quarters(mine_out, lines, "seq")
 
-    finished = run_experts(place, in_hbm(blocks[:1]) + blocks[1:], gate_up, down_proj)
+    gate_up, down_proj = in_hbm([gate_up, down_proj])
+    first = [pltpu.with_memory_space_constraint(w, pltpu.VMEM) for w in fetch_first(gate_up, down_proj)]
+    finished = run_experts(place, blocks, first, gate_up, down_proj)
     summed = lax.all_to_all(finished, "seq", split_axis=0, concat_axis=0, tiled=True)
     residual, coarse, fine = returns(tokens_t, routes_t, scale_t)
 

time: 252 us -> 247 us (0.980)
  waiting for transfers between devices: 170 us -> 164 us
    ppermute x32, waiting for transfers between devices: 68.2 us -> 63 us  [swapped(): lax.ppermute(value, axis, [(i, i ^ 1) for i in range(lax.axis_size(axis))])]
    pallas_call x1 -> x4, Pallas kernels: 2.2 us -> 6.79 us  [the longest x1 3.03 us: fetch_first(): pl.pallas_call(fetch_kernel, out_shape=(pltpu.VMEM(gate_up.shape[1:], BF1...]
    pallas_call x1, Pallas kernels: 18.2 us -> 14.7 us  [run_experts(): pl.pallas_call(functools.partial(experts_kernel, seq_count // 2), out_sha...]
  transfers between devices with their start and end apart: 41 -> 41, of which waited for: 17 -> 16; matrix products, arithmetic and copies ran while one was open for 0% -> 0% of each run, Pallas kernels for 4% -> 6%
where the time goes in v5:
time: 247 us; the launch traced here: 245 us
  waiting for transfers between devices  164 us (66%)
  Pallas kernels  40.2 us (16%)
  starting transfers between devices  38.3 us (16%)
    ppermute x7, waiting for transfers between devices, flipped(): return lax.ppermute(value, 'seq', [(i, i ^ bit * 2) for i in range(count)])  101 us
    ppermute x32, waiting for transfers between devices, swapped(): lax.ppermute(value, axis, [(i, i ^ 1) for i in range(lax.axis_size(axis))])  63 us
    ppermute x32, starting transfers between devices, swapped(): lax.ppermute(value, axis, [(i, i ^ 1) for i in range(lax.axis_size(axis))])  19.3 us
    pallas_call x1, Pallas kernels, run_experts(): pl.pallas_call(functools.partial(experts_kernel, seq_count // 2), out_sha...  14.7 us
    ppermute x7, starting transfers between devices, flipped(): return lax.ppermute(value, 'seq', [(i, i ^ bit * 2) for i in range(count)])  11.1 us
    pallas_call x1, Pallas kernels, attend_and_project(): pl.pallas_call(attention_kernel, out_shape=jax.ShapeDtypeStruct((width, t...  8.1 us
    pallas_call x1, Pallas kernels, project_pairs(): pl.pallas_call(functools.partial(pairs_kernel, rows), out_shape=(jax.Shap...  5.57 us
    all_to_all x1, starting transfers between devices, fused_body(): lax.all_to_all(finished, 'seq', split_axis=0, concat_axis=0, tiled=True)  5.52 us
  transfers between devices with their start and end apart: 41, of which 16 were waited for; matrix products, arithmetic and copies ran while one was open for 0% of the time, Pallas kernels for 6%

profile of v5, /device:TPU:0, one launch (start us, length us, event | category | flops | bytes accessed | tf_op | source)
XLA Modules:
  0.0 244.6 jit_solution(3846762369924323053)
XLA Ops:
  0.0 2.2 prepare.1.refs_0_
  2.2 4.1 %collective-permute-start.3 = (bf16[128,1536]{1,0:T(8,128)(2,1)}, bf16[128,1536]{1,0:T(8,128)(2,1)S(1)}, u32[]{:S(2)}, u32[]{:S(2)}) collective-permute-start(bf16[128,1536]{1,0:T(8,128)(2,1)} %prepare.1.refs_0_), channel_id=1, source_target_pairs={{0,8},{2,10},{4,12},{6,14},{8,0},{10,2},{12,4},{14,6},{1,9},{3,11}... | collective-permute-start | bytes 1179656 | tf_op jit(solution)/shard_map/ppermute | solution.py:474
  6.3 1.6 collective-permute-start.1
  7.8 16.3 %collective-permute-done.3.refs_4_ = bf16[128,1536]{1,0:T(8,128)(2,1)S(1)} collective-permute-done((bf16[128,1536]{1,0:T(8,128)(2,1)}, bf16[128,1536]{1,0:T(8,128)(2,1)S(1)}, u32[]{:S(2)}, u32[]{:S(2)}) %collective-permute-start.3) | collective-permute-done | bytes 393248 | tf_op jit(solution)/shard_map/ppermute | solution.py:474
  24.1 0.7 collective-permute-start.5
  24.8 1.5 collective-permute-start
  26.4 0.6 collective-permute-start.4
  26.9 1.5 collective-permute-start.2
  28.5 5.9 %collective-permute-done.5.refs_6_ = bf16[128,1536]{1,0:T(8,128)(2,1)S(1)} collective-permute-done((bf16[128,1536]{1,0:T(8,128)(2,1)S(1)}, bf16[128,1536]{1,0:T(8,128)(2,1)S(1)}, u32[]{:S(2)}, u32[]{:S(2)}) %collective-permute-start.5) | collective-permute-done | bytes 393248 | tf_op jit(solution)/shard_map/ppermute | solution.py:474
  34.3 1.3 collective-permute-start.6
  35.7 0.9 dynamic-slice_bitcast_fusion.refs_0_
  36.7 3.0 %fetch.1 = (bf16[1440,1440]{1,0:T(8,128)(2,1)S(1)}, bf16[720,1440]{1,0:T(8,128)(2,1)S(1)}) custom-call(bf16[4,1440,1440]{2,1,0:T(8,128)(2,1)} %refs_10_, bf16[4,720,1440]{2,1,0:T(8,128)(2,1)} %refs_11_), custom_call_target="tpu_custom_call" | custom-call | tf_op jit(solution)/shard_map/fetch/pallas_call | solution.py:118
  39.8 5.7 %collective-permute-done.4.refs_5_ = bf16[128,1536]{1,0:T(8,128)(2,1)S(1)} collective-permute-done((bf16[128,1536]{1,0:T(8,128)(2,1)S(1)}, bf16[128,1536]{1,0:T(8,128)(2,1)S(1)}, u32[]{:S(2)}, u32[]{:S(2)}) %collective-permute-start.4) | collective-permute-done | bytes 393248 | tf_op jit(solution)/shard_map/ppermute | solution.py:541
  45.5 8.5 %collective-permute-done.2.refs_3_ = bf16[128,1536]{1,0:T(8,128)(2,1)} collective-permute-done((bf16[128,1536]{1,0:T(8,128)(2,1)S(1)}, bf16[128,1536]{1,0:T(8,128)(2,1)}, u32[]{:S(2)}, u32[]{:S(2)}) %collective-permute-start.2) | collective-permute-done | bytes 393248 | tf_op jit(solution)/shard_map/ppermute | solution.py:541
  54.0 7.2 %collective-permute-done.6.refs_7_ = bf16[128,1536]{1,0:T(8,128)(2,1)} collective-permute-done((bf16[128,1536]{1,0:T(8,128)(2,1)S(1)}, bf16[128,1536]{1,0:T(8,128)(2,1)}, u32[]{:S(2)}, u32[]{:S(2)}) %collective-permute-start.6) | collective-permute-done | bytes 393248 | tf_op jit(solution)/shard_map/ppermute | solution.py:541
  61.2 14.7 %experts.1 = bf16[8,2,48,1440]{3,2,1,0:T(8,128)(2,1)} custom-call(s32[4]{0:T(128)S(1)} %pad_add_fusion.place_ref, bf16[128,1536]{1,0:T(8,128)(2,1)S(1)} %copy-done.1, bf16[128,1536]{1,0:T(8,128)(2,1)S(1)} %collective-permute-done.refs_1_, bf16[128,1536]{1,0:T(8,128)(2,1)S(1)} %collective-permute-done.1.refs_2_, ...), custom_call_target="tpu_custom_call" | custom-call | tf_op jit(solution)/shard_map/experts/pallas_call | solution.py:198
  75.9 5.5 %all-to-all-start = ((bf16[8,2,48,1440]{3,2,1,0:T(8,128)(2,1)}), bf16[8,2,48,1440]{3,2,1,0:T(8,128)(2,1)}, u32[]{:S(2)}, u32[]{:S(2)}) async-start(bf16[8,2,48,1440]{3,2,1,0:T(8,128)(2,1)} %experts.1), calls=%async_computation | async-start | bytes 4718592 | tf_op jit(solution)/shard_map/all_to_all | solution.py:526
  81.4 2.9 %collective-permute-start.24 = (bf16[360,256]{1,0:T(8,128)(2,1)S(1)}, bf16[360,256]{1,0:T(8,128)(2,1)S(1)}, u32[]{:S(2)}, u32[]{:S(2)}) collective-permute-start(bf16[360,256]{1,0:T(8,128)(2,1)S(1)} %dynamic-slice_bitcast_fusion.refs_0_), channel_id=1, source_target_pairs={{0,8},{2,10},{4,12},{6,14},{8,0},{10,2},{12,4},{14,6},{1,9},{3,11}... | collective-permute-start | bytes 552968 | tf_op jit(solution)/shard_map/ppermute | solution.py:474
  84.3 65.3 %collective-permute-done.24.refs_1_ = bf16[360,256]{1,0:T(8,128)(2,1)S(1)} collective-permute-done((bf16[360,256]{1,0:T(8,128)(2,1)S(1)}, bf16[360,256]{1,0:T(8,128)(2,1)S(1)}, u32[]{:S(2)}, u32[]{:S(2)}) %collective-permute-start.24) | collective-permute-done | bytes 184352 | tf_op jit(solution)/shard_map/ppermute | solution.py:474
  149.6 0.8 shard_map.101.rest_0_
  150.6 1.5 collective-permute-start.28
  152.4 0.8 shard_map.100.rest_0_
  153.2 1.7 collective-permute-start.8
  154.9 7.2 %collective-permute-done.25.rest_1_ = bf16[2,360,256]{2,1,0:T(8,128)(2,1)S(1)} collective-permute-done((bf16[2,360,256]{2,1,0:T(8,128)(2,1)}, bf16[2,360,256]{2,1,0:T(8,128)(2,1)S(1)}, u32[]{:S(2)}, u32[]{:S(2)}) %collective-permute-start.25) | collective-permute-done | bytes 368672 | tf_op jit(solution)/shard_map/ppermute | solution.py:474
  162.2 1.5 collective-permute-start.11
  163.8 0.6 collective-permute-start.29
  164.4 5.9 %collective-permute-done.8.rest_1_ = bf16[2,184,640]{2,1,0:T(8,128)(2,1)S(1)} collective-permute-done((bf16[2,184,640]{2,1,0:T(8,128)(2,1)}, bf16[2,184,640]{2,1,0:T(8,128)(2,1)S(1)}, u32[]{:S(2)}, u32[]{:S(2)}) %collective-permute-start.8) | collective-permute-done | bytes 471072 | tf_op jit(solution)/shard_map/ppermute | solution.py:474
  170.3 1.5 collective-permute-start.27
  171.7 0.8 collective-permute-done.9.rest_2_
  172.6 1.7 collective-permute-start.10
  174.3 1.8 collective-permute-done.11.rest_4_
  176.1 1.5 collective-permute-start.12
  177.6 0.5 collective-permute-start.30
  178.1 6.0 %collective-permute-done.29.rest_5_ = bf16[2,360,256]{2,1,0:T(8,128)(2,1)} collective-permute-done((bf16[2,360,256]{2,1,0:T(8,128)(2,1)S(1)}, bf16[2,360,256]{2,1,0:T(8,128)(2,1)}, u32[]{:S(2)}, u32[]{:S(2)}) %collective-permute-start.29) | collective-permute-done | bytes 368672 | tf_op jit(solution)/shard_map/ppermute | solution.py:541
  184.1 0.5 collective-permute-start.34
  184.6 15.2 %collective-permute-done.30.rest_6_ = bf16[2,360,256]{2,1,0:T(8,128)(2,1)} collective-permute-done((bf16[2,360,256]{2,1,0:T(8,128)(2,1)S(1)}, bf16[2,360,256]{2,1,0:T(8,128)(2,1)}, u32[]{:S(2)}, u32[]{:S(2)}) %collective-permute-start.30) | collective-permute-done | bytes 368672 | tf_op jit(solution)/shard_map/ppermute | solution.py:541
  199.8 1.5 collective-permute-start.13
  201.3 0.5 collective-permute-start.17
  201.9 0.5 collective-permute-start.14
  202.5 11.0 %collective-permute-done.13.rest_6_ = bf16[2,184,640]{2,1,0:T(8,128)(2,1)S(1)} collective-permute-done((bf16[2,184,640]{2,1,0:T(8,128)(2,1)S(1)}, bf16[2,184,640]{2,1,0:T(8,128)(2,1)S(1)}, u32[]{:S(2)}, u32[]{:S(2)}) %collective-permute-start.13) | collective-permute-done | bytes 471072 | tf_op jit(solution)/shard_map/ppermute | solution.py:541
  214.6 5.8 %collective-permute-done.14.rest_7_ = bf16[2,184,640]{2,1,0:T(8,128)(2,1)S(1)} collective-permute-done((bf16[2,184,640]{2,1,0:T(8,128)(2,1)S(1)}, bf16[2,184,640]{2,1,0:T(8,128)(2,1)S(1)}, u32[]{:S(2)}, u32[]{:S(2)}) %collective-permute-start.14) | collective-permute-done | bytes 471072 | tf_op jit(solution)/shard_map/ppermute | solution.py:541
  220.4 0.9 collective-permute-done.31.rest_7_
  221.3 0.5 collective-permute-start.37
  223.2 1.3 returns.1
  224.5 5.6 %pairs.1 = (bf16[128,512]{1,0:T(8,128)(2,1)S(1)}, bf16[8,128,184]{2,1,0:T(8,128)(2,1)S(1)}, bf16[1440,128]{1,0:T(8,128)(2,1)S(1)}) custom-call(s32[4]{0:T(128)S(1)} %pad_add_fusion.place_ref, bf16[768,1440]{1,0:T(8,128)(2,1)} %bitcast.9.tables_ref, bf16[128,1440]{1,0:T(8,128)(2,1)S(1)} %get-tuple-element.23.residual_ref, ...), custom_call_target="tpu_custom_call" | custom-call | tf_op jit(solution)/shard_map/pairs/pallas_call | solution.py:312
  230.1 2.4 collective-permute-start.23
  232.5 3.8 %queries.1.packed_ref = bf16[128,2048]{1,0:T(8,128)(2,1)S(1)} custom-call(s32[4]{0:T(128)S(1)} %pad_add_fusion.place_ref, bf16[8,128,184]{2,1,0:T(8,128)(2,1)S(1)} %get-tuple-element.27.slices, bf16[2,184,640]{2,1,0:T(8,128)(2,1)} %shard_map.100.rest_0_, bf16[2,184,640]{2,1,0:T(8,128)(2,1)} %copy-done.3, bf16[2,184,640]{2,1,0:T(8,128)(2,1)} %copy-done.4, ...), custom_call_target="tpu_custom_call" | custom-call | tf_op jit(solution)/shard_map/queries/pallas_call | solution.py:339
  236.4 8.1 %attention.1 = bf16[1440,128]{1,0:T(8,128)(2,1)} custom-call(s32[4]{0:T(128)S(1)} %pad_add_fusion.place_ref, f32[32]{0:T(128)S(1)} %exp.3.sink_ref, bf16[128,2048]{1,0:T(8,128)(2,1)S(1)} %queries.1.packed_ref, bf16[128,512]{1,0:T(8,128)(2,1)S(1)} %get-tuple-element.28.pairs_ref, bf16[128,512]{1,0:T(8,128)(2,1)S(1)} %collective-permute-done.23.halo_ref, ...), custom_call_target="tpu_custom_call" | custom-call | tf_op jit(solution)/shard_map/attention/pallas_call | solution.py:437
  (93 shorter events, 3.2 us)
Async XLA Ops:
  2.2 21.9 %collective-permute-start.3 = (bf16[128,1536]{1,0:T(8,128)(2,1)}, bf16[128,1536]{1,0:T(8,128)(2,1)S(1)}, u32[]{:S(2)}, u32[]{:S(2)}) collective-permute-start(bf16[128,1536]{1,0:T(8,128)(2,1)} %prepare.1.refs_0_), channel_id=1, source_target_pairs={{0,8},{2,10},{4,12},{6,14},{8,0},{10,2},{12,4},{14,6},{1,9},{3,11}... | collective-permute-start | bytes 1179656 | tf_op jit(solution)/shard_map/ppermute | solution.py:474
  6.3 20.7 %collective-permute-start.1 = (bf16[128,1536]{1,0:T(8,128)(2,1)}, bf16[128,1536]{1,0:T(8,128)(2,1)S(1)}, u32[]{:S(2)}, u32[]{:S(2)}) collective-permute-start(bf16[128,1536]{1,0:T(8,128)(2,1)} %prepare.1.refs_0_), channel_id=1, source_target_pairs={{0,4},{2,6},{4,0},{6,2},{8,12},{10,14},{12,8},{14,10},{1,5},{3,7},... | collective-permute-start | bytes 1179656 | tf_op jit(solution)/shard_map/ppermute | solution.py:474
  24.1 10.2 %collective-permute-start.5 = (bf16[128,1536]{1,0:T(8,128)(2,1)S(1)}, bf16[128,1536]{1,0:T(8,128)(2,1)S(1)}, u32[]{:S(2)}, u32[]{:S(2)}) collective-permute-start(bf16[128,1536]{1,0:T(8,128)(2,1)S(1)} %collective-permute-done.3.refs_4_), channel_id=1, source_target_pairs={{0,4},{2,6},{4,0},{6,2},{8,12},{10,14},{12,8},{14,10},{1,5},{3,7},... | collective-permute-start | bytes 1179656 | tf_op jit(solution)/shard_map/ppermute | solution.py:474
  24.8 14.9 %collective-permute-start = (bf16[128,1536]{1,0:T(8,128)(2,1)}, bf16[128,1536]{1,0:T(8,128)(2,1)S(1)}, u32[]{:S(2)}, u32[]{:S(2)}) collective-permute-start(bf16[128,1536]{1,0:T(8,128)(2,1)} %prepare.1.refs_0_), channel_id=1, source_target_pairs={{0,2},{2,0},{4,6},{6,4},{8,10},{10,8},{12,14},{14,12},{1,3},{3,1},... | collective-permute-start | bytes 1179656 | tf_op jit(solution)/shard_map/ppermute | solution.py:541
  26.4 19.1 %collective-permute-start.4 = (bf16[128,1536]{1,0:T(8,128)(2,1)S(1)}, bf16[128,1536]{1,0:T(8,128)(2,1)S(1)}, u32[]{:S(2)}, u32[]{:S(2)}) collective-permute-start(bf16[128,1536]{1,0:T(8,128)(2,1)S(1)} %collective-permute-done.3.refs_4_), channel_id=1, source_target_pairs={{0,2},{2,0},{4,6},{6,4},{8,10},{10,8},{12,14},{14,12},{1,3},{3,1},... | collective-permute-start | bytes 1179656 | tf_op jit(solution)/shard_map/ppermute | solution.py:541
  26.9 27.0 %collective-permute-start.2 = (bf16[128,1536]{1,0:T(8,128)(2,1)S(1)}, bf16[128,1536]{1,0:T(8,128)(2,1)}, u32[]{:S(2)}, u32[]{:S(2)}) collective-permute-start(bf16[128,1536]{1,0:T(8,128)(2,1)S(1)} %collective-permute-done.1.refs_2_), channel_id=1, source_target_pairs={{0,2},{2,0},{4,6},{6,4},{8,10},{10,8},{12,14},{14,12},{1,3},{3,1},... | collective-permute-start | bytes 1179656 | tf_op jit(solution)/shard_map/ppermute | solution.py:541
  34.3 26.9 %collective-permute-start.6 = (bf16[128,1536]{1,0:T(8,128)(2,1)S(1)}, bf16[128,1536]{1,0:T(8,128)(2,1)}, u32[]{:S(2)}, u32[]{:S(2)}) collective-permute-start(bf16[128,1536]{1,0:T(8,128)(2,1)S(1)} %collective-permute-done.5.refs_6_), channel_id=1, source_target_pairs={{0,2},{2,0},{4,6},{6,4},{8,10},{10,8},{12,14},{14,12},{1,3},{3,1},... | collective-permute-start | bytes 1179656 | tf_op jit(solution)/shard_map/ppermute | solution.py:541
  75.9 148.7 %copy-start.2 = (f32[1440]{0:T(1024)S(1)}, f32[1440]{0:T(1024)}, u32[]{:S(2)}) copy-start(f32[1440]{0:T(1024)} %gain_ref.3) | copy-start | bytes 17284
  75.9 148.6 %all-to-all-start = ((bf16[8,2,48,1440]{3,2,1,0:T(8,128)(2,1)}), bf16[8,2,48,1440]{3,2,1,0:T(8,128)(2,1)}, u32[]{:S(2)}, u32[]{:S(2)}) async-start(bf16[8,2,48,1440]{3,2,1,0:T(8,128)(2,1)} %experts.1), calls=%async_computation | async-start | bytes 4718592 | tf_op jit(solution)/shard_map/all_to_all | solution.py:526
  81.4 68.3 %collective-permute-start.24 = (bf16[360,256]{1,0:T(8,128)(2,1)S(1)}, bf16[360,256]{1,0:T(8,128)(2,1)S(1)}, u32[]{:S(2)}, u32[]{:S(2)}) collective-permute-start(bf16[360,256]{1,0:T(8,128)(2,1)S(1)} %dynamic-slice_bitcast_fusion.refs_0_), channel_id=1, source_target_pairs={{0,8},{2,10},{4,12},{6,14},{8,0},{10,2},{12,4},{14,6},{1,9},{3,11}... | collective-permute-start | bytes 552968 | tf_op jit(solution)/shard_map/ppermute | solution.py:474
  84.3 68.1 %collective-permute-start.7 = (bf16[184,640]{1,0:T(8,128)(2,1)S(1)}, bf16[184,640]{1,0:T(8,128)(2,1)S(1)}, u32[]{:S(2)}, u32[]{:S(2)}) collective-permute-start(bf16[184,640]{1,0:T(8,128)(2,1)S(1)} %fusion.2.refs_0_), channel_id=1, source_target_pairs={{0,8},{2,10},{4,12},{6,14},{8,0},{10,2},{12,4},{14,6},{1,9},{3,11}... | collective-permute-start | bytes 706568 | tf_op jit(solution)/shard_map/ppermute | solution.py:474
  150.4 11.7 %collective-permute-start.25 = (bf16[2,360,256]{2,1,0:T(8,128)(2,1)}, bf16[2,360,256]{2,1,0:T(8,128)(2,1)S(1)}, u32[]{:S(2)}, u32[]{:S(2)}) collective-permute-start(bf16[2,360,256]{2,1,0:T(8,128)(2,1)} %shard_map.101.rest_0_), channel_id=1, source_target_pairs={{0,4},{2,6},{4,0},{6,2},{8,12},{10,14},{12,8},{14,10},{1,5},{3,7},... | collective-permute-start | bytes 1105928 | tf_op jit(solution)/shard_map/ppermute | solution.py:474
  150.5 11.7 %collective-permute-start.26 = (bf16[2,360,256]{2,1,0:T(8,128)(2,1)}, bf16[2,360,256]{2,1,0:T(8,128)(2,1)S(1)}, u32[]{:S(2)}, u32[]{:S(2)}) collective-permute-start(bf16[2,360,256]{2,1,0:T(8,128)(2,1)} %shard_map.101.rest_0_), channel_id=1, source_target_pairs={{0,2},{2,0},{4,6},{6,4},{8,10},{10,8},{12,14},{14,12},{1,3},{3,1},... | collective-permute-start | bytes 1105928 | tf_op jit(solution)/shard_map/ppermute | solution.py:541
  150.6 13.1 %collective-permute-start.28 = (bf16[2,360,256]{2,1,0:T(8,128)(2,1)}, bf16[2,360,256]{2,1,0:T(8,128)(2,1)}, u32[]{:S(2)}, u32[]{:S(2)}) collective-permute-start(bf16[2,360,256]{2,1,0:T(8,128)(2,1)} %shard_map.101.rest_0_), channel_id=1, source_target_pairs={{0,16},{16,0},{1,17},{17,1},{2,18},{18,2},{3,19},{19,3},{4,20},{20... | collective-permute-start | bytes 1105928 | tf_op jit(solution)/shard_map/ppermute | solution.py:541
  153.2 17.1 %collective-permute-start.8 = (bf16[2,184,640]{2,1,0:T(8,128)(2,1)}, bf16[2,184,640]{2,1,0:T(8,128)(2,1)S(1)}, u32[]{:S(2)}, u32[]{:S(2)}) collective-permute-start(bf16[2,184,640]{2,1,0:T(8,128)(2,1)} %shard_map.100.rest_0_), channel_id=1, source_target_pairs={{0,4},{2,6},{4,0},{6,2},{8,12},{10,14},{12,8},{14,10},{1,5},{3,7},... | collective-permute-start | bytes 1413128 | tf_op jit(solution)/shard_map/ppermute | solution.py:474
  154.9 8.8 %collective-permute-start.32 = (bf16[2,360,256]{2,1,0:T(8,128)(2,1)}, bf16[2,360,256]{2,1,0:T(8,128)(2,1)S(1)}, u32[]{:S(2)}, u32[]{:S(2)}) collective-permute-start(bf16[2,360,256]{2,1,0:T(8,128)(2,1)} %shard_map.101.rest_0_), channel_id=1, source_target_pairs={{0,1},{1,0},{2,3},{3,2},{4,5},{5,4},{6,7},{7,6},{8,9},{9,8},{10,11... | collective-permute-start | bytes 1105928 | tf_op jit(solution)/shard_map/ppermute | solution.py:541
  162.2 74.2 %copy-start.18 = (bf16[2,360,256]{2,1,0:T(8,128)(2,1)}, bf16[2,360,256]{2,1,0:T(8,128)(2,1)S(1)}, u32[]{:S(2)}) copy-start(bf16[2,360,256]{2,1,0:T(8,128)(2,1)S(1)} %collective-permute-done.25.rest_1_) | copy-start | bytes 1105924
  162.2 10.4 %collective-permute-start.9 = (bf16[2,184,640]{2,1,0:T(8,128)(2,1)}, bf16[2,184,640]{2,1,0:T(8,128)(2,1)S(1)}, u32[]{:S(2)}, u32[]{:S(2)}) collective-permute-start(bf16[2,184,640]{2,1,0:T(8,128)(2,1)} %shard_map.100.rest_0_), channel_id=1, source_target_pairs={{0,2},{2,0},{4,6},{6,4},{8,10},{10,8},{12,14},{14,12},{1,3},{3,1},... | collective-permute-start | bytes 1413128 | tf_op jit(solution)/shard_map/ppermute | solution.py:541
  162.2 60.2 %copy-start.19 = (bf16[2,360,256]{2,1,0:T(8,128)(2,1)}, bf16[2,360,256]{2,1,0:T(8,128)(2,1)S(1)}, u32[]{:S(2)}) copy-start(bf16[2,360,256]{2,1,0:T(8,128)(2,1)S(1)} %collective-permute-done.26.rest_2_) | copy-start | bytes 1105924
  162.2 13.9 %collective-permute-start.11 = (bf16[2,184,640]{2,1,0:T(8,128)(2,1)}, bf16[2,184,640]{2,1,0:T(8,128)(2,1)S(1)}, u32[]{:S(2)}, u32[]{:S(2)}) collective-permute-start(bf16[2,184,640]{2,1,0:T(8,128)(2,1)} %shard_map.100.rest_0_), channel_id=1, source_target_pairs={{0,16},{16,0},{1,17},{17,1},{2,18},{18,2},{3,19},{19,3},{4,20},{20... | collective-permute-start | bytes 1413128 | tf_op jit(solution)/shard_map/ppermute | solution.py:541
  163.7 13.9 %collective-permute-start.15 = (bf16[2,184,640]{2,1,0:T(8,128)(2,1)}, bf16[2,184,640]{2,1,0:T(8,128)(2,1)S(1)}, u32[]{:S(2)}, u32[]{:S(2)}) collective-permute-start(bf16[2,184,640]{2,1,0:T(8,128)(2,1)} %shard_map.100.rest_0_), channel_id=1, source_target_pairs={{0,1},{1,0},{2,3},{3,2},{4,5},{5,4},{6,7},{7,6},{8,9},{9,8},{10,11... | collective-permute-start | bytes 1413128 | tf_op jit(solution)/shard_map/ppermute | solution.py:541
  163.7 58.7 %copy-start.20 = (bf16[2,360,256]{2,1,0:T(8,128)(2,1)}, bf16[2,360,256]{2,1,0:T(8,128)(2,1)S(1)}, u32[]{:S(2)}) copy-start(bf16[2,360,256]{2,1,0:T(8,128)(2,1)S(1)} %collective-permute-done.32.rest_8_) | copy-start | bytes 1105924
  163.8 20.4 %collective-permute-start.29 = (bf16[2,360,256]{2,1,0:T(8,128)(2,1)S(1)}, bf16[2,360,256]{2,1,0:T(8,128)(2,1)}, u32[]{:S(2)}, u32[]{:S(2)}) collective-permute-start(bf16[2,360,256]{2,1,0:T(8,128)(2,1)S(1)} %collective-permute-done.25.rest_1_), channel_id=1, source_target_pairs={{0,16},{16,0},{1,17},{17,1},{2,18},{18,2},{3,19},{19,3},{4,20},{20... | collective-permute-start | bytes 1105928 | tf_op jit(solution)/shard_map/ppermute | solution.py:541
  170.3 54.2 %copy-start.3 = (bf16[2,184,640]{2,1,0:T(8,128)(2,1)}, bf16[2,184,640]{2,1,0:T(8,128)(2,1)S(1)}, u32[]{:S(2)}) copy-start(bf16[2,184,640]{2,1,0:T(8,128)(2,1)S(1)} %collective-permute-done.8.rest_1_) | copy-start | bytes 1413124
  170.3 13.8 %collective-permute-start.27 = (bf16[2,360,256]{2,1,0:T(8,128)(2,1)S(1)}, bf16[2,360,256]{2,1,0:T(8,128)(2,1)}, u32[]{:S(2)}, u32[]{:S(2)}) collective-permute-start(bf16[2,360,256]{2,1,0:T(8,128)(2,1)S(1)} %collective-permute-done.25.rest_1_), channel_id=1, source_target_pairs={{0,2},{2,0},{4,6},{6,4},{8,10},{10,8},{12,14},{14,12},{1,3},{3,1},... | collective-permute-start | bytes 1105928 | tf_op jit(solution)/shard_map/ppermute | solution.py:541
  172.5 51.9 %copy-start.4 = (bf16[2,184,640]{2,1,0:T(8,128)(2,1)}, bf16[2,184,640]{2,1,0:T(8,128)(2,1)S(1)}, u32[]{:S(2)}) copy-start(bf16[2,184,640]{2,1,0:T(8,128)(2,1)S(1)} %collective-permute-done.9.rest_2_) | copy-start | bytes 1413124
  172.6 29.3 %collective-permute-start.10 = (bf16[2,184,640]{2,1,0:T(8,128)(2,1)S(1)}, bf16[2,184,640]{2,1,0:T(8,128)(2,1)S(1)}, u32[]{:S(2)}, u32[]{:S(2)}) collective-permute-start(bf16[2,184,640]{2,1,0:T(8,128)(2,1)S(1)} %collective-permute-done.8.rest_1_), channel_id=1, source_target_pairs={{0,2},{2,0},{4,6},{6,4},{8,10},{10,8},{12,14},{14,12},{1,3},{3,1},... | collective-permute-start | bytes 1413128 | tf_op jit(solution)/shard_map/ppermute | solution.py:541
  176.1 48.4 %copy-start.5 = (bf16[2,184,640]{2,1,0:T(8,128)(2,1)}, bf16[2,184,640]{2,1,0:T(8,128)(2,1)S(1)}, u32[]{:S(2)}) copy-start(bf16[2,184,640]{2,1,0:T(8,128)(2,1)S(1)} %collective-permute-done.11.rest_4_) | copy-start | bytes 1413124
  176.1 25.8 %collective-permute-start.12 = (bf16[2,184,640]{2,1,0:T(8,128)(2,1)S(1)}, bf16[2,184,640]{2,1,0:T(8,128)(2,1)S(1)}, u32[]{:S(2)}, u32[]{:S(2)}) collective-permute-start(bf16[2,184,640]{2,1,0:T(8,128)(2,1)S(1)} %collective-permute-done.8.rest_1_), channel_id=1, source_target_pairs={{0,16},{16,0},{1,17},{17,1},{2,18},{18,2},{3,19},{19,3},{4,20},{20... | collective-permute-start | bytes 1413128 | tf_op jit(solution)/shard_map/ppermute | solution.py:541
  177.6 22.2 %collective-permute-start.30 = (bf16[2,360,256]{2,1,0:T(8,128)(2,1)S(1)}, bf16[2,360,256]{2,1,0:T(8,128)(2,1)}, u32[]{:S(2)}, u32[]{:S(2)}) collective-permute-start(bf16[2,360,256]{2,1,0:T(8,128)(2,1)S(1)} %collective-permute-done.26.rest_2_), channel_id=1, source_target_pairs={{0,16},{16,0},{1,17},{17,1},{2,18},{18,2},{3,19},{19,3},{4,20},{20... | collective-permute-start | bytes 1105928 | tf_op jit(solution)/shard_map/ppermute | solution.py:541
  184.1 17.2 %collective-permute-start.33 = (bf16[2,360,256]{2,1,0:T(8,128)(2,1)S(1)}, bf16[2,360,256]{2,1,0:T(8,128)(2,1)}, u32[]{:S(2)}, u32[]{:S(2)}) collective-permute-start(bf16[2,360,256]{2,1,0:T(8,128)(2,1)S(1)} %collective-permute-done.25.rest_1_), channel_id=1, source_target_pairs={{0,1},{1,0},{2,3},{3,2},{4,5},{5,4},{6,7},{7,6},{8,9},{9,8},{10,11... | collective-permute-start | bytes 1105928 | tf_op jit(solution)/shard_map/ppermute | solution.py:541
  184.1 17.2 %collective-permute-start.34 = (bf16[2,360,256]{2,1,0:T(8,128)(2,1)S(1)}, bf16[2,360,256]{2,1,0:T(8,128)(2,1)}, u32[]{:S(2)}, u32[]{:S(2)}) collective-permute-start(bf16[2,360,256]{2,1,0:T(8,128)(2,1)S(1)} %collective-permute-done.26.rest_2_), channel_id=1, source_target_pairs={{0,1},{1,0},{2,3},{3,2},{4,5},{5,4},{6,7},{7,6},{8,9},{9,8},{10,11... | collective-permute-start | bytes 1105928 | tf_op jit(solution)/shard_map/ppermute | solution.py:541
  199.8 13.7 %collective-permute-start.13 = (bf16[2,184,640]{2,1,0:T(8,128)(2,1)S(1)}, bf16[2,184,640]{2,1,0:T(8,128)(2,1)S(1)}, u32[]{:S(2)}, u32[]{:S(2)}) collective-permute-start(bf16[2,184,640]{2,1,0:T(8,128)(2,1)S(1)} %collective-permute-done.9.rest_2_), channel_id=1, source_target_pairs={{0,16},{16,0},{1,17},{17,1},{2,18},{18,2},{3,19},{19,3},{4,20},{20... | collective-permute-start | bytes 1413128 | tf_op jit(solution)/shard_map/ppermute | solution.py:541
  201.3 12.6 %collective-permute-start.16 = (bf16[2,184,640]{2,1,0:T(8,128)(2,1)S(1)}, bf16[2,184,640]{2,1,0:T(8,128)(2,1)S(1)}, u32[]{:S(2)}, u32[]{:S(2)}) collective-permute-start(bf16[2,184,640]{2,1,0:T(8,128)(2,1)S(1)} %collective-permute-done.8.rest_1_), channel_id=1, source_target_pairs={{0,1},{1,0},{2,3},{3,2},{4,5},{5,4},{6,7},{7,6},{8,9},{9,8},{10,11... | collective-permute-start | bytes 1413128 | tf_op jit(solution)/shard_map/ppermute | solution.py:541
  201.3 12.6 %collective-permute-start.17 = (bf16[2,184,640]{2,1,0:T(8,128)(2,1)S(1)}, bf16[2,184,640]{2,1,0:T(8,128)(2,1)S(1)}, u32[]{:S(2)}, u32[]{:S(2)}) collective-permute-start(bf16[2,184,640]{2,1,0:T(8,128)(2,1)S(1)} %collective-permute-done.9.rest_2_), channel_id=1, source_target_pairs={{0,1},{1,0},{2,3},{3,2},{4,5},{5,4},{6,7},{7,6},{8,9},{9,8},{10,11... | collective-permute-start | bytes 1413128 | tf_op jit(solution)/shard_map/ppermute | solution.py:541
  201.8 12.6 %collective-permute-start.19 = (bf16[2,184,640]{2,1,0:T(8,128)(2,1)S(1)}, bf16[2,184,640]{2,1,0:T(8,128)(2,1)S(1)}, u32[]{:S(2)}, u32[]{:S(2)}) collective-permute-start(bf16[2,184,640]{2,1,0:T(8,128)(2,1)S(1)} %collective-permute-done.11.rest_4_), channel_id=1, source_target_pairs={{0,1},{1,0},{2,3},{3,2},{4,5},{5,4},{6,7},{7,6},{8,9},{9,8},{10,11... | collective-permute-start | bytes 1413128 | tf_op jit(solution)/shard_map/ppermute | solution.py:541
  201.9 18.5 %collective-permute-start.14 = (bf16[2,184,640]{2,1,0:T(8,128)(2,1)S(1)}, bf16[2,184,640]{2,1,0:T(8,128)(2,1)S(1)}, u32[]{:S(2)}, u32[]{:S(2)}) collective-permute-start(bf16[2,184,640]{2,1,0:T(8,128)(2,1)S(1)} %collective-permute-done.10.rest_3_), channel_id=1, source_target_pairs={{0,16},{16,0},{1,17},{17,1},{2,18},{18,2},{3,19},{19,3},{4,20},{20... | collective-permute-start | bytes 1413128 | tf_op jit(solution)/shard_map/ppermute | solution.py:541
  213.5 7.8 %collective-permute-start.31 = (bf16[2,360,256]{2,1,0:T(8,128)(2,1)}, bf16[2,360,256]{2,1,0:T(8,128)(2,1)}, u32[]{:S(2)}, u32[]{:S(2)}) collective-permute-start(bf16[2,360,256]{2,1,0:T(8,128)(2,1)} %collective-permute-done.29.rest_5_), channel_id=1, source_target_pairs={{0,2},{2,0},{4,6},{6,4},{8,10},{10,8},{12,14},{14,12},{1,3},{3,1},... | collective-permute-start | bytes 1105928 | tf_op jit(solution)/shard_map/ppermute | solution.py:541
  214.0 7.3 %collective-permute-start.18 = (bf16[2,184,640]{2,1,0:T(8,128)(2,1)S(1)}, bf16[2,184,640]{2,1,0:T(8,128)(2,1)S(1)}, u32[]{:S(2)}, u32[]{:S(2)}) collective-permute-start(bf16[2,184,640]{2,1,0:T(8,128)(2,1)S(1)} %collective-permute-done.10.rest_3_), channel_id=1, source_target_pairs={{0,1},{1,0},{2,3},{3,2},{4,5},{5,4},{6,7},{7,6},{8,9},{9,8},{10,11... | collective-permute-start | bytes 1413128 | tf_op jit(solution)/shard_map/ppermute | solution.py:541
  214.0 7.8 %collective-permute-start.20 = (bf16[2,184,640]{2,1,0:T(8,128)(2,1)S(1)}, bf16[2,184,640]{2,1,0:T(8,128)(2,1)S(1)}, u32[]{:S(2)}, u32[]{:S(2)}) collective-permute-start(bf16[2,184,640]{2,1,0:T(8,128)(2,1)S(1)} %collective-permute-done.12.rest_5_), channel_id=1, source_target_pairs={{0,1},{1,0},{2,3},{3,2},{4,5},{5,4},{6,7},{7,6},{8,9},{9,8},{10,11... | collective-permute-start | bytes 1413128 | tf_op jit(solution)/shard_map/ppermute | solution.py:541
  214.5 7.4 %collective-permute-start.21 = (bf16[2,184,640]{2,1,0:T(8,128)(2,1)S(1)}, bf16[2,184,640]{2,1,0:T(8,128)(2,1)S(1)}, u32[]{:S(2)}, u32[]{:S(2)}) collective-permute-start(bf16[2,184,640]{2,1,0:T(8,128)(2,1)S(1)} %collective-permute-done.13.rest_6_), channel_id=1, source_target_pairs={{0,1},{1,0},{2,3},{3,2},{4,5},{5,4},{6,7},{7,6},{8,9},{9,8},{10,11... | collective-permute-start | bytes 1413128 | tf_op jit(solution)/shard_map/ppermute | solution.py:541
  220.4 1.9 collective-permute-start.22
  221.3 8.8 %collective-permute-start.36 = (bf16[2,360,256]{2,1,0:T(8,128)(2,1)}, bf16[2,360,256]{2,1,0:T(8,128)(2,1)}, u32[]{:S(2)}, u32[]{:S(2)}) collective-permute-start(bf16[2,360,256]{2,1,0:T(8,128)(2,1)} %collective-permute-done.28.rest_4_), channel_id=1, source_target_pairs={{0,1},{1,0},{2,3},{3,2},{4,5},{5,4},{6,7},{7,6},{8,9},{9,8},{10,11... | collective-permute-start | bytes 1105928 | tf_op jit(solution)/shard_map/ppermute | solution.py:541
  221.3 15.0 %collective-permute-start.37 = (bf16[2,360,256]{2,1,0:T(8,128)(2,1)}, bf16[2,360,256]{2,1,0:T(8,128)(2,1)}, u32[]{:S(2)}, u32[]{:S(2)}) collective-permute-start(bf16[2,360,256]{2,1,0:T(8,128)(2,1)} %collective-permute-done.29.rest_5_), channel_id=1, source_target_pairs={{0,1},{1,0},{2,3},{3,2},{4,5},{5,4},{6,7},{7,6},{8,9},{9,8},{10,11... | collective-permute-start | bytes 1105928 | tf_op jit(solution)/shard_map/ppermute | solution.py:541
  221.8 14.5 %collective-permute-start.35 = (bf16[2,360,256]{2,1,0:T(8,128)(2,1)}, bf16[2,360,256]{2,1,0:T(8,128)(2,1)}, u32[]{:S(2)}, u32[]{:S(2)}) collective-permute-start(bf16[2,360,256]{2,1,0:T(8,128)(2,1)} %collective-permute-done.27.rest_3_), channel_id=1, source_target_pairs={{0,1},{1,0},{2,3},{3,2},{4,5},{5,4},{6,7},{7,6},{8,9},{9,8},{10,11... | collective-permute-start | bytes 1105928 | tf_op jit(solution)/shard_map/ppermute | solution.py:541
  221.9 14.4 %collective-permute-start.38 = (bf16[2,360,256]{2,1,0:T(8,128)(2,1)}, bf16[2,360,256]{2,1,0:T(8,128)(2,1)}, u32[]{:S(2)}, u32[]{:S(2)}) collective-permute-start(bf16[2,360,256]{2,1,0:T(8,128)(2,1)} %collective-permute-done.30.rest_6_), channel_id=1, source_target_pairs={{0,1},{1,0},{2,3},{3,2},{4,5},{5,4},{6,7},{7,6},{8,9},{9,8},{10,11... | collective-permute-start | bytes 1105928 | tf_op jit(solution)/shard_map/ppermute | solution.py:541
  222.3 14.0 %collective-permute-start.39 = (bf16[2,360,256]{2,1,0:T(8,128)(2,1)}, bf16[2,360,256]{2,1,0:T(8,128)(2,1)}, u32[]{:S(2)}, u32[]{:S(2)}) collective-permute-start(bf16[2,360,256]{2,1,0:T(8,128)(2,1)} %collective-permute-done.31.rest_7_), channel_id=1, source_target_pairs={{0,1},{1,0},{2,3},{3,2},{4,5},{5,4},{6,7},{7,6},{8,9},{9,8},{10,11... | collective-permute-start | bytes 1105928 | tf_op jit(solution)/shard_map/ppermute | solution.py:541
  230.1 6.2 %collective-permute-start.23 = (bf16[128,512]{1,0:T(8,128)(2,1)S(1)}, bf16[128,512]{1,0:T(8,128)(2,1)S(1)}, u32[]{:S(2)}, u32[]{:S(2)}) collective-permute-start(bf16[128,512]{1,0:T(8,128)(2,1)S(1)} %get-tuple-element.28.pairs_ref), channel_id=1, source_target_pairs={{0,2},{2,4},{4,6},{6,8},{8,10},{10,12},{12,14},{14,1},{1,3},{3,5},... | collective-permute-start | bytes 393224 | tf_op jit(solution)/shard_map/ppermute | solution.py:692
  (15 other events, 184.5 us)

commit v6 on v5

--- a/solution.py
+++ b/solution.py
@@ -269,17 +269,18 @@
     return (place_ref[2] + group_flip) % 2 * 2 + (place_ref[3] + pipe_flip) % 2
 
 
-def columns_of(held, slices, place_ref, copies, lines, columns, out_ref):
-    tok_count = slices.shape[1]
+def columns_of(held, slices, place_ref, first, copies, out_ref):
+    tok_count, lines = slices.shape[1], held.shape[1]
+    columns = out_ref.shape[1] // 4
     for pair in range(4):
         total = jnp.zeros((tok_count, columns), F32)
         for flip in range(2):
-            for copy in copies[pair * 2 + flip]:
+            for copy in copies[pair * 2 + flip] if copies else ():
                 copy.wait()
             for step in range(lines):
                 total += jnp.dot(
                     slices[shard_of(place_ref, block_step(step, lines), flip, lines)],
-                    held[pair * 2 + flip, step],
+                    held[pair * 2 + flip, step, :, first : first + columns],
                     preferred_element_type=F32,
                 )
         start = quarter_of(place_ref, pair % 2, pair // 2) * columns
@@ -290,64 +291,59 @@
     rows, place_ref, tables_ref, residual_ref, coarse_ref, fine_ref, gain_ref, *rest
 ):
     parts, (pairs_ref, slices, hidden_ref, held, sems) = rest[:16], rest[16:]
-    lines, _, columns = held.shape[1:]
-    copies = start_copies(parts, held, sems, parts[0].shape[2] - columns)
+    copies = start_copies(parts, held, sems, 0)
     table = tables_ref[...]
     mixed = jnp.dot(coarse_ref[...], table, preferred_element_type=F32)
     mixed += jnp.dot(fine_ref[...], table, preferred_element_type=F32)
     hidden = (residual_ref[...].astype(F32) + mixed).astype(BF16)
+    hidden_ref[...] = hidden
     value = hidden.astype(F32)
     mean_square = jnp.mean(value * value, axis=-1, keepdims=True)
     normed = (value * lax.rsqrt(mean_square + eps) * gain_ref[...][None, :]).astype(BF16)
     slices[...] = jnp.zeros_like(slices)
-    for s in range(2 * lines):
+    for s in range(slices.shape[0]):
         slices[s, :, :rows] = normed[:, s * rows : (s + 1) * rows]
-    columns_of(held, slices, place_ref, copies, lines, columns, pairs_ref)
-    hidden_ref[...] = value.T.astype(BF16)
+    columns_of(held, slices, place_ref, held.shape[3] - pairs_ref.shape[1] // 4, copies, pairs_ref)
 
 
 def project_pairs(place, tables, residual, coarse, fine, gain, parts, rows, columns):
     tok_count, width = residual.shape
-    lines, padded = 2 * parts[0].shape[0], parts[0].shape[1]
+    half, padded, both = parts[0].shape
+    lines = 2 * half
     return pl.pallas_call(
         functools.partial(pairs_kernel, rows),
         out_shape=(
             jax.ShapeDtypeStruct((tok_count, 4 * columns), BF16),
             jax.ShapeDtypeStruct((2 * lines, tok_count, padded), BF16),
-            jax.ShapeDtypeStruct((width, tok_count), BF16),
+            jax.ShapeDtypeStruct((tok_count, width), BF16),
+            pltpu.VMEM((8, lines, padded, both), BF16),
         ),
         in_specs=[SMEM] + [VMEM] * 5 + [HBM] * 16,
-        out_specs=(VMEM,) * 3,
-        scratch_shapes=[
-            pltpu.VMEM((8, lines, padded, columns), BF16),
-            pltpu.SemaphoreType.DMA((16,)),
-        ],
+        out_specs=(VMEM,) * 4,
+        scratch_shapes=[pltpu.SemaphoreType.DMA((16,))],
         compiler_params=pltpu.CompilerParams(vmem_limit_bytes=20 << 20),
         name="pairs",
     )(place, tables, residual, coarse, fine, gain, *in_hbm(parts))
 
 
-def queries_kernel(place_ref, slices, *rest):
-    parts, (queries_ref, held, sems) = rest[:16], rest[16:]
-    lines, _, columns = held.shape[1:]
-    copies = start_copies(parts, held, sems, 0)
-    columns_of(held, slices, place_ref, copies, lines, columns, queries_ref)
-
-
-def project_queries(place, slices, parts, columns):
-    count, tok_count, padded = slices.shape
+def queries_kernel(place_ref, slices, hidden_ref, held, queries_ref, turned_ref):
+    turned_ref[...] = hidden_ref[...].astype(F32).T.astype(BF16)
+    columns_of(held, slices, place_ref, 0, None, queries_ref)
+
+
+def project_queries(place, slices, hidden, held, columns):
+    tok_count, width = hidden.shape
     return pl.pallas_call(
         queries_kernel,
-        out_shape=jax.ShapeDtypeStruct((tok_count, 4 * columns), BF16),
-        in_specs=[SMEM, VMEM] + [HBM] * 16,
-        out_specs=VMEM,
-        scratch_shapes=[
-            pltpu.VMEM((8, count // 2, padded, columns), BF16),
-            pltpu.SemaphoreType.DMA((16,)),
-        ],
+        out_shape=(
+            jax.ShapeDtypeStruct((tok_count, 4 * columns), BF16),
+            jax.ShapeDtypeStruct((width, tok_count), BF16),
+        ),
+        in_specs=[SMEM] + [VMEM] * 3,
+        out_specs=(VMEM, VMEM),
         compiler_params=pltpu.CompilerParams(vmem_limit_bytes=20 << 20),
         name="queries",
-    )(place, slices, *in_hbm(parts))
+    )(place, slices, hidden, held)
 
 
 def attention_kernel(
@@ -514,8 +510,8 @@
         for value in (even, odd):
             blocks += [value, swapped(value, "seq")]
     mine_qkv, mine_out = own_quarters(qkv_proj, out_proj)
-    gate_up, down_proj, place, mine_qkv, mine_out = lax.optimization_barrier(
-        (gate_up, down_proj, place, mine_qkv, mine_out)
+    gate_up, down_proj, place, masses, mine_qkv, mine_out = lax.optimization_barrier(
+        (gate_up, down_proj, place, jnp.exp(sinks), mine_qkv, mine_out)
     )
     qkv_parts = gather_quarters(mine_qkv, lines, "groups")
     out_parts = gather_quarters(mine_out, lines, "seq")
@@ -528,12 +524,12 @@
 
     summed = summed.reshape(E * CAP, width)
     query_width = QUERY_HEADS * HEAD_SIZE
-    pairs, slices, hidden_t = project_pairs(
+    pairs, slices, hidden, held = project_pairs(
         place, summed, residual, coarse, fine, attn_gain, qkv_parts, rows, (qkv_width - query_width) // 4
     )
     halo = halo_exchange(pairs[tok_count - WINDOW_SPAN :])
-    queries = project_queries(place, slices, qkv_parts, query_width // 4)
-    out_t = attend_and_project(place, jnp.exp(sinks), queries, pairs, halo, hidden_t, out_parts)
+    queries, hidden_t = project_queries(place, slices, hidden, held, query_width // 4)
+    out_t = attend_and_project(place, masses, queries, pairs, halo, hidden_t, out_parts)
     return out_t.T[None]
 
 

time: 247 us -> 247 us (level)
  Pallas kernels: 40.2 us -> 37.7 us
  transfers between devices with their start and end apart: 41 -> 41, of which waited for: 16 -> 17; matrix products, arithmetic and copies ran while one was open for 0% -> 1% of each run, Pallas kernels for 6% -> 5%
where the time goes in v6:
time: 247 us; the launch traced here: 243 us
  waiting for transfers between devices  164 us (66%)
  starting transfers between devices  38.5 us (16%)
  Pallas kernels  37.7 us (15%)
  local copies, waits for them, and re-layouts  2.98 us (1%)
    ppermute x7, waiting for transfers between devices, flipped(): return lax.ppermute(value, 'seq', [(i, i ^ bit * 2) for i in range(count)])  101 us
    ppermute x32, waiting for transfers between devices, swapped(): lax.ppermute(value, axis, [(i, i ^ 1) for i in range(lax.axis_size(axis))])  61.7 us
    ppermute x32, starting transfers between devices, swapped(): lax.ppermute(value, axis, [(i, i ^ 1) for i in range(lax.axis_size(axis))])  19.2 us
    pallas_call x1, Pallas kernels, run_experts(): pl.pallas_call(functools.partial(experts_kernel, seq_count // 2), out_sha...  14.5 us
    ppermute x7, starting transfers between devices, flipped(): return lax.ppermute(value, 'seq', [(i, i ^ bit * 2) for i in range(count)])  11.2 us
    pallas_call x1, Pallas kernels, attend_and_project(): pl.pallas_call(attention_kernel, out_shape=jax.ShapeDtypeStruct((width, t...  8.07 us
    all_to_all x1, starting transfers between devices, fused_body(): lax.all_to_all(finished, 'seq', split_axis=0, concat_axis=0, tiled=True)  5.65 us
    pallas_call x1, Pallas kernels, project_pairs(): pl.pallas_call(functools.partial(pairs_kernel, rows), out_shape=(jax.Shap...  5.17 us
  transfers between devices with their start and end apart: 41, of which 17 were waited for; matrix products, arithmetic and copies ran while one was open for 1% of the time, Pallas kernels for 5%

profile of v6, /device:TPU:0, one launch (start us, length us, event | category | flops | bytes accessed | tf_op | source)
XLA Modules:
  0.0 243.3 jit_solution(2131222049386311104)
XLA Ops:
  0.0 2.2 prepare.1.refs_0_
  2.2 4.1 %collective-permute-start.3 = (bf16[128,1536]{1,0:T(8,128)(2,1)}, bf16[128,1536]{1,0:T(8,128)(2,1)S(1)}, u32[]{:S(2)}, u32[]{:S(2)}) collective-permute-start(bf16[128,1536]{1,0:T(8,128)(2,1)} %prepare.1.refs_0_), channel_id=1, source_target_pairs={{0,8},{2,10},{4,12},{6,14},{8,0},{10,2},{12,4},{14,6},{1,9},{3,11}... | collective-permute-start | bytes 1179656 | tf_op jit(solution)/shard_map/ppermute | solution.py:470
  6.3 1.6 collective-permute-start.1
  7.8 16.3 %collective-permute-done.3.refs_4_ = bf16[128,1536]{1,0:T(8,128)(2,1)S(1)} collective-permute-done((bf16[128,1536]{1,0:T(8,128)(2,1)}, bf16[128,1536]{1,0:T(8,128)(2,1)S(1)}, u32[]{:S(2)}, u32[]{:S(2)}) %collective-permute-start.3) | collective-permute-done | bytes 393248 | tf_op jit(solution)/shard_map/ppermute | solution.py:470
  24.1 0.7 collective-permute-start.5
  24.8 1.5 collective-permute-start
  26.4 0.6 collective-permute-start.4
  27.0 1.5 collective-permute-start.2
  28.5 5.9 %collective-permute-done.5.refs_6_ = bf16[128,1536]{1,0:T(8,128)(2,1)S(1)} collective-permute-done((bf16[128,1536]{1,0:T(8,128)(2,1)S(1)}, bf16[128,1536]{1,0:T(8,128)(2,1)S(1)}, u32[]{:S(2)}, u32[]{:S(2)}) %collective-permute-start.5) | collective-permute-done | bytes 393248 | tf_op jit(solution)/shard_map/ppermute | solution.py:470
  34.3 1.3 collective-permute-start.6
  35.7 0.7 exp.3.sink_ref
  36.4 1.6 dynamic-slice_bitcast_fusion.refs_0_
  38.1 3.0 %fetch.1 = (bf16[1440,1440]{1,0:T(8,128)(2,1)S(1)}, bf16[720,1440]{1,0:T(8,128)(2,1)S(1)}) custom-call(bf16[4,1440,1440]{2,1,0:T(8,128)(2,1)} %refs_10_, bf16[4,720,1440]{2,1,0:T(8,128)(2,1)} %refs_11_), custom_call_target="tpu_custom_call" | custom-call | tf_op jit(solution)/shard_map/fetch/pallas_call | solution.py:118
  41.1 4.4 %collective-permute-done.4.refs_5_ = bf16[128,1536]{1,0:T(8,128)(2,1)S(1)} collective-permute-done((bf16[128,1536]{1,0:T(8,128)(2,1)S(1)}, bf16[128,1536]{1,0:T(8,128)(2,1)S(1)}, u32[]{:S(2)}, u32[]{:S(2)}) %collective-permute-start.4) | collective-permute-done | bytes 393248 | tf_op jit(solution)/shard_map/ppermute | solution.py:537
  45.5 8.4 %collective-permute-done.2.refs_3_ = bf16[128,1536]{1,0:T(8,128)(2,1)S(1)} collective-permute-done((bf16[128,1536]{1,0:T(8,128)(2,1)S(1)}, bf16[128,1536]{1,0:T(8,128)(2,1)S(1)}, u32[]{:S(2)}, u32[]{:S(2)}) %collective-permute-start.2) | collective-permute-done | bytes 393248 | tf_op jit(solution)/shard_map/ppermute | solution.py:537
  53.9 7.3 %collective-permute-done.6.refs_7_ = bf16[128,1536]{1,0:T(8,128)(2,1)} collective-permute-done((bf16[128,1536]{1,0:T(8,128)(2,1)S(1)}, bf16[128,1536]{1,0:T(8,128)(2,1)}, u32[]{:S(2)}, u32[]{:S(2)}) %collective-permute-start.6) | collective-permute-done | bytes 393248 | tf_op jit(solution)/shard_map/ppermute | solution.py:537
  61.2 14.5 %experts.1 = bf16[8,2,48,1440]{3,2,1,0:T(8,128)(2,1)} custom-call(s32[4]{0:T(128)S(1)} %pad_add_fusion.place_ref, bf16[128,1536]{1,0:T(8,128)(2,1)S(1)} %copy-done.2, bf16[128,1536]{1,0:T(8,128)(2,1)S(1)} %collective-permute-done.refs_1_, bf16[128,1536]{1,0:T(8,128)(2,1)S(1)} %collective-permute-done.1.refs_2_, ...), custom_call_target="tpu_custom_call" | custom-call | tf_op jit(solution)/shard_map/experts/pallas_call | solution.py:198
  75.7 5.6 %all-to-all-start = ((bf16[8,2,48,1440]{3,2,1,0:T(8,128)(2,1)}), bf16[8,2,48,1440]{3,2,1,0:T(8,128)(2,1)S(1)}, u32[]{:S(2)}, u32[]{:S(2)}) async-start(bf16[8,2,48,1440]{3,2,1,0:T(8,128)(2,1)} %experts.1), calls=%async_computation | async-start | bytes 4718592 | tf_op jit(solution)/shard_map/all_to_all | solution.py:522
  81.4 2.9 %collective-permute-start.24 = (bf16[360,256]{1,0:T(8,128)(2,1)S(1)}, bf16[360,256]{1,0:T(8,128)(2,1)S(1)}, u32[]{:S(2)}, u32[]{:S(2)}) collective-permute-start(bf16[360,256]{1,0:T(8,128)(2,1)S(1)} %copy-done.3), channel_id=1, source_target_pairs={{0,8},{2,10},{4,12},{6,14},{8,0},{10,2},{12,4},{14,6},{1,9},{3,11}... | collective-permute-start | bytes 552968 | tf_op jit(solution)/shard_map/ppermute | solution.py:470
  84.4 65.3 %collective-permute-done.24.refs_1_ = bf16[360,256]{1,0:T(8,128)(2,1)S(1)} collective-permute-done((bf16[360,256]{1,0:T(8,128)(2,1)S(1)}, bf16[360,256]{1,0:T(8,128)(2,1)S(1)}, u32[]{:S(2)}, u32[]{:S(2)}) %collective-permute-start.24) | collective-permute-done | bytes 184352 | tf_op jit(solution)/shard_map/ppermute | solution.py:470
  149.7 0.8 shard_map.101.rest_0_
  150.6 1.5 collective-permute-start.28
  152.4 0.8 shard_map.100.rest_0_
  153.2 1.8 collective-permute-start.8
  154.9 7.2 %collective-permute-done.25.rest_1_ = bf16[2,360,256]{2,1,0:T(8,128)(2,1)S(1)} collective-permute-done((bf16[2,360,256]{2,1,0:T(8,128)(2,1)}, bf16[2,360,256]{2,1,0:T(8,128)(2,1)S(1)}, u32[]{:S(2)}, u32[]{:S(2)}) %collective-permute-start.25) | collective-permute-done | bytes 368672 | tf_op jit(solution)/shard_map/ppermute | solution.py:470
  162.2 1.5 collective-permute-start.11
  163.8 0.6 collective-permute-start.29
  164.4 5.9 %collective-permute-done.8.rest_1_ = bf16[2,184,640]{2,1,0:T(8,128)(2,1)S(1)} collective-permute-done((bf16[2,184,640]{2,1,0:T(8,128)(2,1)}, bf16[2,184,640]{2,1,0:T(8,128)(2,1)S(1)}, u32[]{:S(2)}, u32[]{:S(2)}) %collective-permute-start.8) | collective-permute-done | bytes 471072 | tf_op jit(solution)/shard_map/ppermute | solution.py:470
  170.3 1.5 collective-permute-start.27
  171.7 0.8 collective-permute-done.9.rest_2_
  172.6 1.7 collective-permute-start.10
  174.3 1.8 collective-permute-done.11.rest_4_
  176.1 1.5 collective-permute-start.12
  177.6 0.5 collective-permute-start.30
  178.2 6.0 %collective-permute-done.29.rest_5_ = bf16[2,360,256]{2,1,0:T(8,128)(2,1)} collective-permute-done((bf16[2,360,256]{2,1,0:T(8,128)(2,1)S(1)}, bf16[2,360,256]{2,1,0:T(8,128)(2,1)}, u32[]{:S(2)}, u32[]{:S(2)}) %collective-permute-start.29) | collective-permute-done | bytes 368672 | tf_op jit(solution)/shard_map/ppermute | solution.py:537
  184.1 0.5 collective-permute-start.34
  184.6 15.2 %collective-permute-done.30.rest_6_ = bf16[2,360,256]{2,1,0:T(8,128)(2,1)} collective-permute-done((bf16[2,360,256]{2,1,0:T(8,128)(2,1)S(1)}, bf16[2,360,256]{2,1,0:T(8,128)(2,1)}, u32[]{:S(2)}, u32[]{:S(2)}) %collective-permute-start.30) | collective-permute-done | bytes 368672 | tf_op jit(solution)/shard_map/ppermute | solution.py:537
  199.8 1.5 collective-permute-start.13
  201.9 0.5 collective-permute-start.14
  202.5 11.0 %collective-permute-done.13.rest_6_ = bf16[2,184,640]{2,1,0:T(8,128)(2,1)S(1)} collective-permute-done((bf16[2,184,640]{2,1,0:T(8,128)(2,1)S(1)}, bf16[2,184,640]{2,1,0:T(8,128)(2,1)S(1)}, u32[]{:S(2)}, u32[]{:S(2)}) %collective-permute-start.13) | collective-permute-done | bytes 471072 | tf_op jit(solution)/shard_map/ppermute | solution.py:537
  214.5 5.9 %collective-permute-done.14.rest_7_ = bf16[2,184,640]{2,1,0:T(8,128)(2,1)S(1)} collective-permute-done((bf16[2,184,640]{2,1,0:T(8,128)(2,1)S(1)}, bf16[2,184,640]{2,1,0:T(8,128)(2,1)S(1)}, u32[]{:S(2)}, u32[]{:S(2)}) %collective-permute-start.14) | collective-permute-done | bytes 471072 | tf_op jit(solution)/shard_map/ppermute | solution.py:537
  220.4 0.9 collective-permute-done.31.rest_7_
  223.1 1.3 returns.1
  224.5 5.2 %pairs.1 = (bf16[128,512]{1,0:T(8,128)(2,1)S(1)}, bf16[8,128,184]{2,1,0:T(8,128)(2,1)S(1)}, bf16[128,1440]{1,0:T(8,128)(2,1)S(1)}, bf16[8,4,184,640]{3,2,1,0:T(8,128)(2,1)S(1)}) custom-call(s32[4]{0:T(128)S(1)} %pad_add_fusion.place_ref, bf16[768,1440]{1,0:T(8,128)(2,1)S(1)} %bitcast.19, bf16[128,1440]{1,0:T(8,128)(2,1)S(1)} %get-tuple-element.28.residual_ref, ...), custom_call_target="tpu_custom_call" | custom-call | tf_op jit(solution)/shard_map/pairs/pallas_call | solution.py:313
  229.7 2.4 collective-permute-start.23
  232.1 1.8 queries.1
  233.9 1.2 collective-permute-done.23.halo_ref
  235.1 8.1 %attention.1 = bf16[1440,128]{1,0:T(8,128)(2,1)} custom-call(s32[4]{0:T(128)S(1)} %pad_add_fusion.place_ref, f32[32]{0:T(128)S(1)} %exp.3.sink_ref, bf16[128,2048]{1,0:T(8,128)(2,1)S(1)} %get-tuple-element.35.packed_ref, bf16[128,512]{1,0:T(8,128)(2,1)S(1)} %get-tuple-element.36.pairs_ref, bf16[128,512]{1,0:T(8,128)(2,1)S(1)} %collective-permute-done.23.halo_ref, ...), custom_call_target="tpu_custom_call" | custom-call | tf_op jit(solution)/shard_map/attention/pallas_call | solution.py:433
  (95 shorter events, 4.1 us)
Async XLA Ops:
  2.2 21.9 %collective-permute-start.3 = (bf16[128,1536]{1,0:T(8,128)(2,1)}, bf16[128,1536]{1,0:T(8,128)(2,1)S(1)}, u32[]{:S(2)}, u32[]{:S(2)}) collective-permute-start(bf16[128,1536]{1,0:T(8,128)(2,1)} %prepare.1.refs_0_), channel_id=1, source_target_pairs={{0,8},{2,10},{4,12},{6,14},{8,0},{10,2},{12,4},{14,6},{1,9},{3,11}... | collective-permute-start | bytes 1179656 | tf_op jit(solution)/shard_map/ppermute | solution.py:470
  6.3 20.7 %collective-permute-start.1 = (bf16[128,1536]{1,0:T(8,128)(2,1)}, bf16[128,1536]{1,0:T(8,128)(2,1)S(1)}, u32[]{:S(2)}, u32[]{:S(2)}) collective-permute-start(bf16[128,1536]{1,0:T(8,128)(2,1)} %prepare.1.refs_0_), channel_id=1, source_target_pairs={{0,4},{2,6},{4,0},{6,2},{8,12},{10,14},{12,8},{14,10},{1,5},{3,7},... | collective-permute-start | bytes 1179656 | tf_op jit(solution)/shard_map/ppermute | solution.py:470
  24.1 10.2 %collective-permute-start.5 = (bf16[128,1536]{1,0:T(8,128)(2,1)S(1)}, bf16[128,1536]{1,0:T(8,128)(2,1)S(1)}, u32[]{:S(2)}, u32[]{:S(2)}) collective-permute-start(bf16[128,1536]{1,0:T(8,128)(2,1)S(1)} %collective-permute-done.3.refs_4_), channel_id=1, source_target_pairs={{0,4},{2,6},{4,0},{6,2},{8,12},{10,14},{12,8},{14,10},{1,5},{3,7},... | collective-permute-start | bytes 1179656 | tf_op jit(solution)/shard_map/ppermute | solution.py:470
  24.8 16.3 %collective-permute-start = (bf16[128,1536]{1,0:T(8,128)(2,1)}, bf16[128,1536]{1,0:T(8,128)(2,1)S(1)}, u32[]{:S(2)}, u32[]{:S(2)}) collective-permute-start(bf16[128,1536]{1,0:T(8,128)(2,1)} %prepare.1.refs_0_), channel_id=1, source_target_pairs={{0,2},{2,0},{4,6},{6,4},{8,10},{10,8},{12,14},{14,12},{1,3},{3,1},... | collective-permute-start | bytes 1179656 | tf_op jit(solution)/shard_map/ppermute | solution.py:537
  26.4 19.1 %collective-permute-start.4 = (bf16[128,1536]{1,0:T(8,128)(2,1)S(1)}, bf16[128,1536]{1,0:T(8,128)(2,1)S(1)}, u32[]{:S(2)}, u32[]{:S(2)}) collective-permute-start(bf16[128,1536]{1,0:T(8,128)(2,1)S(1)} %collective-permute-done.3.refs_4_), channel_id=1, source_target_pairs={{0,2},{2,0},{4,6},{6,4},{8,10},{10,8},{12,14},{14,12},{1,3},{3,1},... | collective-permute-start | bytes 1179656 | tf_op jit(solution)/shard_map/ppermute | solution.py:537
  27.0 26.9 %collective-permute-start.2 = (bf16[128,1536]{1,0:T(8,128)(2,1)S(1)}, bf16[128,1536]{1,0:T(8,128)(2,1)S(1)}, u32[]{:S(2)}, u32[]{:S(2)}) collective-permute-start(bf16[128,1536]{1,0:T(8,128)(2,1)S(1)} %collective-permute-done.1.refs_2_), channel_id=1, source_target_pairs={{0,2},{2,0},{4,6},{6,4},{8,10},{10,8},{12,14},{14,12},{1,3},{3,1},... | collective-permute-start | bytes 1179656 | tf_op jit(solution)/shard_map/ppermute | solution.py:537
  34.3 26.9 %collective-permute-start.6 = (bf16[128,1536]{1,0:T(8,128)(2,1)S(1)}, bf16[128,1536]{1,0:T(8,128)(2,1)}, u32[]{:S(2)}, u32[]{:S(2)}) collective-permute-start(bf16[128,1536]{1,0:T(8,128)(2,1)S(1)} %collective-permute-done.5.refs_6_), channel_id=1, source_target_pairs={{0,2},{2,0},{4,6},{6,4},{8,10},{10,8},{12,14},{14,12},{1,3},{3,1},... | collective-permute-start | bytes 1179656 | tf_op jit(solution)/shard_map/ppermute | solution.py:537
  75.7 148.7 %copy-start.4 = (f32[1440]{0:T(1024)S(1)}, f32[1440]{0:T(1024)}, u32[]{:S(2)}) copy-start(f32[1440]{0:T(1024)} %gain_ref.3) | copy-start | bytes 17284
  75.7 148.7 %all-to-all-start = ((bf16[8,2,48,1440]{3,2,1,0:T(8,128)(2,1)}), bf16[8,2,48,1440]{3,2,1,0:T(8,128)(2,1)S(1)}, u32[]{:S(2)}, u32[]{:S(2)}) async-start(bf16[8,2,48,1440]{3,2,1,0:T(8,128)(2,1)} %experts.1), calls=%async_computation | async-start | bytes 4718592 | tf_op jit(solution)/shard_map/all_to_all | solution.py:522
  81.4 68.3 %collective-permute-start.24 = (bf16[360,256]{1,0:T(8,128)(2,1)S(1)}, bf16[360,256]{1,0:T(8,128)(2,1)S(1)}, u32[]{:S(2)}, u32[]{:S(2)}) collective-permute-start(bf16[360,256]{1,0:T(8,128)(2,1)S(1)} %copy-done.3), channel_id=1, source_target_pairs={{0,8},{2,10},{4,12},{6,14},{8,0},{10,2},{12,4},{14,6},{1,9},{3,11}... | collective-permute-start | bytes 552968 | tf_op jit(solution)/shard_map/ppermute | solution.py:470
  84.3 68.1 %collective-permute-start.7 = (bf16[184,640]{1,0:T(8,128)(2,1)S(1)}, bf16[184,640]{1,0:T(8,128)(2,1)S(1)}, u32[]{:S(2)}, u32[]{:S(2)}) collective-permute-start(bf16[184,640]{1,0:T(8,128)(2,1)S(1)} %fusion.2.refs_0_), channel_id=1, source_target_pairs={{0,8},{2,10},{4,12},{6,14},{8,0},{10,2},{12,4},{14,6},{1,9},{3,11}... | collective-permute-start | bytes 706568 | tf_op jit(solution)/shard_map/ppermute | solution.py:470
  150.4 11.7 %collective-permute-start.25 = (bf16[2,360,256]{2,1,0:T(8,128)(2,1)}, bf16[2,360,256]{2,1,0:T(8,128)(2,1)S(1)}, u32[]{:S(2)}, u32[]{:S(2)}) collective-permute-start(bf16[2,360,256]{2,1,0:T(8,128)(2,1)} %shard_map.101.rest_0_), channel_id=1, source_target_pairs={{0,4},{2,6},{4,0},{6,2},{8,12},{10,14},{12,8},{14,10},{1,5},{3,7},... | collective-permute-start | bytes 1105928 | tf_op jit(solution)/shard_map/ppermute | solution.py:470
  150.5 11.7 %collective-permute-start.26 = (bf16[2,360,256]{2,1,0:T(8,128)(2,1)}, bf16[2,360,256]{2,1,0:T(8,128)(2,1)S(1)}, u32[]{:S(2)}, u32[]{:S(2)}) collective-permute-start(bf16[2,360,256]{2,1,0:T(8,128)(2,1)} %shard_map.101.rest_0_), channel_id=1, source_target_pairs={{0,2},{2,0},{4,6},{6,4},{8,10},{10,8},{12,14},{14,12},{1,3},{3,1},... | collective-permute-start | bytes 1105928 | tf_op jit(solution)/shard_map/ppermute | solution.py:537
  150.6 13.1 %collective-permute-start.28 = (bf16[2,360,256]{2,1,0:T(8,128)(2,1)}, bf16[2,360,256]{2,1,0:T(8,128)(2,1)}, u32[]{:S(2)}, u32[]{:S(2)}) collective-permute-start(bf16[2,360,256]{2,1,0:T(8,128)(2,1)} %shard_map.101.rest_0_), channel_id=1, source_target_pairs={{0,16},{16,0},{1,17},{17,1},{2,18},{18,2},{3,19},{19,3},{4,20},{20... | collective-permute-start | bytes 1105928 | tf_op jit(solution)/shard_map/ppermute | solution.py:537
  153.2 17.1 %collective-permute-start.8 = (bf16[2,184,640]{2,1,0:T(8,128)(2,1)}, bf16[2,184,640]{2,1,0:T(8,128)(2,1)S(1)}, u32[]{:S(2)}, u32[]{:S(2)}) collective-permute-start(bf16[2,184,640]{2,1,0:T(8,128)(2,1)} %shard_map.100.rest_0_), channel_id=1, source_target_pairs={{0,4},{2,6},{4,0},{6,2},{8,12},{10,14},{12,8},{14,10},{1,5},{3,7},... | collective-permute-start | bytes 1413128 | tf_op jit(solution)/shard_map/ppermute | solution.py:470
  154.9 8.8 %collective-permute-start.32 = (bf16[2,360,256]{2,1,0:T(8,128)(2,1)}, bf16[2,360,256]{2,1,0:T(8,128)(2,1)S(1)}, u32[]{:S(2)}, u32[]{:S(2)}) collective-permute-start(bf16[2,360,256]{2,1,0:T(8,128)(2,1)} %shard_map.101.rest_0_), channel_id=1, source_target_pairs={{0,1},{1,0},{2,3},{3,2},{4,5},{5,4},{6,7},{7,6},{8,9},{9,8},{10,11... | collective-permute-start | bytes 1105928 | tf_op jit(solution)/shard_map/ppermute | solution.py:537
  162.2 60.3 %copy-start.20 = (bf16[2,360,256]{2,1,0:T(8,128)(2,1)}, bf16[2,360,256]{2,1,0:T(8,128)(2,1)S(1)}, u32[]{:S(2)}) copy-start(bf16[2,360,256]{2,1,0:T(8,128)(2,1)S(1)} %collective-permute-done.25.rest_1_) | copy-start | bytes 1105924
  162.2 10.4 %collective-permute-start.9 = (bf16[2,184,640]{2,1,0:T(8,128)(2,1)}, bf16[2,184,640]{2,1,0:T(8,128)(2,1)S(1)}, u32[]{:S(2)}, u32[]{:S(2)}) collective-permute-start(bf16[2,184,640]{2,1,0:T(8,128)(2,1)} %shard_map.100.rest_0_), channel_id=1, source_target_pairs={{0,2},{2,0},{4,6},{6,4},{8,10},{10,8},{12,14},{14,12},{1,3},{3,1},... | collective-permute-start | bytes 1413128 | tf_op jit(solution)/shard_map/ppermute | solution.py:537
  162.2 39.1 %copy-start.21 = (bf16[2,360,256]{2,1,0:T(8,128)(2,1)}, bf16[2,360,256]{2,1,0:T(8,128)(2,1)S(1)}, u32[]{:S(2)}) copy-start(bf16[2,360,256]{2,1,0:T(8,128)(2,1)S(1)} %collective-permute-done.26.rest_2_) | copy-start | bytes 1105924
  162.2 13.9 %collective-permute-start.11 = (bf16[2,184,640]{2,1,0:T(8,128)(2,1)}, bf16[2,184,640]{2,1,0:T(8,128)(2,1)S(1)}, u32[]{:S(2)}, u32[]{:S(2)}) collective-permute-start(bf16[2,184,640]{2,1,0:T(8,128)(2,1)} %shard_map.100.rest_0_), channel_id=1, source_target_pairs={{0,16},{16,0},{1,17},{17,1},{2,18},{18,2},{3,19},{19,3},{4,20},{20... | collective-permute-start | bytes 1413128 | tf_op jit(solution)/shard_map/ppermute | solution.py:537
  163.8 13.9 %collective-permute-start.15 = (bf16[2,184,640]{2,1,0:T(8,128)(2,1)}, bf16[2,184,640]{2,1,0:T(8,128)(2,1)S(1)}, u32[]{:S(2)}, u32[]{:S(2)}) collective-permute-start(bf16[2,184,640]{2,1,0:T(8,128)(2,1)} %shard_map.100.rest_0_), channel_id=1, source_target_pairs={{0,1},{1,0},{2,3},{3,2},{4,5},{5,4},{6,7},{7,6},{8,9},{9,8},{10,11... | collective-permute-start | bytes 1413128 | tf_op jit(solution)/shard_map/ppermute | solution.py:537
  163.8 20.4 %collective-permute-start.29 = (bf16[2,360,256]{2,1,0:T(8,128)(2,1)S(1)}, bf16[2,360,256]{2,1,0:T(8,128)(2,1)}, u32[]{:S(2)}, u32[]{:S(2)}) collective-permute-start(bf16[2,360,256]{2,1,0:T(8,128)(2,1)S(1)} %collective-permute-done.25.rest_1_), channel_id=1, source_target_pairs={{0,16},{16,0},{1,17},{17,1},{2,18},{18,2},{3,19},{19,3},{4,20},{20... | collective-permute-start | bytes 1105928 | tf_op jit(solution)/shard_map/ppermute | solution.py:537
  170.3 52.2 %copy-start.5 = (bf16[2,184,640]{2,1,0:T(8,128)(2,1)}, bf16[2,184,640]{2,1,0:T(8,128)(2,1)S(1)}, u32[]{:S(2)}) copy-start(bf16[2,184,640]{2,1,0:T(8,128)(2,1)S(1)} %collective-permute-done.8.rest_1_) | copy-start | bytes 1413124
  170.3 13.9 %collective-permute-start.27 = (bf16[2,360,256]{2,1,0:T(8,128)(2,1)S(1)}, bf16[2,360,256]{2,1,0:T(8,128)(2,1)}, u32[]{:S(2)}, u32[]{:S(2)}) collective-permute-start(bf16[2,360,256]{2,1,0:T(8,128)(2,1)S(1)} %collective-permute-done.25.rest_1_), channel_id=1, source_target_pairs={{0,2},{2,0},{4,6},{6,4},{8,10},{10,8},{12,14},{14,12},{1,3},{3,1},... | collective-permute-start | bytes 1105928 | tf_op jit(solution)/shard_map/ppermute | solution.py:537
  172.6 49.9 %copy-start.6 = (bf16[2,184,640]{2,1,0:T(8,128)(2,1)}, bf16[2,184,640]{2,1,0:T(8,128)(2,1)S(1)}, u32[]{:S(2)}) copy-start(bf16[2,184,640]{2,1,0:T(8,128)(2,1)S(1)} %collective-permute-done.9.rest_2_) | copy-start | bytes 1413124
  172.6 29.3 %collective-permute-start.10 = (bf16[2,184,640]{2,1,0:T(8,128)(2,1)S(1)}, bf16[2,184,640]{2,1,0:T(8,128)(2,1)S(1)}, u32[]{:S(2)}, u32[]{:S(2)}) collective-permute-start(bf16[2,184,640]{2,1,0:T(8,128)(2,1)S(1)} %collective-permute-done.8.rest_1_), channel_id=1, source_target_pairs={{0,2},{2,0},{4,6},{6,4},{8,10},{10,8},{12,14},{14,12},{1,3},{3,1},... | collective-permute-start | bytes 1413128 | tf_op jit(solution)/shard_map/ppermute | solution.py:537
  176.1 46.3 %copy-start.7 = (bf16[2,184,640]{2,1,0:T(8,128)(2,1)}, bf16[2,184,640]{2,1,0:T(8,128)(2,1)S(1)}, u32[]{:S(2)}) copy-start(bf16[2,184,640]{2,1,0:T(8,128)(2,1)S(1)} %collective-permute-done.11.rest_4_) | copy-start | bytes 1413124
  176.1 25.8 %collective-permute-start.12 = (bf16[2,184,640]{2,1,0:T(8,128)(2,1)S(1)}, bf16[2,184,640]{2,1,0:T(8,128)(2,1)S(1)}, u32[]{:S(2)}, u32[]{:S(2)}) collective-permute-start(bf16[2,184,640]{2,1,0:T(8,128)(2,1)S(1)} %collective-permute-done.8.rest_1_), channel_id=1, source_target_pairs={{0,16},{16,0},{1,17},{17,1},{2,18},{18,2},{3,19},{19,3},{4,20},{20... | collective-permute-start | bytes 1413128 | tf_op jit(solution)/shard_map/ppermute | solution.py:537
  177.6 44.8 %copy-start.8 = (bf16[2,184,640]{2,1,0:T(8,128)(2,1)}, bf16[2,184,640]{2,1,0:T(8,128)(2,1)S(1)}, u32[]{:S(2)}) copy-start(bf16[2,184,640]{2,1,0:T(8,128)(2,1)S(1)} %collective-permute-done.15.rest_8_) | copy-start | bytes 1413124
  177.6 22.2 %collective-permute-start.30 = (bf16[2,360,256]{2,1,0:T(8,128)(2,1)S(1)}, bf16[2,360,256]{2,1,0:T(8,128)(2,1)}, u32[]{:S(2)}, u32[]{:S(2)}) collective-permute-start(bf16[2,360,256]{2,1,0:T(8,128)(2,1)S(1)} %collective-permute-done.26.rest_2_), channel_id=1, source_target_pairs={{0,16},{16,0},{1,17},{17,1},{2,18},{18,2},{3,19},{19,3},{4,20},{20... | collective-permute-start | bytes 1105928 | tf_op jit(solution)/shard_map/ppermute | solution.py:537
  184.1 17.2 %collective-permute-start.33 = (bf16[2,360,256]{2,1,0:T(8,128)(2,1)S(1)}, bf16[2,360,256]{2,1,0:T(8,128)(2,1)}, u32[]{:S(2)}, u32[]{:S(2)}) collective-permute-start(bf16[2,360,256]{2,1,0:T(8,128)(2,1)S(1)} %collective-permute-done.25.rest_1_), channel_id=1, source_target_pairs={{0,1},{1,0},{2,3},{3,2},{4,5},{5,4},{6,7},{7,6},{8,9},{9,8},{10,11... | collective-permute-start | bytes 1105928 | tf_op jit(solution)/shard_map/ppermute | solution.py:537
  184.1 17.2 %collective-permute-start.34 = (bf16[2,360,256]{2,1,0:T(8,128)(2,1)S(1)}, bf16[2,360,256]{2,1,0:T(8,128)(2,1)}, u32[]{:S(2)}, u32[]{:S(2)}) collective-permute-start(bf16[2,360,256]{2,1,0:T(8,128)(2,1)S(1)} %collective-permute-done.26.rest_2_), channel_id=1, source_target_pairs={{0,1},{1,0},{2,3},{3,2},{4,5},{5,4},{6,7},{7,6},{8,9},{9,8},{10,11... | collective-permute-start | bytes 1105928 | tf_op jit(solution)/shard_map/ppermute | solution.py:537
  199.8 13.7 %collective-permute-start.13 = (bf16[2,184,640]{2,1,0:T(8,128)(2,1)S(1)}, bf16[2,184,640]{2,1,0:T(8,128)(2,1)S(1)}, u32[]{:S(2)}, u32[]{:S(2)}) collective-permute-start(bf16[2,184,640]{2,1,0:T(8,128)(2,1)S(1)} %collective-permute-done.9.rest_2_), channel_id=1, source_target_pairs={{0,16},{16,0},{1,17},{17,1},{2,18},{18,2},{3,19},{19,3},{4,20},{20... | collective-permute-start | bytes 1413128 | tf_op jit(solution)/shard_map/ppermute | solution.py:537
  201.3 12.6 %collective-permute-start.16 = (bf16[2,184,640]{2,1,0:T(8,128)(2,1)S(1)}, bf16[2,184,640]{2,1,0:T(8,128)(2,1)S(1)}, u32[]{:S(2)}, u32[]{:S(2)}) collective-permute-start(bf16[2,184,640]{2,1,0:T(8,128)(2,1)S(1)} %collective-permute-done.8.rest_1_), channel_id=1, source_target_pairs={{0,1},{1,0},{2,3},{3,2},{4,5},{5,4},{6,7},{7,6},{8,9},{9,8},{10,11... | collective-permute-start | bytes 1413128 | tf_op jit(solution)/shard_map/ppermute | solution.py:537
  201.3 12.6 %collective-permute-start.17 = (bf16[2,184,640]{2,1,0:T(8,128)(2,1)S(1)}, bf16[2,184,640]{2,1,0:T(8,128)(2,1)S(1)}, u32[]{:S(2)}, u32[]{:S(2)}) collective-permute-start(bf16[2,184,640]{2,1,0:T(8,128)(2,1)S(1)} %collective-permute-done.9.rest_2_), channel_id=1, source_target_pairs={{0,1},{1,0},{2,3},{3,2},{4,5},{5,4},{6,7},{7,6},{8,9},{9,8},{10,11... | collective-permute-start | bytes 1413128 | tf_op jit(solution)/shard_map/ppermute | solution.py:537
  201.8 12.6 %collective-permute-start.19 = (bf16[2,184,640]{2,1,0:T(8,128)(2,1)S(1)}, bf16[2,184,640]{2,1,0:T(8,128)(2,1)S(1)}, u32[]{:S(2)}, u32[]{:S(2)}) collective-permute-start(bf16[2,184,640]{2,1,0:T(8,128)(2,1)S(1)} %collective-permute-done.11.rest_4_), channel_id=1, source_target_pairs={{0,1},{1,0},{2,3},{3,2},{4,5},{5,4},{6,7},{7,6},{8,9},{9,8},{10,11... | collective-permute-start | bytes 1413128 | tf_op jit(solution)/shard_map/ppermute | solution.py:537
  201.9 18.5 %collective-permute-start.14 = (bf16[2,184,640]{2,1,0:T(8,128)(2,1)S(1)}, bf16[2,184,640]{2,1,0:T(8,128)(2,1)S(1)}, u32[]{:S(2)}, u32[]{:S(2)}) collective-permute-start(bf16[2,184,640]{2,1,0:T(8,128)(2,1)S(1)} %collective-permute-done.10.rest_3_), channel_id=1, source_target_pairs={{0,16},{16,0},{1,17},{17,1},{2,18},{18,2},{3,19},{19,3},{4,20},{20... | collective-permute-start | bytes 1413128 | tf_op jit(solution)/shard_map/ppermute | solution.py:537
  213.5 7.8 %collective-permute-start.31 = (bf16[2,360,256]{2,1,0:T(8,128)(2,1)}, bf16[2,360,256]{2,1,0:T(8,128)(2,1)}, u32[]{:S(2)}, u32[]{:S(2)}) collective-permute-start(bf16[2,360,256]{2,1,0:T(8,128)(2,1)} %collective-permute-done.29.rest_5_), channel_id=1, source_target_pairs={{0,2},{2,0},{4,6},{6,4},{8,10},{10,8},{12,14},{14,12},{1,3},{3,1},... | collective-permute-start | bytes 1105928 | tf_op jit(solution)/shard_map/ppermute | solution.py:537
  213.9 7.4 %collective-permute-start.18 = (bf16[2,184,640]{2,1,0:T(8,128)(2,1)S(1)}, bf16[2,184,640]{2,1,0:T(8,128)(2,1)S(1)}, u32[]{:S(2)}, u32[]{:S(2)}) collective-permute-start(bf16[2,184,640]{2,1,0:T(8,128)(2,1)S(1)} %collective-permute-done.10.rest_3_), channel_id=1, source_target_pairs={{0,1},{1,0},{2,3},{3,2},{4,5},{5,4},{6,7},{7,6},{8,9},{9,8},{10,11... | collective-permute-start | bytes 1413128 | tf_op jit(solution)/shard_map/ppermute | solution.py:537
  214.0 7.9 %collective-permute-start.20 = (bf16[2,184,640]{2,1,0:T(8,128)(2,1)S(1)}, bf16[2,184,640]{2,1,0:T(8,128)(2,1)S(1)}, u32[]{:S(2)}, u32[]{:S(2)}) collective-permute-start(bf16[2,184,640]{2,1,0:T(8,128)(2,1)S(1)} %collective-permute-done.12.rest_5_), channel_id=1, source_target_pairs={{0,1},{1,0},{2,3},{3,2},{4,5},{5,4},{6,7},{7,6},{8,9},{9,8},{10,11... | collective-permute-start | bytes 1413128 | tf_op jit(solution)/shard_map/ppermute | solution.py:537
  214.5 7.5 %collective-permute-start.21 = (bf16[2,184,640]{2,1,0:T(8,128)(2,1)S(1)}, bf16[2,184,640]{2,1,0:T(8,128)(2,1)S(1)}, u32[]{:S(2)}, u32[]{:S(2)}) collective-permute-start(bf16[2,184,640]{2,1,0:T(8,128)(2,1)S(1)} %collective-permute-done.13.rest_6_), channel_id=1, source_target_pairs={{0,1},{1,0},{2,3},{3,2},{4,5},{5,4},{6,7},{7,6},{8,9},{9,8},{10,11... | collective-permute-start | bytes 1413128 | tf_op jit(solution)/shard_map/ppermute | solution.py:537
  220.4 1.9 collective-permute-start.22
  221.3 8.4 %collective-permute-start.36 = (bf16[2,360,256]{2,1,0:T(8,128)(2,1)}, bf16[2,360,256]{2,1,0:T(8,128)(2,1)}, u32[]{:S(2)}, u32[]{:S(2)}) collective-permute-start(bf16[2,360,256]{2,1,0:T(8,128)(2,1)} %collective-permute-done.28.rest_4_), channel_id=1, source_target_pairs={{0,1},{1,0},{2,3},{3,2},{4,5},{5,4},{6,7},{7,6},{8,9},{9,8},{10,11... | collective-permute-start | bytes 1105928 | tf_op jit(solution)/shard_map/ppermute | solution.py:537
  221.3 12.6 %collective-permute-start.37 = (bf16[2,360,256]{2,1,0:T(8,128)(2,1)}, bf16[2,360,256]{2,1,0:T(8,128)(2,1)}, u32[]{:S(2)}, u32[]{:S(2)}) collective-permute-start(bf16[2,360,256]{2,1,0:T(8,128)(2,1)} %collective-permute-done.29.rest_5_), channel_id=1, source_target_pairs={{0,1},{1,0},{2,3},{3,2},{4,5},{5,4},{6,7},{7,6},{8,9},{9,8},{10,11... | collective-permute-start | bytes 1105928 | tf_op jit(solution)/shard_map/ppermute | solution.py:537
  221.8 12.1 %collective-permute-start.35 = (bf16[2,360,256]{2,1,0:T(8,128)(2,1)}, bf16[2,360,256]{2,1,0:T(8,128)(2,1)}, u32[]{:S(2)}, u32[]{:S(2)}) collective-permute-start(bf16[2,360,256]{2,1,0:T(8,128)(2,1)} %collective-permute-done.27.rest_3_), channel_id=1, source_target_pairs={{0,1},{1,0},{2,3},{3,2},{4,5},{5,4},{6,7},{7,6},{8,9},{9,8},{10,11... | collective-permute-start | bytes 1105928 | tf_op jit(solution)/shard_map/ppermute | solution.py:537
  221.9 12.0 %collective-permute-start.38 = (bf16[2,360,256]{2,1,0:T(8,128)(2,1)}, bf16[2,360,256]{2,1,0:T(8,128)(2,1)}, u32[]{:S(2)}, u32[]{:S(2)}) collective-permute-start(bf16[2,360,256]{2,1,0:T(8,128)(2,1)} %collective-permute-done.30.rest_6_), channel_id=1, source_target_pairs={{0,1},{1,0},{2,3},{3,2},{4,5},{5,4},{6,7},{7,6},{8,9},{9,8},{10,11... | collective-permute-start | bytes 1105928 | tf_op jit(solution)/shard_map/ppermute | solution.py:537
  222.3 11.6 %collective-permute-start.39 = (bf16[2,360,256]{2,1,0:T(8,128)(2,1)}, bf16[2,360,256]{2,1,0:T(8,128)(2,1)}, u32[]{:S(2)}, u32[]{:S(2)}) collective-permute-start(bf16[2,360,256]{2,1,0:T(8,128)(2,1)} %collective-permute-done.31.rest_7_), channel_id=1, source_target_pairs={{0,1},{1,0},{2,3},{3,2},{4,5},{5,4},{6,7},{7,6},{8,9},{9,8},{10,11... | collective-permute-start | bytes 1105928 | tf_op jit(solution)/shard_map/ppermute | solution.py:537
  229.7 5.4 %collective-permute-start.23 = (bf16[128,512]{1,0:T(8,128)(2,1)S(1)}, bf16[128,512]{1,0:T(8,128)(2,1)S(1)}, u32[]{:S(2)}, u32[]{:S(2)}) collective-permute-start(bf16[128,512]{1,0:T(8,128)(2,1)S(1)} %get-tuple-element.36.pairs_ref), channel_id=1, source_target_pairs={{0,2},{2,4},{4,6},{6,8},{8,10},{10,12},{12,14},{14,1},{1,3},{3,5},... | collective-permute-start | bytes 393224 | tf_op jit(solution)/shard_map/ppermute | solution.py:688
  (16 other events, 155.4 us)

commit v7 on v6

--- a/solution.py
+++ b/solution.py
@@ -25,6 +25,7 @@
 VMEM = pl.BlockSpec(memory_space=pltpu.VMEM)
 SMEM = pl.BlockSpec(memory_space=pltpu.SMEM)
 HBM = pl.BlockSpec(memory_space=pltpu.HBM)
+ANY = pl.BlockSpec(memory_space=pl.ANY)
 
 
 def route_slots(routes_ref):
@@ -300,7 +301,7 @@
     value = hidden.astype(F32)
     mean_square = jnp.mean(value * value, axis=-1, keepdims=True)
     normed = (value * lax.rsqrt(mean_square + eps) * gain_ref[...][None, :]).astype(BF16)
-    slices[...] = jnp.zeros_like(slices)
+    slices[:, :, rows:] = jnp.zeros(slices.shape[:2] + (slices.shape[2] - rows,), BF16)
     for s in range(slices.shape[0]):
         slices[s, :, :rows] = normed[:, s * rows : (s + 1) * rows]
     columns_of(held, slices, place_ref, held.shape[3] - pairs_ref.shape[1] // 4, copies, pairs_ref)
@@ -433,7 +434,7 @@
     return pl.pallas_call(
         attention_kernel,
         out_shape=jax.ShapeDtypeStruct((width, tok_count), BF16),
-        in_specs=[SMEM] * 2 + [VMEM] * 4 + [HBM] * 16,
+        in_specs=[SMEM] * 2 + [VMEM] * 4 + [HBM] * 14 + [ANY] * 2,
         out_specs=VMEM,
         scratch_shapes=[
             pltpu.VMEM((8, lines, quarter_rows, depth), BF16),
@@ -443,7 +444,7 @@
         ],
         compiler_params=pltpu.CompilerParams(vmem_limit_bytes=24 << 20),
         name="attention",
-    )(place, sinks, queries, pairs, halo, hidden_t, *in_hbm(parts))
+    )(place, sinks, queries, pairs, halo, hidden_t, *in_hbm(parts[:14]), *parts[14:])
 
 
 def place_of():

time: 247 us -> 247 us (level)
  no operation moved by 1% of the time
where the time goes in v7:
time: 247 us; the launch traced here: 243 us
  waiting for transfers between devices  164 us (66%)
  starting transfers between devices  38.5 us (16%)
  Pallas kernels  37.7 us (15%)
  local copies, waits for them, and re-layouts  2.98 us (1%)
    ppermute x7, waiting for transfers between devices, flipped(): return lax.ppermute(value, 'seq', [(i, i ^ bit * 2) for i in range(count)])  101 us
    ppermute x32, waiting for transfers between devices, swapped(): lax.ppermute(value, axis, [(i, i ^ 1) for i in range(lax.axis_size(axis))])  61.7 us
    ppermute x32, starting transfers between devices, swapped(): lax.ppermute(value, axis, [(i, i ^ 1) for i in range(lax.axis_size(axis))])  19.2 us
    pallas_call x1, Pallas kernels, run_experts(): pl.pallas_call(functools.partial(experts_kernel, seq_count // 2), out_sha...  14.5 us
    ppermute x7, starting transfers between devices, flipped(): return lax.ppermute(value, 'seq', [(i, i ^ bit * 2) for i in range(count)])  11.2 us
    pallas_call x1, Pallas kernels, attend_and_project(): pl.pallas_call(attention_kernel, out_shape=jax.ShapeDtypeStruct((width, t...  8.07 us
    all_to_all x1, starting transfers between devices, fused_body(): lax.all_to_all(finished, 'seq', split_axis=0, concat_axis=0, tiled=True)  5.65 us
    pallas_call x1, Pallas kernels, project_pairs(): pl.pallas_call(functools.partial(pairs_kernel, rows), out_shape=(jax.Shap...  5.17 us
  transfers between devices with their start and end apart: 41, of which 17 were waited for; matrix products, arithmetic and copies ran while one was open for 1% of the time, Pallas kernels for 5%

profile of v7, /device:TPU:0, one launch (start us, length us, event | category | flops | bytes accessed | tf_op | source)
XLA Modules:
  0.0 243.3 jit_solution(4280320728426848219)
XLA Ops:
  0.0 2.2 prepare.1.refs_0_
  2.2 4.1 %collective-permute-start.3 = (bf16[128,1536]{1,0:T(8,128)(2,1)}, bf16[128,1536]{1,0:T(8,128)(2,1)S(1)}, u32[]{:S(2)}, u32[]{:S(2)}) collective-permute-start(bf16[128,1536]{1,0:T(8,128)(2,1)} %prepare.1.refs_0_), channel_id=1, source_target_pairs={{0,8},{2,10},{4,12},{6,14},{8,0},{10,2},{12,4},{14,6},{1,9},{3,11}... | collective-permute-start | bytes 1179656 | tf_op jit(solution)/shard_map/ppermute | solution.py:471
  6.3 1.6 collective-permute-start.1
  7.8 16.3 %collective-permute-done.3.refs_4_ = bf16[128,1536]{1,0:T(8,128)(2,1)S(1)} collective-permute-done((bf16[128,1536]{1,0:T(8,128)(2,1)}, bf16[128,1536]{1,0:T(8,128)(2,1)S(1)}, u32[]{:S(2)}, u32[]{:S(2)}) %collective-permute-start.3) | collective-permute-done | bytes 393248 | tf_op jit(solution)/shard_map/ppermute | solution.py:471
  24.1 0.7 collective-permute-start.5
  24.8 1.5 collective-permute-start
  26.4 0.6 collective-permute-start.4
  27.0 1.5 collective-permute-start.2
  28.5 5.9 %collective-permute-done.5.refs_6_ = bf16[128,1536]{1,0:T(8,128)(2,1)S(1)} collective-permute-done((bf16[128,1536]{1,0:T(8,128)(2,1)S(1)}, bf16[128,1536]{1,0:T(8,128)(2,1)S(1)}, u32[]{:S(2)}, u32[]{:S(2)}) %collective-permute-start.5) | collective-permute-done | bytes 393248 | tf_op jit(solution)/shard_map/ppermute | solution.py:471
  34.3 1.3 collective-permute-start.6
  35.7 0.7 exp.3.sink_ref
  36.4 1.6 dynamic-slice_bitcast_fusion.refs_0_
  38.1 3.0 %fetch.1 = (bf16[1440,1440]{1,0:T(8,128)(2,1)S(1)}, bf16[720,1440]{1,0:T(8,128)(2,1)S(1)}) custom-call(bf16[4,1440,1440]{2,1,0:T(8,128)(2,1)} %refs_10_, bf16[4,720,1440]{2,1,0:T(8,128)(2,1)} %refs_11_), custom_call_target="tpu_custom_call" | custom-call | tf_op jit(solution)/shard_map/fetch/pallas_call | solution.py:119
  41.1 4.4 %collective-permute-done.4.refs_5_ = bf16[128,1536]{1,0:T(8,128)(2,1)S(1)} collective-permute-done((bf16[128,1536]{1,0:T(8,128)(2,1)S(1)}, bf16[128,1536]{1,0:T(8,128)(2,1)S(1)}, u32[]{:S(2)}, u32[]{:S(2)}) %collective-permute-start.4) | collective-permute-done | bytes 393248 | tf_op jit(solution)/shard_map/ppermute | solution.py:538
  45.5 8.4 %collective-permute-done.2.refs_3_ = bf16[128,1536]{1,0:T(8,128)(2,1)S(1)} collective-permute-done((bf16[128,1536]{1,0:T(8,128)(2,1)S(1)}, bf16[128,1536]{1,0:T(8,128)(2,1)S(1)}, u32[]{:S(2)}, u32[]{:S(2)}) %collective-permute-start.2) | collective-permute-done | bytes 393248 | tf_op jit(solution)/shard_map/ppermute | solution.py:538
  53.9 7.3 %collective-permute-done.6.refs_7_ = bf16[128,1536]{1,0:T(8,128)(2,1)} collective-permute-done((bf16[128,1536]{1,0:T(8,128)(2,1)S(1)}, bf16[128,1536]{1,0:T(8,128)(2,1)}, u32[]{:S(2)}, u32[]{:S(2)}) %collective-permute-start.6) | collective-permute-done | bytes 393248 | tf_op jit(solution)/shard_map/ppermute | solution.py:538
  61.2 14.5 %experts.1 = bf16[8,2,48,1440]{3,2,1,0:T(8,128)(2,1)} custom-call(s32[4]{0:T(128)S(1)} %pad_add_fusion.place_ref, bf16[128,1536]{1,0:T(8,128)(2,1)S(1)} %copy-done.2, bf16[128,1536]{1,0:T(8,128)(2,1)S(1)} %collective-permute-done.refs_1_, bf16[128,1536]{1,0:T(8,128)(2,1)S(1)} %collective-permute-done.1.refs_2_, ...), custom_call_target="tpu_custom_call" | custom-call | tf_op jit(solution)/shard_map/experts/pallas_call | solution.py:199
  75.7 5.6 %all-to-all-start = ((bf16[8,2,48,1440]{3,2,1,0:T(8,128)(2,1)}), bf16[8,2,48,1440]{3,2,1,0:T(8,128)(2,1)S(1)}, u32[]{:S(2)}, u32[]{:S(2)}) async-start(bf16[8,2,48,1440]{3,2,1,0:T(8,128)(2,1)} %experts.1), calls=%async_computation | async-start | bytes 4718592 | tf_op jit(solution)/shard_map/all_to_all | solution.py:523
  81.4 2.9 %collective-permute-start.24 = (bf16[360,256]{1,0:T(8,128)(2,1)S(1)}, bf16[360,256]{1,0:T(8,128)(2,1)S(1)}, u32[]{:S(2)}, u32[]{:S(2)}) collective-permute-start(bf16[360,256]{1,0:T(8,128)(2,1)S(1)} %copy-done.3), channel_id=1, source_target_pairs={{0,8},{2,10},{4,12},{6,14},{8,0},{10,2},{12,4},{14,6},{1,9},{3,11}... | collective-permute-start | bytes 552968 | tf_op jit(solution)/shard_map/ppermute | solution.py:471
  84.4 65.3 %collective-permute-done.24.refs_1_ = bf16[360,256]{1,0:T(8,128)(2,1)S(1)} collective-permute-done((bf16[360,256]{1,0:T(8,128)(2,1)S(1)}, bf16[360,256]{1,0:T(8,128)(2,1)S(1)}, u32[]{:S(2)}, u32[]{:S(2)}) %collective-permute-start.24) | collective-permute-done | bytes 184352 | tf_op jit(solution)/shard_map/ppermute | solution.py:471
  149.7 0.8 shard_map.101.rest_0_
  150.6 1.5 collective-permute-start.28
  152.4 0.8 shard_map.100.rest_0_
  153.2 1.8 collective-permute-start.8
  154.9 7.2 %collective-permute-done.25.rest_1_ = bf16[2,360,256]{2,1,0:T(8,128)(2,1)S(1)} collective-permute-done((bf16[2,360,256]{2,1,0:T(8,128)(2,1)}, bf16[2,360,256]{2,1,0:T(8,128)(2,1)S(1)}, u32[]{:S(2)}, u32[]{:S(2)}) %collective-permute-start.25) | collective-permute-done | bytes 368672 | tf_op jit(solution)/shard_map/ppermute | solution.py:471
  162.2 1.5 collective-permute-start.11
  163.8 0.6 collective-permute-start.29
  164.4 5.9 %collective-permute-done.8.rest_1_ = bf16[2,184,640]{2,1,0:T(8,128)(2,1)S(1)} collective-permute-done((bf16[2,184,640]{2,1,0:T(8,128)(2,1)}, bf16[2,184,640]{2,1,0:T(8,128)(2,1)S(1)}, u32[]{:S(2)}, u32[]{:S(2)}) %collective-permute-start.8) | collective-permute-done | bytes 471072 | tf_op jit(solution)/shard_map/ppermute | solution.py:471
  170.3 1.5 collective-permute-start.27
  171.7 0.8 collective-permute-done.9.rest_2_
  172.6 1.7 collective-permute-start.10
  174.3 1.8 collective-permute-done.11.rest_4_
  176.1 1.5 collective-permute-start.12
  177.6 0.5 collective-permute-start.30
  178.2 6.0 %collective-permute-done.29.rest_5_ = bf16[2,360,256]{2,1,0:T(8,128)(2,1)} collective-permute-done((bf16[2,360,256]{2,1,0:T(8,128)(2,1)S(1)}, bf16[2,360,256]{2,1,0:T(8,128)(2,1)}, u32[]{:S(2)}, u32[]{:S(2)}) %collective-permute-start.29) | collective-permute-done | bytes 368672 | tf_op jit(solution)/shard_map/ppermute | solution.py:538
  184.1 0.5 collective-permute-start.34
  184.6 15.2 %collective-permute-done.30.rest_6_ = bf16[2,360,256]{2,1,0:T(8,128)(2,1)} collective-permute-done((bf16[2,360,256]{2,1,0:T(8,128)(2,1)S(1)}, bf16[2,360,256]{2,1,0:T(8,128)(2,1)}, u32[]{:S(2)}, u32[]{:S(2)}) %collective-permute-start.30) | collective-permute-done | bytes 368672 | tf_op jit(solution)/shard_map/ppermute | solution.py:538
  199.8 1.5 collective-permute-start.13
  201.9 0.5 collective-permute-start.14
  202.5 11.0 %collective-permute-done.13.rest_6_ = bf16[2,184,640]{2,1,0:T(8,128)(2,1)S(1)} collective-permute-done((bf16[2,184,640]{2,1,0:T(8,128)(2,1)S(1)}, bf16[2,184,640]{2,1,0:T(8,128)(2,1)S(1)}, u32[]{:S(2)}, u32[]{:S(2)}) %collective-permute-start.13) | collective-permute-done | bytes 471072 | tf_op jit(solution)/shard_map/ppermute | solution.py:538
  214.5 5.9 %collective-permute-done.14.rest_7_ = bf16[2,184,640]{2,1,0:T(8,128)(2,1)S(1)} collective-permute-done((bf16[2,184,640]{2,1,0:T(8,128)(2,1)S(1)}, bf16[2,184,640]{2,1,0:T(8,128)(2,1)S(1)}, u32[]{:S(2)}, u32[]{:S(2)}) %collective-permute-start.14) | collective-permute-done | bytes 471072 | tf_op jit(solution)/shard_map/ppermute | solution.py:538
  220.4 0.9 collective-permute-done.31.rest_7_
  223.1 1.3 returns.1
  224.5 5.2 %pairs.1 = (bf16[128,512]{1,0:T(8,128)(2,1)S(1)}, bf16[8,128,184]{2,1,0:T(8,128)(2,1)S(1)}, bf16[128,1440]{1,0:T(8,128)(2,1)S(1)}, bf16[8,4,184,640]{3,2,1,0:T(8,128)(2,1)S(1)}) custom-call(s32[4]{0:T(128)S(1)} %pad_add_fusion.place_ref, bf16[768,1440]{1,0:T(8,128)(2,1)S(1)} %bitcast.19, bf16[128,1440]{1,0:T(8,128)(2,1)S(1)} %get-tuple-element.28.residual_ref, ...), custom_call_target="tpu_custom_call" | custom-call | tf_op jit(solution)/shard_map/pairs/pallas_call | solution.py:314
  229.7 2.4 collective-permute-start.23
  232.1 1.8 queries.1
  233.9 1.2 collective-permute-done.23.halo_ref
  235.1 8.1 %attention.1 = bf16[1440,128]{1,0:T(8,128)(2,1)} custom-call(s32[4]{0:T(128)S(1)} %pad_add_fusion.place_ref, f32[32]{0:T(128)S(1)} %exp.3.sink_ref, bf16[128,2048]{1,0:T(8,128)(2,1)S(1)} %get-tuple-element.35.packed_ref, bf16[128,512]{1,0:T(8,128)(2,1)S(1)} %get-tuple-element.36.pairs_ref, bf16[128,512]{1,0:T(8,128)(2,1)S(1)} %collective-permute-done.23.halo_ref, ...), custom_call_target="tpu_custom_call" | custom-call | tf_op jit(solution)/shard_map/attention/pallas_call | solution.py:434
  (95 shorter events, 4.1 us)
Async XLA Ops:
  2.2 21.9 %collective-permute-start.3 = (bf16[128,1536]{1,0:T(8,128)(2,1)}, bf16[128,1536]{1,0:T(8,128)(2,1)S(1)}, u32[]{:S(2)}, u32[]{:S(2)}) collective-permute-start(bf16[128,1536]{1,0:T(8,128)(2,1)} %prepare.1.refs_0_), channel_id=1, source_target_pairs={{0,8},{2,10},{4,12},{6,14},{8,0},{10,2},{12,4},{14,6},{1,9},{3,11}... | collective-permute-start | bytes 1179656 | tf_op jit(solution)/shard_map/ppermute | solution.py:471
  6.3 20.7 %collective-permute-start.1 = (bf16[128,1536]{1,0:T(8,128)(2,1)}, bf16[128,1536]{1,0:T(8,128)(2,1)S(1)}, u32[]{:S(2)}, u32[]{:S(2)}) collective-permute-start(bf16[128,1536]{1,0:T(8,128)(2,1)} %prepare.1.refs_0_), channel_id=1, source_target_pairs={{0,4},{2,6},{4,0},{6,2},{8,12},{10,14},{12,8},{14,10},{1,5},{3,7},... | collective-permute-start | bytes 1179656 | tf_op jit(solution)/shard_map/ppermute | solution.py:471
  24.1 10.2 %collective-permute-start.5 = (bf16[128,1536]{1,0:T(8,128)(2,1)S(1)}, bf16[128,1536]{1,0:T(8,128)(2,1)S(1)}, u32[]{:S(2)}, u32[]{:S(2)}) collective-permute-start(bf16[128,1536]{1,0:T(8,128)(2,1)S(1)} %collective-permute-done.3.refs_4_), channel_id=1, source_target_pairs={{0,4},{2,6},{4,0},{6,2},{8,12},{10,14},{12,8},{14,10},{1,5},{3,7},... | collective-permute-start | bytes 1179656 | tf_op jit(solution)/shard_map/ppermute | solution.py:471
  24.8 16.3 %collective-permute-start = (bf16[128,1536]{1,0:T(8,128)(2,1)}, bf16[128,1536]{1,0:T(8,128)(2,1)S(1)}, u32[]{:S(2)}, u32[]{:S(2)}) collective-permute-start(bf16[128,1536]{1,0:T(8,128)(2,1)} %prepare.1.refs_0_), channel_id=1, source_target_pairs={{0,2},{2,0},{4,6},{6,4},{8,10},{10,8},{12,14},{14,12},{1,3},{3,1},... | collective-permute-start | bytes 1179656 | tf_op jit(solution)/shard_map/ppermute | solution.py:538
  26.4 19.1 %collective-permute-start.4 = (bf16[128,1536]{1,0:T(8,128)(2,1)S(1)}, bf16[128,1536]{1,0:T(8,128)(2,1)S(1)}, u32[]{:S(2)}, u32[]{:S(2)}) collective-permute-start(bf16[128,1536]{1,0:T(8,128)(2,1)S(1)} %collective-permute-done.3.refs_4_), channel_id=1, source_target_pairs={{0,2},{2,0},{4,6},{6,4},{8,10},{10,8},{12,14},{14,12},{1,3},{3,1},... | collective-permute-start | bytes 1179656 | tf_op jit(solution)/shard_map/ppermute | solution.py:538
  27.0 26.9 %collective-permute-start.2 = (bf16[128,1536]{1,0:T(8,128)(2,1)S(1)}, bf16[128,1536]{1,0:T(8,128)(2,1)S(1)}, u32[]{:S(2)}, u32[]{:S(2)}) collective-permute-start(bf16[128,1536]{1,0:T(8,128)(2,1)S(1)} %collective-permute-done.1.refs_2_), channel_id=1, source_target_pairs={{0,2},{2,0},{4,6},{6,4},{8,10},{10,8},{12,14},{14,12},{1,3},{3,1},... | collective-permute-start | bytes 1179656 | tf_op jit(solution)/shard_map/ppermute | solution.py:538
  34.3 26.9 %collective-permute-start.6 = (bf16[128,1536]{1,0:T(8,128)(2,1)S(1)}, bf16[128,1536]{1,0:T(8,128)(2,1)}, u32[]{:S(2)}, u32[]{:S(2)}) collective-permute-start(bf16[128,1536]{1,0:T(8,128)(2,1)S(1)} %collective-permute-done.5.refs_6_), channel_id=1, source_target_pairs={{0,2},{2,0},{4,6},{6,4},{8,10},{10,8},{12,14},{14,12},{1,3},{3,1},... | collective-permute-start | bytes 1179656 | tf_op jit(solution)/shard_map/ppermute | solution.py:538
  75.7 148.7 %copy-start.4 = (f32[1440]{0:T(1024)S(1)}, f32[1440]{0:T(1024)}, u32[]{:S(2)}) copy-start(f32[1440]{0:T(1024)} %gain_ref.3) | copy-start | bytes 17284
  75.7 148.7 %all-to-all-start = ((bf16[8,2,48,1440]{3,2,1,0:T(8,128)(2,1)}), bf16[8,2,48,1440]{3,2,1,0:T(8,128)(2,1)S(1)}, u32[]{:S(2)}, u32[]{:S(2)}) async-start(bf16[8,2,48,1440]{3,2,1,0:T(8,128)(2,1)} %experts.1), calls=%async_computation | async-start | bytes 4718592 | tf_op jit(solution)/shard_map/all_to_all | solution.py:523
  81.4 68.3 %collective-permute-start.24 = (bf16[360,256]{1,0:T(8,128)(2,1)S(1)}, bf16[360,256]{1,0:T(8,128)(2,1)S(1)}, u32[]{:S(2)}, u32[]{:S(2)}) collective-permute-start(bf16[360,256]{1,0:T(8,128)(2,1)S(1)} %copy-done.3), channel_id=1, source_target_pairs={{0,8},{2,10},{4,12},{6,14},{8,0},{10,2},{12,4},{14,6},{1,9},{3,11}... | collective-permute-start | bytes 552968 | tf_op jit(solution)/shard_map/ppermute | solution.py:471
  84.3 68.1 %collective-permute-start.7 = (bf16[184,640]{1,0:T(8,128)(2,1)S(1)}, bf16[184,640]{1,0:T(8,128)(2,1)S(1)}, u32[]{:S(2)}, u32[]{:S(2)}) collective-permute-start(bf16[184,640]{1,0:T(8,128)(2,1)S(1)} %fusion.2.refs_0_), channel_id=1, source_target_pairs={{0,8},{2,10},{4,12},{6,14},{8,0},{10,2},{12,4},{14,6},{1,9},{3,11}... | collective-permute-start | bytes 706568 | tf_op jit(solution)/shard_map/ppermute | solution.py:471
  150.4 11.7 %collective-permute-start.25 = (bf16[2,360,256]{2,1,0:T(8,128)(2,1)}, bf16[2,360,256]{2,1,0:T(8,128)(2,1)S(1)}, u32[]{:S(2)}, u32[]{:S(2)}) collective-permute-start(bf16[2,360,256]{2,1,0:T(8,128)(2,1)} %shard_map.101.rest_0_), channel_id=1, source_target_pairs={{0,4},{2,6},{4,0},{6,2},{8,12},{10,14},{12,8},{14,10},{1,5},{3,7},... | collective-permute-start | bytes 1105928 | tf_op jit(solution)/shard_map/ppermute | solution.py:471
  150.5 11.7 %collective-permute-start.26 = (bf16[2,360,256]{2,1,0:T(8,128)(2,1)}, bf16[2,360,256]{2,1,0:T(8,128)(2,1)S(1)}, u32[]{:S(2)}, u32[]{:S(2)}) collective-permute-start(bf16[2,360,256]{2,1,0:T(8,128)(2,1)} %shard_map.101.rest_0_), channel_id=1, source_target_pairs={{0,2},{2,0},{4,6},{6,4},{8,10},{10,8},{12,14},{14,12},{1,3},{3,1},... | collective-permute-start | bytes 1105928 | tf_op jit(solution)/shard_map/ppermute | solution.py:538
  150.6 13.1 %collective-permute-start.28 = (bf16[2,360,256]{2,1,0:T(8,128)(2,1)}, bf16[2,360,256]{2,1,0:T(8,128)(2,1)}, u32[]{:S(2)}, u32[]{:S(2)}) collective-permute-start(bf16[2,360,256]{2,1,0:T(8,128)(2,1)} %shard_map.101.rest_0_), channel_id=1, source_target_pairs={{0,16},{16,0},{1,17},{17,1},{2,18},{18,2},{3,19},{19,3},{4,20},{20... | collective-permute-start | bytes 1105928 | tf_op jit(solution)/shard_map/ppermute | solution.py:538
  153.2 17.1 %collective-permute-start.8 = (bf16[2,184,640]{2,1,0:T(8,128)(2,1)}, bf16[2,184,640]{2,1,0:T(8,128)(2,1)S(1)}, u32[]{:S(2)}, u32[]{:S(2)}) collective-permute-start(bf16[2,184,640]{2,1,0:T(8,128)(2,1)} %shard_map.100.rest_0_), channel_id=1, source_target_pairs={{0,4},{2,6},{4,0},{6,2},{8,12},{10,14},{12,8},{14,10},{1,5},{3,7},... | collective-permute-start | bytes 1413128 | tf_op jit(solution)/shard_map/ppermute | solution.py:471
  154.9 8.8 %collective-permute-start.32 = (bf16[2,360,256]{2,1,0:T(8,128)(2,1)}, bf16[2,360,256]{2,1,0:T(8,128)(2,1)S(1)}, u32[]{:S(2)}, u32[]{:S(2)}) collective-permute-start(bf16[2,360,256]{2,1,0:T(8,128)(2,1)} %shard_map.101.rest_0_), channel_id=1, source_target_pairs={{0,1},{1,0},{2,3},{3,2},{4,5},{5,4},{6,7},{7,6},{8,9},{9,8},{10,11... | collective-permute-start | bytes 1105928 | tf_op jit(solution)/shard_map/ppermute | solution.py:538
  162.2 60.3 %copy-start.20 = (bf16[2,360,256]{2,1,0:T(8,128)(2,1)}, bf16[2,360,256]{2,1,0:T(8,128)(2,1)S(1)}, u32[]{:S(2)}) copy-start(bf16[2,360,256]{2,1,0:T(8,128)(2,1)S(1)} %collective-permute-done.25.rest_1_) | copy-start | bytes 1105924
  162.2 10.4 %collective-permute-start.9 = (bf16[2,184,640]{2,1,0:T(8,128)(2,1)}, bf16[2,184,640]{2,1,0:T(8,128)(2,1)S(1)}, u32[]{:S(2)}, u32[]{:S(2)}) collective-permute-start(bf16[2,184,640]{2,1,0:T(8,128)(2,1)} %shard_map.100.rest_0_), channel_id=1, source_target_pairs={{0,2},{2,0},{4,6},{6,4},{8,10},{10,8},{12,14},{14,12},{1,3},{3,1},... | collective-permute-start | bytes 1413128 | tf_op jit(solution)/shard_map/ppermute | solution.py:538
  162.2 39.1 %copy-start.21 = (bf16[2,360,256]{2,1,0:T(8,128)(2,1)}, bf16[2,360,256]{2,1,0:T(8,128)(2,1)S(1)}, u32[]{:S(2)}) copy-start(bf16[2,360,256]{2,1,0:T(8,128)(2,1)S(1)} %collective-permute-done.26.rest_2_) | copy-start | bytes 1105924
  162.2 13.9 %collective-permute-start.11 = (bf16[2,184,640]{2,1,0:T(8,128)(2,1)}, bf16[2,184,640]{2,1,0:T(8,128)(2,1)S(1)}, u32[]{:S(2)}, u32[]{:S(2)}) collective-permute-start(bf16[2,184,640]{2,1,0:T(8,128)(2,1)} %shard_map.100.rest_0_), channel_id=1, source_target_pairs={{0,16},{16,0},{1,17},{17,1},{2,18},{18,2},{3,19},{19,3},{4,20},{20... | collective-permute-start | bytes 1413128 | tf_op jit(solution)/shard_map/ppermute | solution.py:538
  163.8 13.9 %collective-permute-start.15 = (bf16[2,184,640]{2,1,0:T(8,128)(2,1)}, bf16[2,184,640]{2,1,0:T(8,128)(2,1)S(1)}, u32[]{:S(2)}, u32[]{:S(2)}) collective-permute-start(bf16[2,184,640]{2,1,0:T(8,128)(2,1)} %shard_map.100.rest_0_), channel_id=1, source_target_pairs={{0,1},{1,0},{2,3},{3,2},{4,5},{5,4},{6,7},{7,6},{8,9},{9,8},{10,11... | collective-permute-start | bytes 1413128 | tf_op jit(solution)/shard_map/ppermute | solution.py:538
  163.8 20.4 %collective-permute-start.29 = (bf16[2,360,256]{2,1,0:T(8,128)(2,1)S(1)}, bf16[2,360,256]{2,1,0:T(8,128)(2,1)}, u32[]{:S(2)}, u32[]{:S(2)}) collective-permute-start(bf16[2,360,256]{2,1,0:T(8,128)(2,1)S(1)} %collective-permute-done.25.rest_1_), channel_id=1, source_target_pairs={{0,16},{16,0},{1,17},{17,1},{2,18},{18,2},{3,19},{19,3},{4,20},{20... | collective-permute-start | bytes 1105928 | tf_op jit(solution)/shard_map/ppermute | solution.py:538
  170.3 52.2 %copy-start.5 = (bf16[2,184,640]{2,1,0:T(8,128)(2,1)}, bf16[2,184,640]{2,1,0:T(8,128)(2,1)S(1)}, u32[]{:S(2)}) copy-start(bf16[2,184,640]{2,1,0:T(8,128)(2,1)S(1)} %collective-permute-done.8.rest_1_) | copy-start | bytes 1413124
  170.3 13.9 %collective-permute-start.27 = (bf16[2,360,256]{2,1,0:T(8,128)(2,1)S(1)}, bf16[2,360,256]{2,1,0:T(8,128)(2,1)}, u32[]{:S(2)}, u32[]{:S(2)}) collective-permute-start(bf16[2,360,256]{2,1,0:T(8,128)(2,1)S(1)} %collective-permute-done.25.rest_1_), channel_id=1, source_target_pairs={{0,2},{2,0},{4,6},{6,4},{8,10},{10,8},{12,14},{14,12},{1,3},{3,1},... | collective-permute-start | bytes 1105928 | tf_op jit(solution)/shard_map/ppermute | solution.py:538
  172.6 49.9 %copy-start.6 = (bf16[2,184,640]{2,1,0:T(8,128)(2,1)}, bf16[2,184,640]{2,1,0:T(8,128)(2,1)S(1)}, u32[]{:S(2)}) copy-start(bf16[2,184,640]{2,1,0:T(8,128)(2,1)S(1)} %collective-permute-done.9.rest_2_) | copy-start | bytes 1413124
  172.6 29.3 %collective-permute-start.10 = (bf16[2,184,640]{2,1,0:T(8,128)(2,1)S(1)}, bf16[2,184,640]{2,1,0:T(8,128)(2,1)S(1)}, u32[]{:S(2)}, u32[]{:S(2)}) collective-permute-start(bf16[2,184,640]{2,1,0:T(8,128)(2,1)S(1)} %collective-permute-done.8.rest_1_), channel_id=1, source_target_pairs={{0,2},{2,0},{4,6},{6,4},{8,10},{10,8},{12,14},{14,12},{1,3},{3,1},... | collective-permute-start | bytes 1413128 | tf_op jit(solution)/shard_map/ppermute | solution.py:538
  176.1 46.3 %copy-start.7 = (bf16[2,184,640]{2,1,0:T(8,128)(2,1)}, bf16[2,184,640]{2,1,0:T(8,128)(2,1)S(1)}, u32[]{:S(2)}) copy-start(bf16[2,184,640]{2,1,0:T(8,128)(2,1)S(1)} %collective-permute-done.11.rest_4_) | copy-start | bytes 1413124
  176.1 25.8 %collective-permute-start.12 = (bf16[2,184,640]{2,1,0:T(8,128)(2,1)S(1)}, bf16[2,184,640]{2,1,0:T(8,128)(2,1)S(1)}, u32[]{:S(2)}, u32[]{:S(2)}) collective-permute-start(bf16[2,184,640]{2,1,0:T(8,128)(2,1)S(1)} %collective-permute-done.8.rest_1_), channel_id=1, source_target_pairs={{0,16},{16,0},{1,17},{17,1},{2,18},{18,2},{3,19},{19,3},{4,20},{20... | collective-permute-start | bytes 1413128 | tf_op jit(solution)/shard_map/ppermute | solution.py:538
  177.6 44.8 %copy-start.8 = (bf16[2,184,640]{2,1,0:T(8,128)(2,1)}, bf16[2,184,640]{2,1,0:T(8,128)(2,1)S(1)}, u32[]{:S(2)}) copy-start(bf16[2,184,640]{2,1,0:T(8,128)(2,1)S(1)} %collective-permute-done.15.rest_8_) | copy-start | bytes 1413124
  177.6 22.2 %collective-permute-start.30 = (bf16[2,360,256]{2,1,0:T(8,128)(2,1)S(1)}, bf16[2,360,256]{2,1,0:T(8,128)(2,1)}, u32[]{:S(2)}, u32[]{:S(2)}) collective-permute-start(bf16[2,360,256]{2,1,0:T(8,128)(2,1)S(1)} %collective-permute-done.26.rest_2_), channel_id=1, source_target_pairs={{0,16},{16,0},{1,17},{17,1},{2,18},{18,2},{3,19},{19,3},{4,20},{20... | collective-permute-start | bytes 1105928 | tf_op jit(solution)/shard_map/ppermute | solution.py:538
  184.1 17.2 %collective-permute-start.33 = (bf16[2,360,256]{2,1,0:T(8,128)(2,1)S(1)}, bf16[2,360,256]{2,1,0:T(8,128)(2,1)}, u32[]{:S(2)}, u32[]{:S(2)}) collective-permute-start(bf16[2,360,256]{2,1,0:T(8,128)(2,1)S(1)} %collective-permute-done.25.rest_1_), channel_id=1, source_target_pairs={{0,1},{1,0},{2,3},{3,2},{4,5},{5,4},{6,7},{7,6},{8,9},{9,8},{10,11... | collective-permute-start | bytes 1105928 | tf_op jit(solution)/shard_map/ppermute | solution.py:538
  184.1 17.2 %collective-permute-start.34 = (bf16[2,360,256]{2,1,0:T(8,128)(2,1)S(1)}, bf16[2,360,256]{2,1,0:T(8,128)(2,1)}, u32[]{:S(2)}, u32[]{:S(2)}) collective-permute-start(bf16[2,360,256]{2,1,0:T(8,128)(2,1)S(1)} %collective-permute-done.26.rest_2_), channel_id=1, source_target_pairs={{0,1},{1,0},{2,3},{3,2},{4,5},{5,4},{6,7},{7,6},{8,9},{9,8},{10,11... | collective-permute-start | bytes 1105928 | tf_op jit(solution)/shard_map/ppermute | solution.py:538
  199.8 13.7 %collective-permute-start.13 = (bf16[2,184,640]{2,1,0:T(8,128)(2,1)S(1)}, bf16[2,184,640]{2,1,0:T(8,128)(2,1)S(1)}, u32[]{:S(2)}, u32[]{:S(2)}) collective-permute-start(bf16[2,184,640]{2,1,0:T(8,128)(2,1)S(1)} %collective-permute-done.9.rest_2_), channel_id=1, source_target_pairs={{0,16},{16,0},{1,17},{17,1},{2,18},{18,2},{3,19},{19,3},{4,20},{20... | collective-permute-start | bytes 1413128 | tf_op jit(solution)/shard_map/ppermute | solution.py:538
  201.3 12.6 %collective-permute-start.16 = (bf16[2,184,640]{2,1,0:T(8,128)(2,1)S(1)}, bf16[2,184,640]{2,1,0:T(8,128)(2,1)S(1)}, u32[]{:S(2)}, u32[]{:S(2)}) collective-permute-start(bf16[2,184,640]{2,1,0:T(8,128)(2,1)S(1)} %collective-permute-done.8.rest_1_), channel_id=1, source_target_pairs={{0,1},{1,0},{2,3},{3,2},{4,5},{5,4},{6,7},{7,6},{8,9},{9,8},{10,11... | collective-permute-start | bytes 1413128 | tf_op jit(solution)/shard_map/ppermute | solution.py:538
  201.3 12.6 %collective-permute-start.17 = (bf16[2,184,640]{2,1,0:T(8,128)(2,1)S(1)}, bf16[2,184,640]{2,1,0:T(8,128)(2,1)S(1)}, u32[]{:S(2)}, u32[]{:S(2)}) collective-permute-start(bf16[2,184,640]{2,1,0:T(8,128)(2,1)S(1)} %collective-permute-done.9.rest_2_), channel_id=1, source_target_pairs={{0,1},{1,0},{2,3},{3,2},{4,5},{5,4},{6,7},{7,6},{8,9},{9,8},{10,11... | collective-permute-start | bytes 1413128 | tf_op jit(solution)/shard_map/ppermute | solution.py:538
  201.8 12.6 %collective-permute-start.19 = (bf16[2,184,640]{2,1,0:T(8,128)(2,1)S(1)}, bf16[2,184,640]{2,1,0:T(8,128)(2,1)S(1)}, u32[]{:S(2)}, u32[]{:S(2)}) collective-permute-start(bf16[2,184,640]{2,1,0:T(8,128)(2,1)S(1)} %collective-permute-done.11.rest_4_), channel_id=1, source_target_pairs={{0,1},{1,0},{2,3},{3,2},{4,5},{5,4},{6,7},{7,6},{8,9},{9,8},{10,11... | collective-permute-start | bytes 1413128 | tf_op jit(solution)/shard_map/ppermute | solution.py:538
  201.9 18.5 %collective-permute-start.14 = (bf16[2,184,640]{2,1,0:T(8,128)(2,1)S(1)}, bf16[2,184,640]{2,1,0:T(8,128)(2,1)S(1)}, u32[]{:S(2)}, u32[]{:S(2)}) collective-permute-start(bf16[2,184,640]{2,1,0:T(8,128)(2,1)S(1)} %collective-permute-done.10.rest_3_), channel_id=1, source_target_pairs={{0,16},{16,0},{1,17},{17,1},{2,18},{18,2},{3,19},{19,3},{4,20},{20... | collective-permute-start | bytes 1413128 | tf_op jit(solution)/shard_map/ppermute | solution.py:538
  213.5 7.8 %collective-permute-start.31 = (bf16[2,360,256]{2,1,0:T(8,128)(2,1)}, bf16[2,360,256]{2,1,0:T(8,128)(2,1)}, u32[]{:S(2)}, u32[]{:S(2)}) collective-permute-start(bf16[2,360,256]{2,1,0:T(8,128)(2,1)} %collective-permute-done.29.rest_5_), channel_id=1, source_target_pairs={{0,2},{2,0},{4,6},{6,4},{8,10},{10,8},{12,14},{14,12},{1,3},{3,1},... | collective-permute-start | bytes 1105928 | tf_op jit(solution)/shard_map/ppermute | solution.py:538
  213.9 7.4 %collective-permute-start.18 = (bf16[2,184,640]{2,1,0:T(8,128)(2,1)S(1)}, bf16[2,184,640]{2,1,0:T(8,128)(2,1)S(1)}, u32[]{:S(2)}, u32[]{:S(2)}) collective-permute-start(bf16[2,184,640]{2,1,0:T(8,128)(2,1)S(1)} %collective-permute-done.10.rest_3_), channel_id=1, source_target_pairs={{0,1},{1,0},{2,3},{3,2},{4,5},{5,4},{6,7},{7,6},{8,9},{9,8},{10,11... | collective-permute-start | bytes 1413128 | tf_op jit(solution)/shard_map/ppermute | solution.py:538
  214.0 7.9 %collective-permute-start.20 = (bf16[2,184,640]{2,1,0:T(8,128)(2,1)S(1)}, bf16[2,184,640]{2,1,0:T(8,128)(2,1)S(1)}, u32[]{:S(2)}, u32[]{:S(2)}) collective-permute-start(bf16[2,184,640]{2,1,0:T(8,128)(2,1)S(1)} %collective-permute-done.12.rest_5_), channel_id=1, source_target_pairs={{0,1},{1,0},{2,3},{3,2},{4,5},{5,4},{6,7},{7,6},{8,9},{9,8},{10,11... | collective-permute-start | bytes 1413128 | tf_op jit(solution)/shard_map/ppermute | solution.py:538
  214.5 7.5 %collective-permute-start.21 = (bf16[2,184,640]{2,1,0:T(8,128)(2,1)S(1)}, bf16[2,184,640]{2,1,0:T(8,128)(2,1)S(1)}, u32[]{:S(2)}, u32[]{:S(2)}) collective-permute-start(bf16[2,184,640]{2,1,0:T(8,128)(2,1)S(1)} %collective-permute-done.13.rest_6_), channel_id=1, source_target_pairs={{0,1},{1,0},{2,3},{3,2},{4,5},{5,4},{6,7},{7,6},{8,9},{9,8},{10,11... | collective-permute-start | bytes 1413128 | tf_op jit(solution)/shard_map/ppermute | solution.py:538
  220.4 1.9 collective-permute-start.22
  221.3 8.4 %collective-permute-start.36 = (bf16[2,360,256]{2,1,0:T(8,128)(2,1)}, bf16[2,360,256]{2,1,0:T(8,128)(2,1)}, u32[]{:S(2)}, u32[]{:S(2)}) collective-permute-start(bf16[2,360,256]{2,1,0:T(8,128)(2,1)} %collective-permute-done.28.rest_4_), channel_id=1, source_target_pairs={{0,1},{1,0},{2,3},{3,2},{4,5},{5,4},{6,7},{7,6},{8,9},{9,8},{10,11... | collective-permute-start | bytes 1105928 | tf_op jit(solution)/shard_map/ppermute | solution.py:538
  221.3 12.6 %collective-permute-start.37 = (bf16[2,360,256]{2,1,0:T(8,128)(2,1)}, bf16[2,360,256]{2,1,0:T(8,128)(2,1)}, u32[]{:S(2)}, u32[]{:S(2)}) collective-permute-start(bf16[2,360,256]{2,1,0:T(8,128)(2,1)} %collective-permute-done.29.rest_5_), channel_id=1, source_target_pairs={{0,1},{1,0},{2,3},{3,2},{4,5},{5,4},{6,7},{7,6},{8,9},{9,8},{10,11... | collective-permute-start | bytes 1105928 | tf_op jit(solution)/shard_map/ppermute | solution.py:538
  221.8 12.1 %collective-permute-start.35 = (bf16[2,360,256]{2,1,0:T(8,128)(2,1)}, bf16[2,360,256]{2,1,0:T(8,128)(2,1)}, u32[]{:S(2)}, u32[]{:S(2)}) collective-permute-start(bf16[2,360,256]{2,1,0:T(8,128)(2,1)} %collective-permute-done.27.rest_3_), channel_id=1, source_target_pairs={{0,1},{1,0},{2,3},{3,2},{4,5},{5,4},{6,7},{7,6},{8,9},{9,8},{10,11... | collective-permute-start | bytes 1105928 | tf_op jit(solution)/shard_map/ppermute | solution.py:538
  221.9 12.0 %collective-permute-start.38 = (bf16[2,360,256]{2,1,0:T(8,128)(2,1)}, bf16[2,360,256]{2,1,0:T(8,128)(2,1)}, u32[]{:S(2)}, u32[]{:S(2)}) collective-permute-start(bf16[2,360,256]{2,1,0:T(8,128)(2,1)} %collective-permute-done.30.rest_6_), channel_id=1, source_target_pairs={{0,1},{1,0},{2,3},{3,2},{4,5},{5,4},{6,7},{7,6},{8,9},{9,8},{10,11... | collective-permute-start | bytes 1105928 | tf_op jit(solution)/shard_map/ppermute | solution.py:538
  222.3 11.6 %collective-permute-start.39 = (bf16[2,360,256]{2,1,0:T(8,128)(2,1)}, bf16[2,360,256]{2,1,0:T(8,128)(2,1)}, u32[]{:S(2)}, u32[]{:S(2)}) collective-permute-start(bf16[2,360,256]{2,1,0:T(8,128)(2,1)} %collective-permute-done.31.rest_7_), channel_id=1, source_target_pairs={{0,1},{1,0},{2,3},{3,2},{4,5},{5,4},{6,7},{7,6},{8,9},{9,8},{10,11... | collective-permute-start | bytes 1105928 | tf_op jit(solution)/shard_map/ppermute | solution.py:538
  229.7 5.4 %collective-permute-start.23 = (bf16[128,512]{1,0:T(8,128)(2,1)S(1)}, bf16[128,512]{1,0:T(8,128)(2,1)S(1)}, u32[]{:S(2)}, u32[]{:S(2)}) collective-permute-start(bf16[128,512]{1,0:T(8,128)(2,1)S(1)} %get-tuple-element.36.pairs_ref), channel_id=1, source_target_pairs={{0,2},{2,4},{4,6},{6,8},{8,10},{10,12},{12,14},{14,1},{1,3},{3,5},... | collective-permute-start | bytes 393224 | tf_op jit(solution)/shard_map/ppermute | solution.py:689
  (16 other events, 155.4 us)
